TPU v7x, 256 devices: a whole 4x4x8 slice. The times are simulated.
256 devices in a mesh: dp: 64 (over z, x, core), tp: 4 (over y).
Axes of the slice: x: 4, y: 4, z: 8, core: 2. Of those that a mesh axis runs over, the one named last changes fastest.
Arguments:
- queries: bfloat16 [4096, 73728], P('dp', 'tp'), may hold values from -32 to 32
- prefix_cache: bfloat16 [64, 576, 1024], P('dp', None, 'tp'), may hold values from -12 to 12
- suffix_cache: bfloat16 [4096, 576, 128], P('dp'), may hold values from -48 to 48
- w_uv: bfloat16 [128, 512, 128], P('tp'), may hold values from -1 to 1
- fork_prompt: int32 [4096, 1], P('dp'), may hold values from 0 to 63; in each aligned block of 64 rows (0 to 63, 64 to 127, ...) at most 2 rows name the same one
- prompt_slot: int32 [64], replicated, may hold values from 0 to 63, each once
- suffix_len: int32 [4096], P('dp'), may hold values from 32 to 128
Outputs:
- attended: bfloat16 [4096, 16384], P('dp', 'tp')
Inputs may be any that keep to these rules, and one draw needn't show every extreme that they name: `fork_prompt`: among the 64 forks of one index of dp no prompt is named more than 2 times. `prompt_slot`: each slot holds exactly one prompt.
All inputs are finite; a program needn't handle non-finite values.
Results may differ from a plain program's by a relative error of at most 0.033.
Values may be sent and summed in bfloat16 or wider, within the bound.
No kernel may reach another device: no remote copies, remote signals or barrier semaphores. Data moves between devices by JAX's collectives and lax.ppermute only.
A program may use at most 128 MiB of HBM per device.

v0:
```python
import jax
import jax.numpy as jnp
from jax import lax
from jax.sharding import PartitionSpec as P

R = 512
P_SIZE = 64
V = 128


score_scale = 192.0 ** (-0.5)


def in_order(parts, dim):
    shape = list(parts.shape[1:])
    shape[dim] *= parts.shape[0]
    return jnp.moveaxis(parts, 0, dim).reshape(shape)


def from_everyone(value, axis):
    copies = jnp.broadcast_to(value, (lax.axis_size(axis), *value.shape))
    return lax.all_to_all(copies, axis, split_axis=0, concat_axis=0, tiled=True)


def gathered_copies(value, axis, dim):
    return in_order(from_everyone(value, axis), dim)


def project(latent, w_uv):
    return jnp.einsum("nhr,hrv->nhv", latent, w_uv, preferred_element_type=jnp.float32).astype(
        jnp.bfloat16
    )


def shards(queries, prefix_cache, suffix_cache, w_uv, fork_prompt, prompt_slot, suffix_len):
    owners_count = lax.axis_size("dp")
    forks_here = queries.shape[0]
    heads_here = w_uv.shape[0]
    key_width = R + P_SIZE
    capacity = max(2, 2 * forks_here // owners_count)
    slots_all = owners_count * capacity
    prompt_ids = jnp.arange(prompt_slot.shape[0], dtype=jnp.int32)
    chosen = fork_prompt[:, 0][:, None] == prompt_ids[None, :]
    owner_slot = jnp.sum(jnp.where(chosen, prompt_slot[None, :], 0), axis=1)
    fork_order = jnp.arange(forks_here, dtype=jnp.int32)
    before = (owner_slot[:, None] == owner_slot[None, :]) & (
        fork_order[None, :] < fork_order[:, None]
    )
    slot_rank = jnp.sum(before.astype(jnp.int32), axis=1)
    target = owner_slot * capacity + slot_rank
    placing = target[None, :] == jnp.arange(slots_all, dtype=jnp.int32)[:, None]
    outbound = jnp.dot(
        placing.astype(jnp.bfloat16), queries, preferred_element_type=jnp.float32
    ).astype(jnp.bfloat16)
    outbound = outbound.reshape(owners_count, capacity, heads_here * key_width)
    gathered = gathered_copies(prefix_cache, "tp", 2)[0]
    received = lax.all_to_all(outbound, "dp", split_axis=0, concat_axis=0, tiled=True)
    sources = received.shape[0]
    items = received.shape[1]
    lead_rows = sources * items
    query_rows = received.reshape(lead_rows * heads_here, key_width)
    scores = jnp.dot(query_rows, gathered, preferred_element_type=jnp.float32) * score_scale
    peak_score = jnp.max(scores, axis=1, keepdims=True)
    weights = jnp.exp(scores - peak_score)
    mass_sum = jnp.sum(weights, axis=1)
    summed = lax.dot_general(
        weights.astype(jnp.bfloat16),
        gathered[:R],
        (((1,), (1,)), ((), ())),
        preferred_element_type=jnp.float32,
    )
    latent = (summed / mass_sum[:, None]).astype(jnp.bfloat16)
    log_mass = (peak_score[:, 0] + jnp.log(mass_sum)).reshape(sources, items, heads_here)
    result = project(latent.reshape(lead_rows, heads_here, R), w_uv)
    result = result.reshape(sources, items, heads_here * V)
    answer, answer_mass = (
        lax.all_to_all(result, "dp", split_axis=0, concat_axis=0, tiled=True),
        lax.all_to_all(
            log_mass.astype(jnp.bfloat16), "dp", split_axis=0, concat_axis=0, tiled=True
        ).astype(log_mass.dtype),
    )
    picking = placing.astype(jnp.bfloat16)
    flat_answer = answer.reshape(slots_all, answer.shape[2])
    returned = lax.dot_general(
        picking, flat_answer, (((0,), (0,)), ((), ())), preferred_element_type=jnp.float32
    ).astype(jnp.bfloat16)
    mass_prefix = lax.dot_general(
        placing.astype(jnp.float32),
        answer_mass.reshape(slots_all, heads_here),
        (((0,), (0,)), ((), ())),
        precision=lax.Precision.HIGHEST,
    )
    value_prefix = returned.reshape(forks_here, heads_here, V)
    query_heads = queries.reshape(forks_here, heads_here, key_width)
    suffix_scores = (
        jnp.einsum("fhe,fes->fhs", query_heads, suffix_cache, preferred_element_type=jnp.float32)
        * score_scale
    )
    positions = jnp.arange(suffix_cache.shape[2], dtype=jnp.int32)
    live_mask = (positions[None, :] < suffix_len[:, None])[:, None, :]
    suffix_scores = jnp.where(live_mask, suffix_scores, -jnp.inf)
    suffix_peak = jnp.max(suffix_scores, axis=2, keepdims=True)
    suffix_weights = jnp.where(live_mask, jnp.exp(suffix_scores - suffix_peak), 0.0)
    suffix_sum = jnp.sum(suffix_weights, axis=2)
    suffix_summed = jnp.einsum(
        "fhs,frs->fhr",
        suffix_weights.astype(jnp.bfloat16),
        suffix_cache[:, :R, :],
        preferred_element_type=jnp.float32,
    )
    latent_suffix = (suffix_summed / suffix_sum[..., None]).astype(jnp.bfloat16)
    mass_suffix = suffix_peak[..., 0] + jnp.log(suffix_sum)
    value_suffix = project(latent_suffix, w_uv)
    top_mass = jnp.maximum(mass_prefix, mass_suffix)
    share_prefix = jnp.exp(mass_prefix - top_mass)[..., None]
    share_suffix = jnp.exp(mass_suffix - top_mass)[..., None]
    combined = (
        share_prefix * value_prefix.astype(jnp.float32)
        + share_suffix * value_suffix.astype(jnp.float32)
    ) / (share_prefix + share_suffix)
    return combined.astype(jnp.bfloat16).reshape(forks_here, heads_here * V)


def solution(mesh):
    placed = (
        P("dp", "tp"),
        P("dp", None, "tp"),
        P("dp", None, None),
        P("tp", None, None),
        P("dp", None),
        P(),
        P("dp"),
    )
    return jax.shard_map(
        shards, mesh=mesh, in_specs=placed, out_specs=P("dp", "tp"), check_vma=False
    )
```

profile of v0, /device:TPU:1, one launch (start us, length us, event | category | flops | bytes accessed | tf_op | source)
XLA Modules:
  0.0 248.8 jit_solution(2788197232239932484)
XLA Ops:
  0.0 0.0 copy-start
  0.0 2.2 broadcast_in_dim.52
  2.2 5.0 %all-to-all-start.1 = ((bf16[4,1,576,256]{3,2,1,0:T(8,128)(2,1)}), bf16[4,1,576,256]{3,2,1,0:T(8,128)(2,1)S(1)}, u32[]{:S(2)}, u32[]{:S(2)}) async-start(bf16[4,1,576,256]{3,2,1,0:T(8,128)(2,1)} %broadcast_in_dim.52), calls=%async_computation.1 | async-start | bytes 2359296 | tf_op jit(solution)/shard_map/all_to_all | solution.py:22
  7.2 0.8 select_reduce_fusion
  8.1 0.2 convert_reduce_fusion
  8.3 0.0 copy-done
  8.3 3.5 %convolution_convert_fusion = bf16[128,18432]{1,0:T(8,128)(2,1)} fusion(bf16[64,18432]{1,0:T(8,128)(2,1)S(1)} %copy-done, s32[64]{0:T(128)S(1)} %multiply_add_fusion), kind=kOutput, calls=%fused_computation | convolution fusion | flops 304357376 | bytes 7078144 | tf_op jit(solution)/shard_map/dot_general | solution.py:52
  11.8 7.9 %reshape.69 = bf16[64,2,18432]{2,1,0:T(2,128)(2,1)} reshape(bf16[128,18432]{1,0:T(8,128)(2,1)} %convolution_convert_fusion) | data formatting | bytes 9437184 | tf_op jit(solution)/shard_map/reshape | solution.py:55
  19.7 2.3 all-to-all-done.1
  22.0 0.0 copy-start.1
  22.0 1.0 copy-done.1
  23.0 14.3 %all-to-all-start = ((bf16[64,2,18432]{2,1,0:T(2,128)(2,1)}), bf16[64,2,18432]{2,1,0:T(2,128)(2,1)}, u32[]{:S(2)}, u32[]{:S(2)}) async-start(bf16[64,2,18432]{2,1,0:T(2,128)(2,1)} %reshape.69), calls=%async_computation | async-start | bytes 9437184 | tf_op jit(solution)/shard_map/all_to_all | solution.py:57
  37.3 0.0 copy-start.2
  37.3 4.5 %reshape.72 = bf16[64,32,576]{2,1,0:T(8,128)(2,1)S(1)} reshape(bf16[64,18432]{1,0:T(8,128)(2,1)} %param.7) | data formatting | bytes 4718592 | tf_op jit(solution)/shard_map/reshape | solution.py:94
  41.8 0.0 copy-done.2
  41.8 0.1 iota_compare_fusion.4
  41.9 2.4 copy.27
  44.3 2.3 slice.12
  46.6 95.9 %all-to-all-done = bf16[64,2,18432]{2,1,0:T(2,128)(2,1)} async-done(((bf16[64,2,18432]{2,1,0:T(2,128)(2,1)}), bf16[64,2,18432]{2,1,0:T(2,128)(2,1)}, u32[]{:S(2)}, u32[]{:S(2)}) %all-to-all-start) | async-done | bytes 4718624 | tf_op jit(solution)/shard_map/all_to_all | solution.py:57
  142.6 12.3 %reshape.70 = bf16[4096,576]{1,0:T(8,128)(2,1)} reshape(bf16[64,2,18432]{2,1,0:T(2,128)(2,1)} %all-to-all-done) | data formatting | bytes 9437184 | tf_op jit(solution)/shard_map/reshape | solution.py:61
  154.9 12.8 %multiply_reduce_fusion = (f32[4096]{0:T(1024)S(1)}, f32[4096,1024]{0,1:T(8,128)}) fusion(bf16[4096,576]{1,0:T(8,128)(2,1)} %reshape.70, bf16[576,1024]{0,1:T(8,128)(2,1)} %bitcast.44), kind=kOutput, calls=%fused_computation.2 | convolution fusion | flops 4840222720 | bytes 22691840 | tf_op jit(solution)/shard_map/dot_general | solution.py:62
  167.7 8.5 %fusion.1 = f32[4096]{0:T(1024)S(1)} fusion(f32[4096,1024]{0,1:T(8,128)} %get-tuple-element.11, f32[4096]{0:T(1024)S(1)} %get-tuple-element.10), kind=kLoop, calls=%fused_computation.4 | loop fusion | flops 12578816 | bytes 16809984 | tf_op jit(solution)/shard_map/reduce_sum | solution.py:65
  176.3 0.7 convert_element_type.59
  177.0 7.6 %all-to-all-start.2 = ((bf16[64,2,32]{2,1,0:T(2,128)(2,1)}), bf16[64,2,32]{2,1,0:T(2,128)(2,1)S(1)}, u32[]{:S(2)}, u32[]{:S(2)}) async-start(bf16[64,2,32]{2,1,0:T(2,128)(2,1)} %convert_element_type.59), calls=%async_computation.2 | async-start | bytes 65536 | tf_op jit(solution)/shard_map/all_to_all | solution.py:78
  184.5 0.0 copy-start.3
  184.5 9.0 %divide_convert_fusion = bf16[4096,512]{1,0:T(8,128)(2,1)S(1)} fusion(f32[4096]{0:T(1024)S(1)} %fusion.1, bf16[512,1024]{0,1:T(8,128)(2,1)} %bitcast.45, f32[4096,1024]{0,1:T(8,128)} %get-tuple-element.11, f32[4096]{0:T(1024)S(1)} %get-tuple-element.10), kind=kOutput, calls=%fused_computation.8 | convolution fusion | flops 4311744512 | bytes 22052864 | tf_op jit(solution)/shard_map/dot_general | solution.py:66
  193.6 0.0 copy-done.3
  193.6 4.9 %fusion.18 = bf16[128,32,128]{2,0,1:T(8,128)(2,1)S(1)} fusion(bf16[32,512,128]{2,1,0:T(8,128)(2,1)S(1)} %copy-done.3, bf16[128,32,512]{2,1,0:T(8,128)(2,1)S(1)} %bitcast.49), kind=kOutput, calls=%fused_computation.19 | convolution fusion | flops 537395200 | bytes 9437184 | tf_op jit(solution)/shard_map/nhr,hrv->nhv/dot_general | solution.py:30
  198.4 1.7 copy.32
  200.1 2.1 reshape.74
  202.2 0.0 all-to-all-done.2
  202.2 10.5 %all-to-all-start.3 = ((bf16[64,2,4096]{2,1,0:T(2,128)(2,1)}), bf16[64,2,4096]{2,1,0:T(2,128)(2,1)}, u32[]{:S(2)}, u32[]{:S(2)}) async-start(bf16[64,2,4096]{2,1,0:T(2,128)(2,1)} %reshape.74), calls=%async_computation.3 | async-start | bytes 2097152 | tf_op jit(solution)/shard_map/all_to_all | solution.py:77
  212.7 6.3 %fusion.67 = (f32[64,32]{1,0:T(8,128)S(1)}, f32[64,32,128]{2,1,0:T(8,128)}) fusion(bf16[64,32,576]{2,1,0:T(8,128)(2,1)S(1)} %reshape.72, bf16[64,576,128]{2,1,0:T(8,128)(2,1)} %param.9, pred[64,128]{1,0:T(8,128)(4,1)S(1)} %iota_compare_fusion.4), kind=kOutput, calls=%fused_computation.60 | convolution fusion | flops 302774272 | bytes 12861440 | tf_op jit(solution)/shard_map/fhe,fes->fhs/dot_general | solution.py:96
  219.0 0.1 copy.30
  219.1 1.9 fusion.50
  221.0 0.1 copy.29
  221.0 8.1 %divide_convert_fusion.1 = bf16[64,32,512]{2,1,0:T(8,128)(2,1)} fusion(f32[64,32]{1,0:T(8,128)S(1)} %fusion.50, bf16[64,576,128]{2,1,0:T(8,128)(2,1)} %param.9, f32[64,32,128]{2,1,0:T(8,128)} %get-tuple-element.9, f32[64,32]{1,0:T(8,128)S(1)} %get-tuple-element.8, pred[64,128]{1,0:T(8,128)(4,1)S(1)} %iota_compare_fusion.4), kind=kOutput, calls=%fused_computation.15 | convolution fusion | flops 271319040 | bytes 11558912 | tf_op jit(solution)/shard_map/fhs,frs->fhr/dot_general | solution.py:105
  229.1 0.2 fusion.64
  229.3 11.3 %all-to-all-done.3 = bf16[64,2,4096]{2,1,0:T(2,128)(2,1)} async-done(((bf16[64,2,4096]{2,1,0:T(2,128)(2,1)}), bf16[64,2,4096]{2,1,0:T(2,128)(2,1)}, u32[]{:S(2)}, u32[]{:S(2)}) %all-to-all-start.3) | async-done | bytes 1048608 | tf_op jit(solution)/shard_map/all_to_all | solution.py:77
  240.6 1.5 reshape.75
  242.1 0.3 fusion.21
  242.5 5.5 %fusion.46 = bf16[32,8,8,128]{3,2,1,0:T(8,128)(2,1)S(1)} fusion(bf16[32,512,128]{2,1,0:T(8,128)(2,1)} %param.10, bf16[64,32,512]{2,1,0:T(8,128)(2,1)} %divide_convert_fusion.1, f32[8,32,8,128]{3,2,1,0:T(8,128)S(1)} %fusion.21, f32[64,32]{0,1:T(8,128)S(1)} %get-tuple-element.5, f32[64,32]{0,1:T(8,128)S(1)} %get-tuple-element.6, ...), kind=kOutput, calls=%fused_computation.30 | convolution fusion | flops 270270464 | bytes 7888896 | tf_op jit(solution)/shard_map/nhr,hrv->nhv/dot_general | solution.py:30
  248.0 0.9 copy.65
  (2 shorter events, 0.0 us)
Async XLA Ops:
  0.0 8.3 %copy-start = (bf16[64,18432]{1,0:T(8,128)(2,1)S(1)}, bf16[64,18432]{1,0:T(8,128)(2,1)}, u32[]{:S(2)}) copy-start(bf16[64,18432]{1,0:T(8,128)(2,1)} %param.7) | copy-start | bytes 7077892
  2.2 19.8 %all-to-all-start.1 = ((bf16[4,1,576,256]{3,2,1,0:T(8,128)(2,1)}), bf16[4,1,576,256]{3,2,1,0:T(8,128)(2,1)S(1)}, u32[]{:S(2)}, u32[]{:S(2)}) async-start(bf16[4,1,576,256]{3,2,1,0:T(8,128)(2,1)} %broadcast_in_dim.52), calls=%async_computation.1 | async-start | bytes 2359296 | tf_op jit(solution)/shard_map/all_to_all | solution.py:22
  22.0 1.0 copy-start.1
  23.0 119.6 %all-to-all-start = ((bf16[64,2,18432]{2,1,0:T(2,128)(2,1)}), bf16[64,2,18432]{2,1,0:T(2,128)(2,1)}, u32[]{:S(2)}, u32[]{:S(2)}) async-start(bf16[64,2,18432]{2,1,0:T(2,128)(2,1)} %reshape.69), calls=%async_computation | async-start | bytes 9437184 | tf_op jit(solution)/shard_map/all_to_all | solution.py:57
  37.3 4.5 %copy-start.2 = (s32[64]{0:T(128)S(1)}, s32[64]{0:T(128)}, u32[]{:S(2)}) copy-start(s32[64]{0:T(128)} %param.13) | copy-start | bytes 772
  177.0 25.3 %all-to-all-start.2 = ((bf16[64,2,32]{2,1,0:T(2,128)(2,1)}), bf16[64,2,32]{2,1,0:T(2,128)(2,1)S(1)}, u32[]{:S(2)}, u32[]{:S(2)}) async-start(bf16[64,2,32]{2,1,0:T(2,128)(2,1)} %convert_element_type.59), calls=%async_computation.2 | async-start | bytes 65536 | tf_op jit(solution)/shard_map/all_to_all | solution.py:78
  184.5 9.0 %copy-start.3 = (bf16[32,512,128]{2,1,0:T(8,128)(2,1)S(1)}, bf16[32,512,128]{2,1,0:T(8,128)(2,1)}, u32[]{:S(2)}) copy-start(bf16[32,512,128]{2,1,0:T(8,128)(2,1)} %param.10) | copy-start | bytes 12582916
  202.2 38.4 %all-to-all-start.3 = ((bf16[64,2,4096]{2,1,0:T(2,128)(2,1)}), bf16[64,2,4096]{2,1,0:T(2,128)(2,1)}, u32[]{:S(2)}, u32[]{:S(2)}) async-start(bf16[64,2,4096]{2,1,0:T(2,128)(2,1)} %reshape.74), calls=%async_computation.3 | async-start | bytes 2097152 | tf_op jit(solution)/shard_map/all_to_all | solution.py:77
where the time goes:
time: 250 us; the launch traced here: 249 us
  waiting for transfers between devices  110 us (44%)
  matrix products  50.6 us (20%)
  local copies, waits for them, and re-layouts  39.7 us (16%)
  starting transfers between devices  37.4 us (15%)
  other arithmetic  11.5 us (5%)
    all_to_all x1, waiting for transfers between devices, shards(): lax.all_to_all(outbound, 'dp', split_axis=0, concat_axis=0, tiled=True)  95.9 us
    all_to_all x1, starting transfers between devices, shards(): lax.all_to_all(outbound, 'dp', split_axis=0, concat_axis=0, tiled=True)  14.3 us
    dot_general x1, matrix products, shards(): jnp.dot(query_rows, gathered, preferred_element_type=jnp.float32)  12.8 us
    reshape x1, local copies, waits for them, and re-layouts, shards(): query_rows = received.reshape(lead_rows * heads_here, key_width)  12.3 us
    all_to_all x1, waiting for transfers between devices, shards(): lax.all_to_all(result, 'dp', split_axis=0, concat_axis=0, tiled=True)  11.3 us
    all_to_all x1, starting transfers between devices, shards(): lax.all_to_all(result, 'dp', split_axis=0, concat_axis=0, tiled=True)  10.5 us
    dot_general x2, matrix products, project(): jnp.einsum('nhr,hrv->nhv', latent, w_uv, preferred_element_type=jnp.float32)  10.3 us
    dot_general x1, matrix products, shards(): lax.dot_general(weights.astype(jnp.bfloat16), gathered[:R], (((1,), (1,))...  9 us
  transfers between devices with their start and end apart: 4, of which 3 were waited for; matrix products, arithmetic and copies ran while one was open for 23% of the time, Pallas kernels for 0%

commit v1 on v0

v1 whole, which is shorter than its diff:
```python
import functools

import jax
import jax.numpy as jnp
from jax import lax
from jax.experimental import pallas as pl
from jax.experimental.pallas import tpu as pltpu
from jax.sharding import Mesh
from jax.sharding import PartitionSpec as P

R = 512
P_SIZE = 64
V = 128
KEY = R + P_SIZE
MOST = 2
COPIES = 4
LANES = 128
SCALE = 192.0 ** (-0.5)
LOG2E = 1.4426950408889634


def row_targets(prompt_col, slot_row, group):
    forks = prompt_col.shape[0]
    prompts = slot_row.shape[1]
    ids = lax.broadcasted_iota(jnp.int32, (forks, prompts), 1)
    owner = jnp.sum(jnp.where(prompt_col == ids, slot_row, 0), axis=1, keepdims=True)
    down = lax.broadcasted_iota(jnp.int32, (forks, forks), 0)
    along = lax.broadcasted_iota(jnp.int32, (forks, forks), 1)

    def turned(column):
        return jnp.sum(jnp.where(down == along, column, 0), axis=0, keepdims=True)

    owner_row = turned(owner)
    before = (owner == owner_row) & (along < down)
    rank = jnp.sum(before.astype(jnp.int32), axis=1, keepdims=True)
    held = COPIES * MOST
    target = (owner % group) * held + (owner // group) * MOST + rank
    return turned(target), target


def place_kernel(group, prompt_ref, slot_ref, q_ref, out_ref):
    target_row, _ = row_targets(prompt_ref[...], slot_ref[...], group)
    rows = out_ref.shape[0]
    at = lax.broadcasted_iota(jnp.int32, (rows, target_row.shape[1]), 0)
    placing = (at == target_row).astype(jnp.bfloat16)
    out_ref[...] = jnp.dot(placing, q_ref[...], preferred_element_type=jnp.float32).astype(
        jnp.bfloat16
    )


def place(prompt, slots, queries, group):
    forks, width = queries.shape
    rows = group * COPIES * MOST
    tile = width // 8
    return pl.pallas_call(
        functools.partial(place_kernel, group),
        out_shape=jax.ShapeDtypeStruct((rows, width), jnp.bfloat16),
        grid=(width // tile,),
        in_specs=[
            pl.BlockSpec(prompt.shape, lambda i: (0, 0)),
            pl.BlockSpec(slots.shape, lambda i: (0, 0)),
            pl.BlockSpec((forks, tile), lambda i: (0, i)),
        ],
        out_specs=pl.BlockSpec((rows, tile), lambda i: (0, i)),
        name="place",
    )(prompt, slots, queries)


def prefix_kernel(group, q_ref, kv_ref, w_ref, out_ref, key_ref, lat_ref, mass_ref):
    step = pl.program_id(0)
    heads = w_ref.shape[0]
    pairs = heads // 2
    quarter = kv_ref.shape[2]

    @pl.when(step == 0)
    def _():
        zero = jnp.zeros((P_SIZE, key_ref.shape[1]), key_ref.dtype)
        key_ref[0:P_SIZE, :] = zero
        key_ref[P_SIZE + KEY : P_SIZE + KEY + P_SIZE, :] = zero

    @pl.when(step % MOST == 0)
    def _():
        for part in range(kv_ref.shape[0]):
            key_ref[P_SIZE : P_SIZE + KEY, part * quarter : (part + 1) * quarter] = kv_ref[part]

    wide = KEY + P_SIZE
    lane = lax.broadcasted_iota(jnp.int32, (group, LANES), 1)
    masses = jnp.zeros((group, LANES), jnp.float32)
    rows = pl.ds(pl.multiple_of(step * group, group), group)
    for odd in range(2):
        query = jnp.concatenate(
            [
                q_ref[:, p * 2 * KEY + odd * R : p * 2 * KEY + odd * R + wide]
                for p in range(pairs)
            ],
            axis=0,
        )
        first = 0 if odd else P_SIZE
        scores = jnp.dot(
            query, key_ref[first : first + wide, :], preferred_element_type=jnp.float32
        )
        peak = jnp.max(scores, axis=1, keepdims=True)
        weights = jnp.exp2((scores - peak) * (SCALE * LOG2E))
        total = jnp.sum(weights, axis=1, keepdims=True)
        summed = lax.dot_general(
            weights.astype(jnp.bfloat16),
            key_ref[P_SIZE : P_SIZE + R, :],
            (((1,), (1,)), ((), ())),
            preferred_element_type=jnp.float32,
        )
        latent = (summed / total).astype(jnp.bfloat16)
        mass = peak * SCALE + jnp.log(total)
        for p in range(pairs):
            head = 2 * p + odd
            lat_ref[head, rows, :] = latent[p * group : (p + 1) * group]
            masses = jnp.where(lane == head, mass[p * group : (p + 1) * group], masses)
    mass_ref[rows, :] = masses

    @pl.when(step == pl.num_programs(0) - 1)
    def _():
        count = mass_ref.shape[0]
        held = count // group
        to = lax.broadcasted_iota(jnp.int32, (count, count), 0)
        come = lax.broadcasted_iota(jnp.int32, (count, count), 1)
        turn = (come == (to % held) * group + to // held).astype(jnp.bfloat16)

        def put(at, block):
            out_ref[:, at : at + block.shape[1]] = jnp.dot(
                turn, block, preferred_element_type=jnp.float32
            ).astype(jnp.bfloat16)

        for head in range(0, heads, 2):
            both = [
                jnp.dot(lat_ref[h], w_ref[h], preferred_element_type=jnp.float32)
                for h in (head, head + 1)
            ]
            put(head * V, jnp.concatenate(both, axis=1).astype(jnp.bfloat16))
        high = mass_ref[...].astype(jnp.bfloat16)
        low = (mass_ref[...] - high.astype(jnp.float32)).astype(jnp.bfloat16)
        put(heads * V, jnp.concatenate([high, low], axis=1))


def prefix(sorted_queries, caches, w_uv, group):
    rows, width = sorted_queries.shape
    heads = w_uv.shape[0]
    steps = rows // group
    parts = caches.shape[0] // COPIES
    length = parts * caches.shape[2]
    return pl.pallas_call(
        functools.partial(prefix_kernel, group),
        out_shape=jax.ShapeDtypeStruct((rows, heads * V + 2 * LANES), jnp.bfloat16),
        grid=(steps,),
        in_specs=[
            pl.BlockSpec((group, width), lambda i: (i, 0)),
            pl.BlockSpec((parts, *caches.shape[1:]), lambda i: (i // MOST, 0, 0)),
            pl.BlockSpec(w_uv.shape, lambda i: (0, 0, 0), pipeline_mode=pl.Buffered(1)),
        ],
        out_specs=pl.BlockSpec((rows, heads * V + 2 * LANES), lambda i: (0, 0)),
        scratch_shapes=[
            pltpu.VMEM((KEY + 2 * P_SIZE, length), jnp.bfloat16),
            pltpu.VMEM((heads, rows, R), jnp.bfloat16),
            pltpu.VMEM((rows, LANES), jnp.float32),
        ],
        compiler_params=pltpu.CompilerParams(vmem_limit_bytes=48 << 20),
        name="prefix",
    )(sorted_queries, caches, w_uv)


def merge_kernel(group, prompt_ref, slot_ref, answer_ref, value_ref, mass_ref, out_ref):
    _, target = row_targets(prompt_ref[...], slot_ref[...], group)
    forks, heads = mass_ref.shape
    rows = answer_ref.shape[0]
    at = lax.broadcasted_iota(jnp.int32, (forks, rows), 1)
    picking = (at == target).astype(jnp.bfloat16)

    def pick(start, size):
        return jnp.dot(
            picking, answer_ref[:, start : start + size], preferred_element_type=jnp.float32
        )

    come = pick(heads * V, 2 * LANES)
    mass_prefix = come[:, :heads] + come[:, LANES : LANES + heads]
    mass_suffix = mass_ref[...]
    top = jnp.maximum(mass_prefix, mass_suffix)
    share_prefix = jnp.exp(mass_prefix - top)
    share_suffix = jnp.exp(mass_suffix - top)
    both = share_prefix + share_suffix
    part_prefix = share_prefix / both
    part_suffix = share_suffix / both
    for head in range(0, heads, 2):
        value = pick(head * V, 2 * V)
        for h in (head, head + 1):
            cut = slice(h * V, (h + 1) * V)
            out_ref[:, cut] = (
                part_prefix[:, h : h + 1] * value[:, (h - head) * V : (h - head + 1) * V]
                + part_suffix[:, h : h + 1] * value_ref[:, cut].astype(jnp.float32)
            ).astype(out_ref.dtype)


def merge(prompt, slots, answer, value_suffix, mass_suffix, group):
    forks = value_suffix.shape[0]
    return pl.pallas_call(
        functools.partial(merge_kernel, group),
        out_shape=jax.ShapeDtypeStruct((forks, value_suffix.shape[1]), jnp.bfloat16),
        compiler_params=pltpu.CompilerParams(vmem_limit_bytes=24 << 20),
        name="merge",
    )(prompt, slots, answer, value_suffix, mass_suffix)


def suffix(queries, suffix_cache, suffix_len, w_uv):
    forks = queries.shape[0]
    heads = w_uv.shape[0]
    query_heads = queries.reshape(forks, heads, KEY)
    scores = (
        jnp.einsum("fhe,fes->fhs", query_heads, suffix_cache, preferred_element_type=jnp.float32)
        * SCALE
    )
    positions = jnp.arange(suffix_cache.shape[2], dtype=jnp.int32)
    live = (positions[None, :] < suffix_len[:, None])[:, None, :]
    scores = jnp.where(live, scores, -jnp.inf)
    peak = jnp.max(scores, axis=2, keepdims=True)
    weights = jnp.where(live, jnp.exp(scores - peak), 0.0)
    total = jnp.sum(weights, axis=2)
    summed = jnp.einsum(
        "fhs,frs->fhr",
        weights.astype(jnp.bfloat16),
        suffix_cache[:, :R, :],
        preferred_element_type=jnp.float32,
    )
    latent = (summed / total[..., None]).astype(jnp.bfloat16)
    value = jnp.einsum("nhr,hrv->nhv", latent, w_uv, preferred_element_type=jnp.float32)
    return value.astype(jnp.bfloat16).reshape(forks, heads * V), peak[..., 0] + jnp.log(total)


def shards(queries, prefix_cache, suffix_cache, w_uv, fork_prompt, prompt_slot, suffix_len):
    near = ("zl", "xc")
    group = lax.axis_size("zl") * lax.axis_size("xc")
    held = COPIES * MOST
    slots = prompt_slot[None, :]
    caches = lax.all_gather(prefix_cache, ("zh", "tp"), axis=0, tiled=True)
    outbound = place(fork_prompt, slots, queries, group)
    width = queries.shape[1]
    received = lax.all_to_all(
        outbound.reshape(group, held, width), near, split_axis=0, concat_axis=0, tiled=True
    )
    by_slot = jnp.swapaxes(received, 0, 1).reshape(held * group, width)
    value_suffix, mass_suffix = suffix(queries, suffix_cache, suffix_len, w_uv)
    by_slot, caches, value_suffix, mass_suffix = lax.optimization_barrier(
        (by_slot, caches, value_suffix, mass_suffix)
    )
    result = prefix(by_slot, caches, w_uv, group)
    answer = lax.all_to_all(
        result.reshape(group, held, result.shape[1]), near, split_axis=0, concat_axis=0, tiled=True
    )
    return merge(
        fork_prompt, slots, answer.reshape(result.shape), value_suffix, mass_suffix, group
    )


def solution(mesh):
    owners = mesh.shape["dp"]
    tp = mesh.shape["tp"]
    group = owners // COPIES
    devices = mesh.devices.reshape(COPIES, 2, group // 2, tp)
    split = Mesh(devices, ("zh", "zl", "xc", "tp"))
    dp = ("zh", "zl", "xc")
    placed = (
        P(dp, "tp"),
        P(dp, None, "tp"),
        P(dp, None, None),
        P("tp", None, None),
        P(dp, None),
        P(),
        P(dp),
    )
    return jax.shard_map(
        shards, mesh=split, in_specs=placed, out_specs=P(dp, "tp"), check_vma=False
    )
```

time: 250 us -> 190 us (0.76)
  matrix products: 50.6 us -> 14.2 us
  Pallas kernels: 0 us -> 32.4 us
  starting transfers between devices: 37.4 us -> 7.54 us
  waiting for transfers between devices: 110 us -> 80.4 us
  local copies, waits for them, and re-layouts: 39.7 us -> 16.4 us
  blocking collectives: 0 us -> 22.6 us
  between operations: 0.14 us -> 13.5 us
  other arithmetic: 11.5 us -> 0.73 us
    dot_general x9 -> x3, matrix products: 50.6 us -> 14.2 us  [the longest x1 6.9 us: suffix(): jnp.einsum('fhs,frs->fhr', weights.astype(jnp.bfloat16), suffix_cache[:,...]
    all_to_all x4 -> x1, waiting for transfers between devices: 110 us -> 74.3 us  [shards(): lax.all_to_all(outbound.reshape(group, held, width), near, split_axis=0,...]
    pallas_call x0 -> x3, Pallas kernels: none -> 32.4 us  [the longest x1 22.2 us: prefix(): pl.pallas_call(functools.partial(prefix_kernel, group), out_shape=jax.Sha...]
    all_to_all x4 -> x1, starting transfers between devices: 37.4 us -> 7.5 us  [shards(): lax.all_to_all(outbound.reshape(group, held, width), near, split_axis=0,...]
    reshape x6 -> x2, local copies, waits for them, and re-layouts: 29.3 us -> 4.59 us  [the longest x1 4.49 us: suffix(): query_heads = queries.reshape(forks, heads, KEY)]
    all_to_all x0 -> x1, blocking collectives: none -> 22.6 us  [shards(): lax.all_to_all(result.reshape(group, held, result.shape[1]), near, split_...]
    reduce_sum x4 -> x1, other arithmetic: 11.4 us -> 0.65 us  [suffix(): total = jnp.sum(weights, axis=2)]
    transpose x0 -> x1, local copies, waits for them, and re-layouts: none -> 7.23 us  [shards(): by_slot = jnp.swapaxes(received, 0, 1).reshape(held * group, width)]
  transfers between devices with their start and end apart: 4 -> 2, of which waited for: 3 -> 2; matrix products, arithmetic and copies ran while one was open for 23% -> 14% of each run, Pallas kernels for 0% -> 0%
where the time goes in v1:
time: 190 us; the launch traced here: 188 us
  waiting for transfers between devices  80.4 us (42%)
  Pallas kernels  32.4 us (17%)
  blocking collectives  22.6 us (12%)
  local copies, waits for them, and re-layouts  16.4 us (9%)
  matrix products  14.2 us (7%)
  between operations  13.5 us (7%)
  starting transfers between devices  7.54 us (4%)
    all_to_all x1, waiting for transfers between devices, shards(): lax.all_to_all(outbound.reshape(group, held, width), near, split_axis=0,...  74.3 us
    all_to_all x1, blocking collectives, shards(): lax.all_to_all(result.reshape(group, held, result.shape[1]), near, split_...  22.6 us
    pallas_call x1, Pallas kernels, prefix(): pl.pallas_call(functools.partial(prefix_kernel, group), out_shape=jax.Sha...  22.2 us
    pallas_call x1, Pallas kernels, place(): pl.pallas_call(functools.partial(place_kernel, group), out_shape=jax.Shap...  8.32 us
    all_to_all x1, starting transfers between devices, shards(): lax.all_to_all(outbound.reshape(group, held, width), near, split_axis=0,...  7.5 us
    transpose x1, local copies, waits for them, and re-layouts, shards(): by_slot = jnp.swapaxes(received, 0, 1).reshape(held * group, width)  7.23 us
    dot_general x1, matrix products, suffix(): jnp.einsum('fhs,frs->fhr', weights.astype(jnp.bfloat16), suffix_cache[:,...  6.9 us
    all_gather x1, waiting for transfers between devices, shards(): caches = lax.all_gather(prefix_cache, ('zh', 'tp'), axis=0, tiled=True)  5.45 us
  transfers between devices with their start and end apart: 2, of which 2 were waited for; matrix products, arithmetic and copies ran while one was open for 14% of the time, Pallas kernels for 0%

profile of v1, /device:TPU:1, one launch (start us, length us, event | category | flops | bytes accessed | tf_op | source)
XLA Modules:
  0.0 187.9 jit_solution(6557765627320810213)
XLA Ops:
  6.5 1.4 copy.17.prompt_ref
  7.9 8.3 %place.1 = bf16[128,18432]{1,0:T(8,128)(2,1)} custom-call(s32[64,1]{1,0:T(8,128)} %copy.17.prompt_ref, s32[1,64]{1,0:T(1,128)} %bitcast.18, bf16[64,18432]{1,0:T(8,128)(2,1)} %q_ref.1), custom_call_target="tpu_custom_call" | custom-call | tf_op jit(solution)/shard_map/place/pallas_call | solution.py:55
  16.2 7.5 %all-to-all-start = ((bf16[16,8,18432]{2,1,0:T(8,128)(2,1)}), bf16[16,8,18432]{2,1,0:T(8,128)(2,1)}, u32[]{:S(2)}, u32[]{:S(2)}) async-start(bf16[16,8,18432]{2,1,0:T(8,128)(2,1)} %bitcast.20), calls=%async_computation | async-start | bytes 9437184 | tf_op jit(solution)/shard_map/all_to_all | solution.py:243
  23.7 0.0 copy-start.5
  23.7 0.0 all-gather.2.cloned.1.call-start
  23.8 0.7 all-gather.2.cloned.1.call-update
  24.5 4.5 %reshape.39 = bf16[64,32,576]{2,1,0:T(8,128)(2,1)S(1)} reshape(bf16[64,18432]{1,0:T(8,128)(2,1)} %q_ref.1) | data formatting | bytes 4718592 | tf_op jit(solution)/shard_map/reshape | solution.py:213
  29.0 0.0 copy-done.5
  29.0 0.1 iota_compare_fusion
  29.0 4.7 %fusion.19 = (f32[64,32]{1,0:T(8,128)S(1)}, f32[64,32,128]{2,1,0:T(8,128)S(1)}) fusion(bf16[64,32,576]{2,1,0:T(8,128)(2,1)S(1)} %reshape.39, bf16[64,576,128]{2,1,0:T(8,128)(2,1)} %param.9, pred[64,128]{1,0:T(8,128)(4,1)S(1)} %iota_compare_fusion), kind=kOutput, calls=%fused_computation.19 | convolution fusion | flops 302774272 | bytes 12861440 | tf_op jit(solution)/shard_map/fhe,fes->fhs/dot_general | solution.py:215
  33.8 0.0 copy-start.4
  33.8 1.0 copy-done.4
  34.8 0.6 fusion.12
  35.4 0.1 copy.15
  35.5 0.0 copy-start
  35.5 6.9 %fusion = f32[64,32,512]{2,1,0:T(8,128)S(1)} fusion(bf16[64,576,128]{2,1,0:T(8,128)(2,1)} %param.9, f32[64,32,128]{2,1,0:T(8,128)} %copy-done.4, f32[64,32]{1,0:T(8,128)S(1)} %get-tuple-element.13, pred[64,128]{1,0:T(8,128)(4,1)S(1)} %iota_compare_fusion), kind=kOutput, calls=%fused_computation | convolution fusion | flops 269221888 | bytes 13647872 | tf_op jit(solution)/shard_map/fhs,frs->fhr/dot_general | solution.py:224
  42.4 0.0 copy-done
  42.4 2.6 %fusion.9 = bf16[32,8,8,128]{3,2,1,0:T(8,128)(2,1)S(1)} fusion(bf16[32,512,128]{2,1,0:T(8,128)(2,1)S(1)} %copy-done, f32[64,32,512]{2,1,0:T(8,128)S(1)} %fusion, f32[64,32]{0,1:T(8,128)S(1)} %copy.15), kind=kOutput, calls=%fused_computation.8 | convolution fusion | flops 270794752 | bytes 8921088 | tf_op jit(solution)/shard_map/nhr,hrv->nhv/dot_general | solution.py:231
  45.0 0.1 copy.29
  45.1 74.3 %all-to-all-done = bf16[16,8,18432]{2,1,0:T(8,128)(2,1)} async-done(((bf16[16,8,18432]{2,1,0:T(8,128)(2,1)}), bf16[16,8,18432]{2,1,0:T(8,128)(2,1)}, u32[]{:S(2)}, u32[]{:S(2)}) %all-to-all-start) | async-done | bytes 4718624 | tf_op jit(solution)/shard_map/all_to_all | solution.py:243
  119.4 7.2 %copy.14 = bf16[8,16,18432]{2,1,0:T(8,128)(2,1)} copy(bf16[8,16,18432]{2,0,1:T(8,128)(2,1)} %bitcast.2) | data formatting | bytes 9437184 | tf_op jit(solution)/shard_map/transpose | solution.py:246
  126.7 5.4 %all-gather.2.cloned.1.call-done.kv_ref = bf16[16,576,256]{2,1,0:T(8,128)(2,1)} async-done(((bf16[1,576,256]{2,1,0:T(8,128)(2,1)}), bf16[16,576,256]{2,1,0:T(8,128)(2,1)}) %all-gather.2.cloned.1.call-update) | async-done | bytes 4718608 | tf_op jit(solution)/shard_map/all_gather | solution.py:240
  132.1 0.0 copy-start.1
  132.1 2.2 %copy-done.1 = bf16[32,512,128]{2,1,0:T(8,128)(2,1)S(1)} copy-done((bf16[32,512,128]{2,1,0:T(8,128)(2,1)S(1)}, bf16[32,512,128]{2,1,0:T(8,128)(2,1)}, u32[]{:S(2)}) %copy-start.1) | copy-done | bytes 4194328
  134.3 0.0 copy-start.2
  134.3 0.0 copy-start.3
  134.3 22.2 %prefix.1 = bf16[128,4352]{1,0:T(8,128)(2,1)S(1)} custom-call(bf16[128,18432]{1,0:T(8,128)(2,1)} %bitcast.21, bf16[16,576,256]{2,1,0:T(8,128)(2,1)} %all-gather.2.cloned.1.call-done.kv_ref, bf16[32,512,128]{2,1,0:T(8,128)(2,1)S(1)} %copy-done.1), custom_call_target="tpu_custom_call" | custom-call | tf_op jit(solution)/shard_map/prefix/pallas_call | solution.py:149
  156.5 22.6 %all_to_all.10 = bf16[16,8,4352]{2,1,0:T(8,128)(2,1)S(1)} all-to-all(bf16[16,8,4352]{2,1,0:T(8,128)(2,1)S(1)} %bitcast.15), channel_id=1, replica_groups=mesh['zh'=4,'zl'=2,'xc'=8,'tp'=4] {'zl','xc'}, dimensions={0} | all-to-all | bytes 2228224 | tf_op jit(solution)/shard_map/all_to_all | solution.py:252
  179.1 0.0 copy-done.2
  179.1 0.0 copy-done.3
  179.1 1.9 %merge.1 = bf16[64,4096]{1,0:T(8,128)(2,1)} custom-call(s32[64,1]{1,0:T(8,128)S(1)} %copy-done.2, s32[1,64]{1,0:T(1,128)S(1)} %bitcast.19, bf16[128,4352]{1,0:T(8,128)(2,1)S(1)} %bitcast.16, bf16[64,4096]{1,0:T(8,128)(2,1)S(1)} %bitcast.17, f32[64,32]{1,0:T(8,128)S(1)} %log_add_fusion.mass_ref), custom_call_target="tpu_custom_call" | custom-call | tf_op jit(solution)/shard_map/merge/pallas_call | solution.py:202
  (1 shorter events, 0.0 us)
Async XLA Ops:
  16.2 103.2 %all-to-all-start = ((bf16[16,8,18432]{2,1,0:T(8,128)(2,1)}), bf16[16,8,18432]{2,1,0:T(8,128)(2,1)}, u32[]{:S(2)}, u32[]{:S(2)}) async-start(bf16[16,8,18432]{2,1,0:T(8,128)(2,1)} %bitcast.20), calls=%async_computation | async-start | bytes 9437184 | tf_op jit(solution)/shard_map/all_to_all | solution.py:243
  23.7 5.2 %copy-start.5 = (s32[64]{0:T(128)S(1)}, s32[64]{0:T(128)}, u32[]{:S(2)}) copy-start(s32[64]{0:T(128)} %param.13) | copy-start | bytes 772
  23.7 108.4 %all-gather.2.cloned.1.call-start = ((), (), s32[]{:S(2)}) async-start(), calls=%async_computation.2 | async-start | bytes 5013504 | tf_op jit(solution)/shard_map/all_gather | solution.py:240
  33.8 1.0 copy-start.4
  35.5 6.9 %copy-start = (bf16[32,512,128]{2,1,0:T(8,128)(2,1)S(1)}, bf16[32,512,128]{2,1,0:T(8,128)(2,1)}, u32[]{:S(2)}) copy-start(bf16[32,512,128]{2,1,0:T(8,128)(2,1)} %w_ref.1) | copy-start | bytes 12582916
  132.1 2.2 %copy-start.1 = (bf16[32,512,128]{2,1,0:T(8,128)(2,1)S(1)}, bf16[32,512,128]{2,1,0:T(8,128)(2,1)}, u32[]{:S(2)}) copy-start(bf16[32,512,128]{2,1,0:T(8,128)(2,1)} %w_ref.1) | copy-start | bytes 12582916
  134.3 44.8 %copy-start.2 = (s32[64,1]{1,0:T(8,128)S(1)}, s32[64,1]{1,0:T(8,128)}, u32[]{:S(2)}) copy-start(s32[64,1]{1,0:T(8,128)} %copy.17.prompt_ref) | copy-start | bytes 772
  134.3 44.8 %copy-start.3 = (s32[64]{0:T(128)S(1)}, s32[64]{0:T(128)}, u32[]{:S(2)}) copy-start(s32[64]{0:T(128)} %param.12) | copy-start | bytes 772
Sparse Core Ops, SparseCore 0:
  27.0 105.0 all-gather.1

commit v2 on v1

v2 whole, which is shorter than its diff:
```python
import jax
import jax.numpy as jnp
from jax import lax
from jax.experimental import pallas as pl
from jax.experimental.pallas import tpu as pltpu
from jax.sharding import Mesh
from jax.sharding import PartitionSpec as P

R = 512
P_SIZE = 64
V = 128
KEY = R + P_SIZE
MOST = 2
COPIES = 4
SPLIT = 4
LANES = 128
SCALE = 192.0 ** (-0.5)
LOG2E = 1.4426950408889634


def row_targets(prompt_col, base_row):
    forks = prompt_col.shape[0]
    prompts = base_row.shape[1]
    ids = lax.broadcasted_iota(jnp.int32, (forks, prompts), 1)
    base = jnp.sum(jnp.where(prompt_col == ids, base_row, 0), axis=1, keepdims=True)
    down = lax.broadcasted_iota(jnp.int32, (forks, forks), 0)
    along = lax.broadcasted_iota(jnp.int32, (forks, forks), 1)

    def turned(column):
        return jnp.sum(jnp.where(down == along, column, 0), axis=0, keepdims=True)

    before = (base == turned(base)) & (along < down)
    target = base + jnp.sum(before.astype(jnp.int32), axis=1, keepdims=True)
    return turned(target), target


def place_kernel(prompt_ref, base_ref, *refs):
    parts = refs[:SPLIT]
    out_ref, placing_ref = refs[SPLIT:]
    forks = parts[0].shape[0]

    @pl.when(pl.program_id(0) == 0)
    def _():
        target_row, _ = row_targets(prompt_ref[...], base_ref[...])
        at = lax.broadcasted_iota(jnp.int32, (out_ref.shape[0], forks), 0)
        for n in range(SPLIT):
            placing_ref[:, n * forks : (n + 1) * forks] = (at == target_row * SPLIT + n).astype(
                jnp.bfloat16
            )

    stacked = jnp.concatenate([part[...] for part in parts], axis=0)
    out_ref[...] = jnp.dot(
        placing_ref[...], stacked, preferred_element_type=jnp.float32
    ).astype(jnp.bfloat16)


def place(prompt, base, queries, group):
    forks, width = queries.shape
    rows = group * COPIES * MOST * SPLIT
    part = width // SPLIT
    steps = 6
    tile = part // steps

    def part_spec(n):
        return pl.BlockSpec((forks, tile), lambda i: (0, n * steps + i))

    return pl.pallas_call(
        place_kernel,
        out_shape=jax.ShapeDtypeStruct((rows, part), jnp.bfloat16),
        grid=(steps,),
        in_specs=[
            pl.BlockSpec(prompt.shape, lambda i: (0, 0)),
            pl.BlockSpec(base.shape, lambda i: (0, 0)),
            *[part_spec(n) for n in range(SPLIT)],
        ],
        out_specs=pl.BlockSpec((rows, tile), lambda i: (0, i)),
        scratch_shapes=[pltpu.VMEM((rows, SPLIT * forks), jnp.bfloat16)],
        name="place",
    )(prompt, base, *[queries] * SPLIT)


def prefix_kernel(
    q_ref, kv_ref, w_hbm, out_ref, w_ref, key_ref, lat_ref, part_ref, cell_ref, mass_ref, sem
):
    step = pl.program_id(0)
    last = pl.num_programs(0) - 1
    heads = w_ref.shape[0]
    group = q_ref.shape[0]
    held = COPIES * MOST
    quarter = kv_ref.shape[2]
    fetch = pltpu.make_async_copy(w_hbm, w_ref, sem)

    @pl.when(step == 0)
    def _():
        fetch.start()
        zero = jnp.zeros((P_SIZE, key_ref.shape[1]), key_ref.dtype)
        key_ref[0:P_SIZE, :] = zero
        key_ref[P_SIZE + KEY : P_SIZE + KEY + P_SIZE, :] = zero

    for n in range(kv_ref.shape[0]):
        key_ref[P_SIZE : P_SIZE + KEY, n * quarter : (n + 1) * quarter] = kv_ref[n]

    wide = KEY + P_SIZE
    tall = group * MOST * SPLIT
    span = group * MOST
    pairs = heads // SPLIT // 2
    lane = lax.broadcasted_iota(jnp.int32, (tall, LANES), 1)
    cells = jnp.zeros((tall, LANES), jnp.float32)
    rows = pl.ds(pl.multiple_of(step * span, span), span)

    def score(odd):
        query = jnp.concatenate(
            [
                q_ref[:, :, p * 2 * KEY + odd * R : p * 2 * KEY + odd * R + wide].reshape(
                    tall, wide
                )
                for p in range(pairs)
            ],
            axis=0,
        )
        first = 0 if odd else P_SIZE
        return jnp.dot(query, key_ref[first : first + wide, :], preferred_element_type=jnp.float32)

    ahead = [score(0), score(1)]
    for odd in range(2):
        scores = ahead[odd]
        peak = jnp.max(scores, axis=1, keepdims=True)
        weights = jnp.exp2((scores - peak) * (SCALE * LOG2E))
        total = jnp.sum(weights, axis=1, keepdims=True)
        summed = lax.dot_general(
            weights.astype(jnp.bfloat16),
            key_ref[P_SIZE : P_SIZE + R, :],
            (((1,), (1,)), ((), ())),
            preferred_element_type=jnp.float32,
        )
        latent = summed / total
        for b in range(R // LANES):
            part_ref[b] = latent[:, b * LANES : (b + 1) * LANES]
        mass = peak * SCALE + jnp.log(total)
        for p in range(pairs):
            cells = jnp.where(lane == 2 * p + odd, mass[p * tall : (p + 1) * tall], cells)
            for n in range(SPLIT):
                head = n * 2 * pairs + 2 * p + odd
                for b in range(R // LANES):
                    lat_ref[head, rows, b * LANES : (b + 1) * LANES] = part_ref[
                        b, pl.ds(p * tall + n, span, stride=SPLIT), :
                    ].astype(jnp.bfloat16)
    cell_ref[...] = cells
    masses = jnp.zeros((span, LANES), jnp.float32)
    for n in range(SPLIT):
        block = cell_ref[pl.ds(n, span, stride=SPLIT), :]
        masses = masses + (pltpu.roll(block, n * 2 * pairs, 1) if n else block)
    mass_ref[rows, :] = masses

    @pl.when(step == last)
    def _():
        fetch.wait()
        count = mass_ref.shape[0]
        to = lax.broadcasted_iota(jnp.int32, (count, count), 0)
        come = lax.broadcasted_iota(jnp.int32, (count, count), 1)
        source, slot = to // held, to % held
        turn = (come == (slot // MOST) * span + source * MOST + slot % MOST).astype(jnp.bfloat16)

        def put(at, block):
            out_ref[:, at : at + block.shape[1]] = jnp.dot(
                turn, block, preferred_element_type=jnp.float32
            ).astype(jnp.bfloat16)

        for head in range(0, heads, 2):
            both = [
                jnp.dot(lat_ref[h], w_ref[h], preferred_element_type=jnp.float32)
                for h in (head, head + 1)
            ]
            put(head * V, jnp.concatenate(both, axis=1).astype(jnp.bfloat16))
        high = mass_ref[...].astype(jnp.bfloat16)
        low = (mass_ref[...] - high.astype(jnp.float32)).astype(jnp.bfloat16)
        put(heads * V, jnp.concatenate([high, low], axis=1))


def prefix(received, caches, w_uv):
    group, _, part = received.shape
    heads = w_uv.shape[0]
    rows = group * COPIES * MOST
    tall = group * MOST * SPLIT
    parts = caches.shape[0] // COPIES
    length = parts * caches.shape[2]
    caches = caches.reshape(parts, COPIES, *caches.shape[1:])
    wide = heads * V + 2 * LANES
    return pl.pallas_call(
        prefix_kernel,
        out_shape=jax.ShapeDtypeStruct((rows, wide), jnp.bfloat16),
        grid=(COPIES,),
        in_specs=[
            pl.BlockSpec((group, MOST * SPLIT, part), lambda i: (0, i, 0)),
            pl.BlockSpec((parts, None, *caches.shape[2:]), lambda i: (0, i, 0, 0)),
            pl.BlockSpec(memory_space=pl.ANY),
        ],
        out_specs=pl.BlockSpec((rows, wide), lambda i: (0, 0)),
        scratch_shapes=[
            pltpu.VMEM(w_uv.shape, jnp.bfloat16),
            pltpu.VMEM((KEY + 2 * P_SIZE, length), jnp.bfloat16),
            pltpu.VMEM((heads, rows, R), jnp.bfloat16),
            pltpu.VMEM((R // LANES, heads // SPLIT // 2 * tall, LANES), jnp.float32),
            pltpu.VMEM((tall, LANES), jnp.float32),
            pltpu.VMEM((rows, LANES), jnp.float32),
            pltpu.SemaphoreType.DMA,
        ],
        compiler_params=pltpu.CompilerParams(vmem_limit_bytes=52 << 20),
        name="prefix",
    )(received, caches, w_uv)


def merge_kernel(prompt_ref, base_ref, answer_ref, value_ref, mass_ref, out_ref):
    _, target = row_targets(prompt_ref[...], base_ref[...])
    forks, heads = mass_ref.shape
    rows = answer_ref.shape[0]
    at = lax.broadcasted_iota(jnp.int32, (forks, rows), 1)
    picking = (at == target).astype(jnp.bfloat16)

    def pick(start, size):
        return jnp.dot(
            picking, answer_ref[:, start : start + size], preferred_element_type=jnp.float32
        )

    come = pick(heads * V, 2 * LANES)
    mass_prefix = come[:, :heads] + come[:, LANES : LANES + heads]
    mass_suffix = mass_ref[...]
    top = jnp.maximum(mass_prefix, mass_suffix)
    share_prefix = jnp.exp(mass_prefix - top)
    share_suffix = jnp.exp(mass_suffix - top)
    both = share_prefix + share_suffix
    part_prefix = share_prefix / both
    part_suffix = share_suffix / both
    for head in range(0, heads, 2):
        value = pick(head * V, 2 * V)
        for h in (head, head + 1):
            cut = slice(h * V, (h + 1) * V)
            out_ref[:, cut] = (
                part_prefix[:, h : h + 1] * value[:, (h - head) * V : (h - head + 1) * V]
                + part_suffix[:, h : h + 1] * value_ref[:, cut].astype(jnp.float32)
            ).astype(out_ref.dtype)


def merge(prompt, base, answer, value_suffix, mass_suffix):
    forks = value_suffix.shape[0]
    return pl.pallas_call(
        merge_kernel,
        out_shape=jax.ShapeDtypeStruct((forks, value_suffix.shape[1]), jnp.bfloat16),
        compiler_params=pltpu.CompilerParams(vmem_limit_bytes=24 << 20),
        name="merge",
    )(prompt, base, answer, value_suffix, mass_suffix)


def suffix(queries, suffix_cache, suffix_len, w_uv):
    forks = queries.shape[0]
    heads = w_uv.shape[0]
    query_heads = queries.reshape(forks, heads, KEY)
    scores = (
        jnp.einsum("fhe,fes->fhs", query_heads, suffix_cache, preferred_element_type=jnp.float32)
        * SCALE
    )
    positions = jnp.arange(suffix_cache.shape[2], dtype=jnp.int32)
    live = (positions[None, :] < suffix_len[:, None])[:, None, :]
    scores = jnp.where(live, scores, -jnp.inf)
    peak = jnp.max(scores, axis=2, keepdims=True)
    weights = jnp.where(live, jnp.exp(scores - peak), 0.0)
    total = jnp.sum(weights, axis=2)
    summed = jnp.einsum(
        "fhs,frs->fhr",
        weights.astype(jnp.bfloat16),
        suffix_cache[:, :R, :],
        preferred_element_type=jnp.float32,
    )
    latent = (summed / total[..., None]).astype(jnp.bfloat16)
    value = jnp.einsum("nhr,hrv->nhv", latent, w_uv, preferred_element_type=jnp.float32)
    return value.astype(jnp.bfloat16).reshape(forks, heads * V), peak[..., 0] + jnp.log(total)


def shards(queries, prefix_cache, suffix_cache, w_uv, fork_prompt, prompt_slot, suffix_len):
    near = ("zl", "xc")
    group = lax.axis_size("zl") * lax.axis_size("xc")
    held = COPIES * MOST
    back = (lax.axis_index("zh") - prompt_slot // group) % COPIES
    base = ((prompt_slot % group) * held + back * MOST)[None, :].astype(jnp.int32)

    def from_behind(steps):
        return lax.ppermute(
            prefix_cache, "zh", [(n, (n + steps) % COPIES) for n in range(COPIES)]
        )

    moved = [from_behind(1), from_behind(3), from_behind(2)]
    outbound = place(fork_prompt, base, queries, group)
    outbound, *moved = lax.optimization_barrier((outbound, *moved))
    stacked = jnp.concatenate([prefix_cache, moved[0], moved[2], moved[1]], axis=0)
    caches = lax.all_gather(stacked, "tp", axis=0, tiled=True)
    received = lax.all_to_all(
        outbound.reshape(group, held * SPLIT, queries.shape[1] // SPLIT),
        near,
        split_axis=0,
        concat_axis=0,
        tiled=True,
    )
    value_suffix, mass_suffix = suffix(queries, suffix_cache, suffix_len, w_uv)
    received, caches, value_suffix, mass_suffix = lax.optimization_barrier(
        (received, caches, value_suffix, mass_suffix)
    )
    result = prefix(received, caches, w_uv)
    answer = lax.all_to_all(
        result.reshape(group, held, result.shape[1]), near, split_axis=0, concat_axis=0, tiled=True
    )
    return merge(fork_prompt, base, answer.reshape(result.shape), value_suffix, mass_suffix)


def solution(mesh):
    owners = mesh.shape["dp"]
    tp = mesh.shape["tp"]
    group = owners // COPIES
    devices = mesh.devices.reshape(COPIES, 2, group // 2, tp)
    split = Mesh(devices, ("zh", "zl", "xc", "tp"))
    dp = ("zh", "zl", "xc")
    placed = (
        P(dp, "tp"),
        P(dp, None, "tp"),
        P(dp, None, None),
        P("tp", None, None),
        P(dp, None),
        P(),
        P(dp),
    )
    return jax.shard_map(
        shards, mesh=split, in_specs=placed, out_specs=P(dp, "tp"), check_vma=False
    )
```

time: 190 us -> 169 us (0.89)
  waiting for transfers between devices: 80.4 us -> 50.7 us
  starting transfers between devices: 7.54 us -> 25 us
  local copies, waits for them, and re-layouts: 16.4 us -> 5.59 us
  blocking collectives: 22.6 us -> 28.5 us
  Pallas kernels: 32.4 us -> 27.3 us
  other arithmetic: 0.73 us -> 3.07 us
    all_to_all x1, waiting for transfers between devices: 74.3 us -> 7.7 us  [shards(): lax.all_to_all(outbound.reshape(group, held * SPLIT, queries.shape[1] //...]
    all_gather x1, waiting for transfers between devices: 5.45 us -> 34.7 us  [shards(): caches = lax.all_gather(stacked, 'tp', axis=0, tiled=True)]
    ppermute x0 -> x3, starting transfers between devices: none -> 10.1 us  [from_behind(): lax.ppermute(prefix_cache, 'zh', [(n, (n + steps) % COPIES) for n in rang...]
    ppermute x0 -> x3, waiting for transfers between devices: none -> 8.3 us  [from_behind(): lax.ppermute(prefix_cache, 'zh', [(n, (n + steps) % COPIES) for n in rang...]
    transpose x1 -> x0, local copies, waits for them, and re-layouts: 7.23 us -> none  [shards(): by_slot = jnp.swapaxes(received, 0, 1).reshape(held * group, width)]
    all_to_all x1, starting transfers between devices: 7.5 us -> 14.7 us  [shards(): lax.all_to_all(outbound.reshape(group, held * SPLIT, queries.shape[1] //...]
    all_to_all x1, blocking collectives: 22.6 us -> 28.5 us  [shards(): lax.all_to_all(result.reshape(group, held, result.shape[1]), near, split_...]
    pallas_call x3, Pallas kernels: 32.4 us -> 27.3 us  [the longest x1 18.4 us: prefix(): pl.pallas_call(prefix_kernel, out_shape=jax.ShapeDtypeStruct((rows, wide)...]
  transfers between devices with their start and end apart: 2 -> 5, of which waited for: 2 -> 4; matrix products, arithmetic and copies ran while one was open for 14% -> 14% of each run, Pallas kernels for 0% -> 4%
where the time goes in v2:
time: 169 us; the launch traced here: 168 us
  waiting for transfers between devices  50.7 us (30%)
  blocking collectives  28.5 us (17%)
  Pallas kernels  27.3 us (16%)
  starting transfers between devices  25 us (15%)
  matrix products  14.7 us (9%)
  between operations  13.5 us (8%)
  local copies, waits for them, and re-layouts  5.59 us (3%)
  other arithmetic  3.07 us (2%)
    all_gather x1, waiting for transfers between devices, shards(): caches = lax.all_gather(stacked, 'tp', axis=0, tiled=True)  34.7 us
    all_to_all x1, blocking collectives, shards(): lax.all_to_all(result.reshape(group, held, result.shape[1]), near, split_...  28.5 us
    pallas_call x1, Pallas kernels, prefix(): pl.pallas_call(prefix_kernel, out_shape=jax.ShapeDtypeStruct((rows, wide)...  18.4 us
    all_to_all x1, starting transfers between devices, shards(): lax.all_to_all(outbound.reshape(group, held * SPLIT, queries.shape[1] //...  14.7 us
    ppermute x3, starting transfers between devices, from_behind(): lax.ppermute(prefix_cache, 'zh', [(n, (n + steps) % COPIES) for n in rang...  10.1 us
    ppermute x3, waiting for transfers between devices, from_behind(): lax.ppermute(prefix_cache, 'zh', [(n, (n + steps) % COPIES) for n in rang...  8.3 us
    all_to_all x1, waiting for transfers between devices, shards(): lax.all_to_all(outbound.reshape(group, held * SPLIT, queries.shape[1] //...  7.7 us
    pallas_call x1, Pallas kernels, place(): pl.pallas_call(place_kernel, out_shape=jax.ShapeDtypeStruct((rows, part),...  7 us
  transfers between devices with their start and end apart: 5, of which 4 were waited for; matrix products, arithmetic and copies ran while one was open for 14% of the time, Pallas kernels for 4%

profile of v2, /device:TPU:1, one launch (start us, length us, event | category | flops | bytes accessed | tf_op | source)
XLA Modules:
  0.0 168.3 jit_solution(4382397562346489191)
XLA Ops:
  6.5 6.8 %collective-permute-start.1 = (bf16[1,576,256]{2,1,0:T(8,128)(2,1)}, bf16[1,576,256]{2,1,0:T(8,128)(2,1)S(1)}, u32[]{:S(2)}, u32[]{:S(2)}) collective-permute-start(bf16[1,576,256]{2,1,0:T(8,128)(2,1)} %param.8), channel_id=1, source_target_pairs={{0,192},{64,0},{128,64},{192,128},{1,193},{65,1},{129,65},{193,129... | collective-permute-start | bytes 884744 | tf_op jit(solution)/shard_map/ppermute | solution.py:287
  13.4 0.0 collective-permute-start
  13.4 3.3 %collective-permute-start.2 = (bf16[1,576,256]{2,1,0:T(8,128)(2,1)}, bf16[1,576,256]{2,1,0:T(8,128)(2,1)S(1)}, u32[]{:S(2)}, u32[]{:S(2)}) collective-permute-start(bf16[1,576,256]{2,1,0:T(8,128)(2,1)} %param.8), channel_id=1, source_target_pairs={{0,128},{64,192},{128,0},{192,64},{1,129},{65,193},{129,1},{193,65... | collective-permute-start | bytes 884744 | tf_op jit(solution)/shard_map/ppermute | solution.py:287
  16.6 1.4 copy.15.prompt_ref
  18.0 1.2 fusion.22.base_ref
  19.2 7.0 %place.1 = bf16[512,4608]{1,0:T(8,128)(2,1)} custom-call(s32[64,1]{1,0:T(8,128)} %copy.15.prompt_ref, s32[1,64]{1,0:T(1,128)} %fusion.22.base_ref, bf16[64,18432]{1,0:T(8,128)(2,1)} %refs_3_.1, bf16[64,18432]{1,0:T(8,128)(2,1)} %refs_3_.1, bf16[64,18432]{1,0:T(8,128)(2,1)} %refs_3_.1, bf16[64,18432]{1,0:T(8,128)(2,1)} %refs_3_.1), custom_call_target="tpu_custom_call" | custom-call | tf_op jit(solution)/shard_map/place/pallas_call | solution.py:67
  26.1 1.5 collective-permute-done.1
  27.6 0.0 collective-permute-done
  27.6 6.8 %collective-permute-done.2 = bf16[1,576,256]{2,1,0:T(8,128)(2,1)S(1)} collective-permute-done((bf16[1,576,256]{2,1,0:T(8,128)(2,1)}, bf16[1,576,256]{2,1,0:T(8,128)(2,1)S(1)}, u32[]{:S(2)}, u32[]{:S(2)}) %collective-permute-start.2) | collective-permute-done | bytes 294944 | tf_op jit(solution)/shard_map/ppermute | solution.py:287
  34.5 0.0 copy-start.4
  34.5 0.0 copy-start.2
  34.5 14.7 %all-to-all-start = ((bf16[16,32,4608]{2,1,0:T(8,128)(2,1)}), bf16[16,32,4608]{2,1,0:T(8,128)(2,1)}, u32[]{:S(2)}, u32[]{:S(2)}) async-start(bf16[16,32,4608]{2,1,0:T(8,128)(2,1)} %bitcast.18), calls=%async_computation | async-start | bytes 9437184 | tf_op jit(solution)/shard_map/all_to_all | solution.py:296
  49.1 0.0 copy-start.5
  49.1 0.2 all-gather.2.cloned.1.call-start
  49.4 0.0 copy-done.4
  49.4 1.2 pad_maximum_fusion
  50.6 0.0 all-gather.2.cloned.1.call-update
  50.6 0.0 copy-done.2
  50.6 4.0 %reshape.38 = bf16[64,32,576]{2,1,0:T(8,128)(2,1)} reshape(bf16[64,18432]{1,0:T(8,128)(2,1)S(1)} %copy-done.2) | data formatting | bytes 4718592 | tf_op jit(solution)/shard_map/reshape | solution.py:257
  54.6 0.0 copy-done.5
  54.6 0.1 iota_compare_fusion
  54.7 6.2 %fusion.24 = (f32[64,32]{1,0:T(8,128)S(1)}, f32[64,32,128]{2,1,0:T(8,128)S(1)}) fusion(bf16[64,32,576]{2,1,0:T(8,128)(2,1)} %reshape.38, bf16[64,576,128]{2,1,0:T(8,128)(2,1)} %param.9, pred[64,128]{1,0:T(8,128)(4,1)S(1)} %iota_compare_fusion), kind=kOutput, calls=%fused_computation.33 | convolution fusion | flops 302774272 | bytes 12861440 | tf_op jit(solution)/shard_map/fhe,fes->fhs/dot_general | solution.py:259
  60.9 0.6 fusion.12
  61.6 0.1 copy.13
  61.6 0.0 copy-start.3
  61.6 5.9 %fusion = f32[64,32,512]{2,1,0:T(8,128)S(1)} fusion(bf16[64,576,128]{2,1,0:T(8,128)(2,1)} %param.9, f32[64,32,128]{2,1,0:T(8,128)S(1)} %get-tuple-element.22, f32[64,32]{1,0:T(8,128)S(1)} %get-tuple-element.21, pred[64,128]{1,0:T(8,128)(4,1)S(1)} %iota_compare_fusion), kind=kOutput, calls=%fused_computation | convolution fusion | flops 269221888 | bytes 13647872 | tf_op jit(solution)/shard_map/fhs,frs->fhr/dot_general | solution.py:268
  67.6 0.0 copy-done.3
  67.6 2.6 %fusion.9 = bf16[32,8,8,128]{3,2,1,0:T(8,128)(2,1)S(1)} fusion(bf16[32,512,128]{2,1,0:T(8,128)(2,1)S(1)} %copy-done.3, f32[64,32,512]{2,1,0:T(8,128)S(1)} %fusion, f32[64,32]{0,1:T(8,128)S(1)} %copy.13), kind=kOutput, calls=%fused_computation.8 | convolution fusion | flops 270794752 | bytes 8921088 | tf_op jit(solution)/shard_map/nhr,hrv->nhv/dot_general | solution.py:275
  70.2 0.1 copy.27
  70.3 34.7 %all-gather.2.cloned.1.call-done = bf16[16,576,256]{2,1,0:T(8,128)(2,1)} async-done(((bf16[4,576,256]{2,1,0:T(8,128)(2,1)}), bf16[16,576,256]{2,1,0:T(8,128)(2,1)}) %all-gather.2.cloned.1.call-update) | async-done | bytes 4718608 | tf_op jit(solution)/shard_map/all_gather | solution.py:295
  105.0 7.7 %all-to-all-done.q_ref = bf16[16,32,4608]{2,1,0:T(8,128)(2,1)} async-done(((bf16[16,32,4608]{2,1,0:T(8,128)(2,1)}), bf16[16,32,4608]{2,1,0:T(8,128)(2,1)}, u32[]{:S(2)}, u32[]{:S(2)}) %all-to-all-start) | async-done | bytes 4718624 | tf_op jit(solution)/shard_map/all_to_all | solution.py:296
  112.7 0.0 copy-start
  112.7 0.0 copy-start.1
  112.7 18.4 %prefix.1 = bf16[128,4352]{1,0:T(8,128)(2,1)S(1)} custom-call(bf16[16,32,4608]{2,1,0:T(8,128)(2,1)} %all-to-all-done.q_ref, bf16[4,4,576,256]{3,2,1,0:T(8,128)(2,1)} %bitcast.19, bf16[32,512,128]{2,1,0:T(8,128)(2,1)} %w_hbm.1), custom_call_target="tpu_custom_call" | custom-call | tf_op jit(solution)/shard_map/prefix/pallas_call | solution.py:189
  131.0 28.5 %all_to_all.10 = bf16[16,8,4352]{2,1,0:T(8,128)(2,1)S(1)} all-to-all(bf16[16,8,4352]{2,1,0:T(8,128)(2,1)S(1)} %bitcast.15), channel_id=1, replica_groups=mesh['zh'=4,'zl'=2,'xc'=8,'tp'=4] {'zl','xc'}, dimensions={0} | all-to-all | bytes 2228224 | tf_op jit(solution)/shard_map/all_to_all | solution.py:308
  159.5 0.0 copy-done
  159.5 0.0 copy-done.1
  159.5 1.9 %merge.1 = bf16[64,4096]{1,0:T(8,128)(2,1)} custom-call(s32[64,1]{1,0:T(8,128)S(1)} %copy-done, s32[1,64]{1,0:T(1,128)S(1)} %copy-done.1, bf16[128,4352]{1,0:T(8,128)(2,1)S(1)} %bitcast.16, bf16[64,4096]{1,0:T(8,128)(2,1)S(1)} %bitcast.17, f32[64,32]{1,0:T(8,128)S(1)} %log_add_fusion.mass_ref), custom_call_target="tpu_custom_call" | custom-call | tf_op jit(solution)/shard_map/merge/pallas_call | solution.py:246
  (1 shorter events, 0.0 us)
Async XLA Ops:
  6.5 21.1 %collective-permute-start.1 = (bf16[1,576,256]{2,1,0:T(8,128)(2,1)}, bf16[1,576,256]{2,1,0:T(8,128)(2,1)S(1)}, u32[]{:S(2)}, u32[]{:S(2)}) collective-permute-start(bf16[1,576,256]{2,1,0:T(8,128)(2,1)} %param.8), channel_id=1, source_target_pairs={{0,192},{64,0},{128,64},{192,128},{1,193},{65,1},{129,65},{193,129... | collective-permute-start | bytes 884744 | tf_op jit(solution)/shard_map/ppermute | solution.py:287
  13.4 14.2 %collective-permute-start = (bf16[1,576,256]{2,1,0:T(8,128)(2,1)}, bf16[1,576,256]{2,1,0:T(8,128)(2,1)S(1)}, u32[]{:S(2)}, u32[]{:S(2)}) collective-permute-start(bf16[1,576,256]{2,1,0:T(8,128)(2,1)} %param.8), channel_id=1, source_target_pairs={{0,64},{64,128},{128,192},{192,0},{1,65},{65,129},{129,193},{193,1... | collective-permute-start | bytes 884744 | tf_op jit(solution)/shard_map/ppermute | solution.py:287
  13.4 21.1 %collective-permute-start.2 = (bf16[1,576,256]{2,1,0:T(8,128)(2,1)}, bf16[1,576,256]{2,1,0:T(8,128)(2,1)S(1)}, u32[]{:S(2)}, u32[]{:S(2)}) collective-permute-start(bf16[1,576,256]{2,1,0:T(8,128)(2,1)} %param.8), channel_id=1, source_target_pairs={{0,128},{64,192},{128,0},{192,64},{1,129},{65,193},{129,1},{193,65... | collective-permute-start | bytes 884744 | tf_op jit(solution)/shard_map/ppermute | solution.py:287
  34.5 14.9 %copy-start.4 = (bf16[1,576,256]{2,1,0:T(8,128)(2,1)S(1)}, bf16[1,576,256]{2,1,0:T(8,128)(2,1)}, u32[]{:S(2)}) copy-start(bf16[1,576,256]{2,1,0:T(8,128)(2,1)} %param.8) | copy-start | bytes 884740
  34.5 16.1 %copy-start.2 = (bf16[64,18432]{1,0:T(8,128)(2,1)S(1)}, bf16[64,18432]{1,0:T(8,128)(2,1)}, u32[]{:S(2)}) copy-start(bf16[64,18432]{1,0:T(8,128)(2,1)} %refs_3_.1) | copy-start | bytes 7077892
  34.5 78.2 %all-to-all-start = ((bf16[16,32,4608]{2,1,0:T(8,128)(2,1)}), bf16[16,32,4608]{2,1,0:T(8,128)(2,1)}, u32[]{:S(2)}, u32[]{:S(2)}) async-start(bf16[16,32,4608]{2,1,0:T(8,128)(2,1)} %bitcast.18), calls=%async_computation | async-start | bytes 9437184 | tf_op jit(solution)/shard_map/all_to_all | solution.py:296
  49.1 5.5 %copy-start.5 = (s32[64]{0:T(128)S(1)}, s32[64]{0:T(128)}, u32[]{:S(2)}) copy-start(s32[64]{0:T(128)} %param.13) | copy-start | bytes 772
  49.1 55.8 %all-gather.2.cloned.1.call-start = ((), (), s32[]{:S(2)}) async-start(), calls=%async_computation.2 | async-start | bytes 5898240 | tf_op jit(solution)/shard_map/all_gather | solution.py:295
  61.6 5.9 %copy-start.3 = (bf16[32,512,128]{2,1,0:T(8,128)(2,1)S(1)}, bf16[32,512,128]{2,1,0:T(8,128)(2,1)}, u32[]{:S(2)}) copy-start(bf16[32,512,128]{2,1,0:T(8,128)(2,1)} %w_hbm.1) | copy-start | bytes 12582916
  112.7 46.8 %copy-start = (s32[64,1]{1,0:T(8,128)S(1)}, s32[64,1]{1,0:T(8,128)}, u32[]{:S(2)}) copy-start(s32[64,1]{1,0:T(8,128)} %copy.15.prompt_ref) | copy-start | bytes 772
  112.7 46.8 %copy-start.1 = (s32[1,64]{1,0:T(1,128)S(1)}, s32[1,64]{1,0:T(1,128)}, u32[]{:S(2)}) copy-start(s32[1,64]{1,0:T(1,128)} %fusion.22.base_ref) | copy-start | bytes 772
Sparse Core Ops, SparseCore 0:
  51.8 53.1 all-gather.1

commit v3 on v2

v3 whole, which is shorter than its diff:
```python
import functools

import jax
import jax.numpy as jnp
from jax import lax
from jax.experimental import pallas as pl
from jax.experimental.pallas import tpu as pltpu
from jax.sharding import Mesh
from jax.sharding import PartitionSpec as P

R = 512
P_SIZE = 64
V = 128
KEY = R + P_SIZE
MOST = 2
COPIES = 4
SPLIT = 4
HALVES = 2
CHUNKS = 2
LANES = 128
SCALE = 192.0 ** (-0.5)
LOG2E = 1.4426950408889634


def row_targets(prompt_col, base_row):
    forks = prompt_col.shape[0]
    prompts = base_row.shape[1]
    ids = lax.broadcasted_iota(jnp.int32, (forks, prompts), 1)
    base = jnp.sum(jnp.where(prompt_col == ids, base_row, 0), axis=1, keepdims=True)
    down = lax.broadcasted_iota(jnp.int32, (forks, forks), 0)
    along = lax.broadcasted_iota(jnp.int32, (forks, forks), 1)

    def turned(column):
        return jnp.sum(jnp.where(down == along, column, 0), axis=0, keepdims=True)

    before = (base == turned(base)) & (along < down)
    target = base + jnp.sum(before.astype(jnp.int32), axis=1, keepdims=True)
    return turned(target), target


def place_kernel(prompt_ref, base_ref, *refs):
    parts = refs[:SPLIT]
    out_ref, placing_ref = refs[SPLIT:]
    forks = parts[0].shape[0]

    @pl.when(pl.program_id(0) == 0)
    def _():
        target_row, _ = row_targets(prompt_ref[...], base_ref[...])
        at = lax.broadcasted_iota(jnp.int32, (out_ref.shape[0], forks), 0)
        for n in range(SPLIT):
            placing_ref[:, n * forks : (n + 1) * forks] = (at == target_row * SPLIT + n).astype(
                jnp.bfloat16
            )

    def paired(part):
        odd = part[:, KEY:]
        return jnp.concatenate([part[:, :R], odd[:, :R], part[:, R:KEY], odd[:, R:]], axis=1)

    stacked = jnp.concatenate([paired(part[...]) for part in parts], axis=0)
    out_ref[...] = jnp.dot(
        placing_ref[...], stacked, preferred_element_type=jnp.float32
    ).astype(jnp.bfloat16)


def place(prompt, base, queries, group, half):
    forks, width = queries.shape
    rows = group * COPIES * MOST * SPLIT
    part = width // SPLIT
    tile = 2 * KEY
    steps = part // tile
    mine = steps // HALVES

    def part_spec(n):
        return pl.BlockSpec((forks, tile), lambda i: (0, n * steps + half * mine + i))

    return pl.pallas_call(
        place_kernel,
        out_shape=jax.ShapeDtypeStruct((rows, part // HALVES), jnp.bfloat16),
        grid=(mine,),
        in_specs=[
            pl.BlockSpec(prompt.shape, lambda i: (0, 0)),
            pl.BlockSpec(base.shape, lambda i: (0, 0)),
            *[part_spec(n) for n in range(SPLIT)],
        ],
        out_specs=pl.BlockSpec((rows, tile), lambda i: (0, i)),
        scratch_shapes=[pltpu.VMEM((rows, SPLIT * forks), jnp.bfloat16)],
        name="place",
    )(prompt, base, *[queries] * SPLIT)


def prefix_kernel(
    half, q_ref, kv_ref, w_hbm, out_ref, w_ref, key_ref, lat_ref, part_ref, cell_ref, mass_ref, sem
):
    step = pl.program_id(0)
    last = pl.num_programs(0) - 1
    heads = w_ref.shape[0]
    group = q_ref.shape[0]
    held = COPIES * MOST
    quarter = kv_ref.shape[2]
    run = heads // SPLIT
    fetches = [
        pltpu.make_async_copy(
            w_hbm.at[pl.ds((n * HALVES + half) * run, run)],
            w_ref.at[pl.ds(n * run, run)],
            sem.at[n],
        )
        for n in range(SPLIT)
    ]

    @pl.when(step == 0)
    def _():
        for fetch in fetches:
            fetch.start()

    for n in range(kv_ref.shape[0]):
        cut = slice(n * quarter, (n + 1) * quarter)
        key_ref[0:KEY, cut] = kv_ref[n]
        key_ref[KEY : KEY + P_SIZE, cut] = kv_ref[n, R:KEY, :]

    tall = group * MOST * SPLIT
    span = group * MOST
    pairs = heads // SPLIT // 2
    lane = lax.broadcasted_iota(jnp.int32, (tall, LANES), 1)
    cells = jnp.zeros((tall, LANES), jnp.float32)
    rows = pl.ds(pl.multiple_of(step * span, span), span)

    def piece(start, size):
        return q_ref[:, :, start : start + size].reshape(tall, size)

    def query(pair, odd):
        start = pair * 2 * KEY
        ropes = piece(start + 2 * R, LANES)
        mine = (lane >= P_SIZE) if odd else (lane < P_SIZE)
        return jnp.concatenate(
            [piece(start + odd * R, R), jnp.where(mine, ropes, jnp.zeros_like(ropes))], axis=1
        )

    order = [(pair, odd) for odd in range(2) for pair in range(pairs)]
    chunks = CHUNKS
    per = len(order) // chunks

    def score(chunk):
        return jnp.dot(
            jnp.concatenate([query(*one) for one in order[chunk * per : (chunk + 1) * per]], axis=0),
            key_ref[...],
            preferred_element_type=jnp.float32,
        )

    ahead = [score(chunk) for chunk in range(1)]
    for chunk in range(chunks):
        scores = ahead.pop(0)
        if chunk + 1 < chunks:
            ahead.append(score(chunk + 1))
        peak = jnp.max(scores, axis=1, keepdims=True)
        weights = jnp.exp2((scores - peak) * (SCALE * LOG2E))
        total = jnp.sum(weights, axis=1, keepdims=True)
        summed = lax.dot_general(
            weights.astype(jnp.bfloat16),
            key_ref[0:R, :],
            (((1,), (1,)), ((), ())),
            preferred_element_type=jnp.float32,
        )
        latent = summed * (1.0 / total)
        for b in range(R // LANES):
            part_ref[b, chunk * per * tall : (chunk + 1) * per * tall, :] = latent[:, b * LANES : (b + 1) * LANES]
        mass = peak * SCALE + jnp.log(total)
        for at, (pair, odd) in enumerate(order[chunk * per : (chunk + 1) * per]):
            cells = jnp.where(lane == 2 * pair + odd, mass[at * tall : (at + 1) * tall], cells)
    for at, (pair, odd) in enumerate(order):
        for n in range(SPLIT):
            head = n * 2 * pairs + 2 * pair + odd
            for b in range(R // LANES):
                lat_ref[head, rows, b * LANES : (b + 1) * LANES] = part_ref[
                    b, pl.ds(at * tall + n, span, stride=SPLIT), :
                ].astype(jnp.bfloat16)
    cell_ref[...] = cells
    masses = jnp.zeros((span, LANES), jnp.float32)
    for n in range(SPLIT):
        block = cell_ref[pl.ds(n, span, stride=SPLIT), :]
        masses = masses + (pltpu.roll(block, n * 2 * pairs, 1) if n else block)
    mass_ref[rows, :] = masses

    @pl.when(step == last)
    def _():
        for fetch in fetches:
            fetch.wait()
        count = mass_ref.shape[0]
        to = lax.broadcasted_iota(jnp.int32, (count, count), 0)
        come = lax.broadcasted_iota(jnp.int32, (count, count), 1)
        source, slot = to // held, to % held
        turn = (come == (slot // MOST) * span + source * MOST + slot % MOST).astype(jnp.bfloat16)

        def put(at, block):
            out_ref[:, at : at + block.shape[1]] = jnp.dot(
                turn, block, preferred_element_type=jnp.float32
            ).astype(jnp.bfloat16)

        for head in range(0, heads, 2):
            both = [
                jnp.dot(lat_ref[h], w_ref[h], preferred_element_type=jnp.float32)
                for h in (head, head + 1)
            ]
            put(head * V, jnp.concatenate(both, axis=1).astype(jnp.bfloat16))
        high = mass_ref[...].astype(jnp.bfloat16)
        low = (mass_ref[...] - high.astype(jnp.float32)).astype(jnp.bfloat16)
        put(heads * V, jnp.concatenate([high, low], axis=1))


def prefix(received, caches, w_uv, half):
    group, _, part = received.shape
    heads = w_uv.shape[0] // HALVES
    rows = group * COPIES * MOST
    tall = group * MOST * SPLIT
    parts = caches.shape[0] // COPIES
    length = parts * caches.shape[2]
    caches = caches.reshape(parts, COPIES, *caches.shape[1:])
    wide = heads * V + 2 * LANES
    return pl.pallas_call(
        functools.partial(prefix_kernel, half),
        out_shape=jax.ShapeDtypeStruct((rows, wide), jnp.bfloat16),
        grid=(COPIES,),
        in_specs=[
            pl.BlockSpec((group, MOST * SPLIT, part), lambda i: (0, i, 0)),
            pl.BlockSpec((parts, None, *caches.shape[2:]), lambda i: (0, i, 0, 0)),
            pl.BlockSpec(memory_space=pl.ANY),
        ],
        out_specs=pl.BlockSpec((rows, wide), lambda i: (0, 0)),
        scratch_shapes=[
            pltpu.VMEM((heads, *w_uv.shape[1:]), jnp.bfloat16),
            pltpu.VMEM((KEY + P_SIZE, length), jnp.bfloat16),
            pltpu.VMEM((heads, rows, R), jnp.bfloat16),
            pltpu.VMEM((R // LANES, heads // SPLIT * tall, LANES), jnp.float32),
            pltpu.VMEM((tall, LANES), jnp.float32),
            pltpu.VMEM((rows, LANES), jnp.float32),
            pltpu.SemaphoreType.DMA((SPLIT,)),
        ],
        compiler_params=pltpu.CompilerParams(vmem_limit_bytes=56 << 20),
        cost_estimate=pl.CostEstimate(
            flops=2 * rows * heads * length * (KEY + R) + 2 * rows * heads * R * V,
            bytes_accessed=2 * (received.size + caches.size + w_uv.size // HALVES + rows * wide),
            transcendentals=rows * heads * length,
        ),
        name="prefix",
    )(received, caches, w_uv)


def merge_kernel(prompt_ref, base_ref, *refs):
    answers = refs[:HALVES]
    value_ref, mass_ref, out_ref = refs[HALVES:]
    _, target = row_targets(prompt_ref[...], base_ref[...])
    forks, heads = mass_ref.shape
    run = heads // SPLIT // HALVES
    at = lax.broadcasted_iota(jnp.int32, (forks, answers[0].shape[0]), 1)
    picking = (at == target).astype(jnp.bfloat16)

    def pick(ref, start, size):
        return jnp.dot(
            picking, ref[:, start : start + size], preferred_element_type=jnp.float32
        )

    for half, answer in enumerate(answers):
        come = pick(answer, heads // HALVES * V, 2 * LANES)
        mass = come[:, :LANES] + come[:, LANES:]
        for n in range(SPLIT):
            first = (n * HALVES + half) * run
            mass_prefix = mass[:, n * run : (n + 1) * run]
            mass_suffix = mass_ref[:, first : first + run]
            top = jnp.maximum(mass_prefix, mass_suffix)
            share_prefix = jnp.exp(mass_prefix - top)
            share_suffix = jnp.exp(mass_suffix - top)
            both = share_prefix + share_suffix
            part_prefix = share_prefix / both
            part_suffix = share_suffix / both
            value = pick(answer, n * run * V, run * V)
            for h in range(run):
                cut = slice((first + h) * V, (first + h + 1) * V)
                out_ref[:, cut] = (
                    part_prefix[:, h : h + 1] * value[:, h * V : (h + 1) * V]
                    + part_suffix[:, h : h + 1] * value_ref[:, cut].astype(jnp.float32)
                ).astype(out_ref.dtype)


def merge(prompt, base, answers, value_suffix, mass_suffix):
    forks = value_suffix.shape[0]
    return pl.pallas_call(
        merge_kernel,
        out_shape=jax.ShapeDtypeStruct((forks, value_suffix.shape[1]), jnp.bfloat16),
        compiler_params=pltpu.CompilerParams(vmem_limit_bytes=24 << 20),
        name="merge",
    )(prompt, base, *answers, value_suffix, mass_suffix)


def suffix(queries, suffix_cache, suffix_len, w_uv):
    forks = queries.shape[0]
    heads = w_uv.shape[0]
    query_heads = queries.reshape(forks, heads, KEY)
    scores = (
        jnp.einsum("fhe,fes->fhs", query_heads, suffix_cache, preferred_element_type=jnp.float32)
        * SCALE
    )
    positions = jnp.arange(suffix_cache.shape[2], dtype=jnp.int32)
    live = (positions[None, :] < suffix_len[:, None])[:, None, :]
    scores = jnp.where(live, scores, -jnp.inf)
    peak = jnp.max(scores, axis=2, keepdims=True)
    weights = jnp.where(live, jnp.exp(scores - peak), 0.0)
    total = jnp.sum(weights, axis=2)
    summed = jnp.einsum(
        "fhs,frs->fhr",
        weights.astype(jnp.bfloat16),
        suffix_cache[:, :R, :],
        preferred_element_type=jnp.float32,
    )
    latent = (summed / total[..., None]).astype(jnp.bfloat16)
    value = jnp.einsum("nhr,hrv->nhv", latent, w_uv, preferred_element_type=jnp.float32)
    return value.astype(jnp.bfloat16).reshape(forks, heads * V), peak[..., 0] + jnp.log(total)


def shards(queries, prefix_cache, suffix_cache, w_uv, fork_prompt, prompt_slot, suffix_len):
    near = ("zl", "xc")
    group = lax.axis_size("zl") * lax.axis_size("xc")
    held = COPIES * MOST
    back = (lax.axis_index("zh") - prompt_slot // group) % COPIES
    base = ((prompt_slot % group) * held + back * MOST)[None, :].astype(jnp.int32)

    def from_behind(steps):
        return lax.ppermute(
            prefix_cache, "zh", [(n, (n + steps) % COPIES) for n in range(COPIES)]
        )

    def exchange(value):
        return lax.all_to_all(
            value.reshape(group, -1, value.shape[1]), near, split_axis=0, concat_axis=0, tiled=True
        )

    moved = [from_behind(n) for n in range(1, COPIES)]
    outbound = [place(fork_prompt, base, queries, group, half) for half in range(HALVES)]
    outbound[0], *moved = lax.optimization_barrier((outbound[0], *moved))
    caches = lax.all_gather(
        jnp.concatenate([prefix_cache, *moved], axis=0), "tp", axis=0, tiled=True
    )
    value_suffix, mass_suffix = suffix(queries, suffix_cache, suffix_len, w_uv)
    received = [exchange(outbound[0])]
    outbound[1], value_suffix, mass_suffix = lax.optimization_barrier(
        (outbound[1], value_suffix, mass_suffix)
    )
    received.append(exchange(outbound[1]))
    results = [prefix(received[0], caches, w_uv, 0)]
    received[1], results[0] = lax.optimization_barrier((received[1], results[0]))
    results.append(prefix(received[1], caches, w_uv, 1))
    answers = [exchange(result) for result in results]
    answers = [answer.reshape(-1, answer.shape[2]) for answer in answers]
    return merge(fork_prompt, base, answers, value_suffix, mass_suffix)


def solution(mesh):
    owners = mesh.shape["dp"]
    tp = mesh.shape["tp"]
    group = owners // COPIES
    devices = mesh.devices.reshape(COPIES, 2, group // 2, tp)
    split = Mesh(devices, ("zh", "zl", "xc", "tp"))
    dp = ("zh", "zl", "xc")
    placed = (
        P(dp, "tp"),
        P(dp, None, "tp"),
        P(dp, None, None),
        P("tp", None, None),
        P(dp, None),
        P(),
        P(dp),
    )
    return jax.shard_map(
        shards, mesh=split, in_specs=placed, out_specs=P(dp, "tp"), check_vma=False
    )
```

time: 169 us -> 162 us (0.959)
  blocking collectives: 28.5 us -> 17 us
  waiting for transfers between devices: 50.7 us -> 44.2 us
  starting transfers between devices: 25 us -> 31.1 us
  Pallas kernels: 27.3 us -> 32.5 us
    all_gather x1, waiting for transfers between devices: 34.7 us -> 19.5 us  [shards(): lax.all_gather(jnp.concatenate([prefix_cache, *moved], axis=0), 'tp', axi...]
    all_to_all x1, blocking collectives: 28.5 us -> 17 us  [exchange(): lax.all_to_all(value.reshape(group, -1, value.shape[1]), near, split_axis...]
    ppermute x3, waiting for transfers between devices: 8.3 us -> 18.3 us  [from_behind(): lax.ppermute(prefix_cache, 'zh', [(n, (n + steps) % COPIES) for n in rang...]
    all_to_all x1 -> x3, starting transfers between devices: 14.7 us -> 19.8 us  [exchange(): lax.all_to_all(value.reshape(group, -1, value.shape[1]), near, split_axis...]
    pallas_call x2 -> x4, Pallas kernels: 25.4 us -> 29.7 us  [the longest x2 21.9 us: prefix(): pl.pallas_call(functools.partial(prefix_kernel, half), out_shape=jax.Shap...]
    all_to_all x1 -> x3, waiting for transfers between devices: 7.7 us -> 6.32 us  [exchange(): lax.all_to_all(value.reshape(group, -1, value.shape[1]), near, split_axis...]
  transfers between devices with their start and end apart: 5 -> 7, of which waited for: 4 -> 5; matrix products, arithmetic and copies ran while one was open for 14% -> 14% of each run, Pallas kernels for 4% -> 18%
where the time goes in v3:
time: 162 us
  waiting for transfers between devices  44.2 us (27%)
  Pallas kernels  32.5 us (20%)
  starting transfers between devices  31.1 us (19%)
  blocking collectives  17 us (10%)
  matrix products  14.6 us (9%)
  between operations  13.5 us (8%)
  local copies, waits for them, and re-layouts  5.6 us (3%)
  other arithmetic  3.19 us (2%)
    pallas_call x2, Pallas kernels, prefix(): pl.pallas_call(functools.partial(prefix_kernel, half), out_shape=jax.Shap...  21.9 us
    all_to_all x3, starting transfers between devices, exchange(): lax.all_to_all(value.reshape(group, -1, value.shape[1]), near, split_axis...  19.8 us
    all_gather x1, waiting for transfers between devices, shards(): lax.all_gather(jnp.concatenate([prefix_cache, *moved], axis=0), 'tp', axi...  19.5 us
    ppermute x3, waiting for transfers between devices, from_behind(): lax.ppermute(prefix_cache, 'zh', [(n, (n + steps) % COPIES) for n in rang...  18.3 us
    all_to_all x1, blocking collectives, exchange(): lax.all_to_all(value.reshape(group, -1, value.shape[1]), near, split_axis...  17 us
    ppermute x3, starting transfers between devices, from_behind(): lax.ppermute(prefix_cache, 'zh', [(n, (n + steps) % COPIES) for n in rang...  11.3 us
    pallas_call x2, Pallas kernels, place(): pl.pallas_call(place_kernel, out_shape=jax.ShapeDtypeStruct((rows, part /...  7.84 us
    all_to_all x3, waiting for transfers between devices, exchange(): lax.all_to_all(value.reshape(group, -1, value.shape[1]), near, split_axis...  6.32 us
  transfers between devices with their start and end apart: 7, of which 5 were waited for; matrix products, arithmetic and copies ran while one was open for 14% of the time, Pallas kernels for 18%

profile of v3, /device:TPU:1, one launch (start us, length us, event | category | flops | bytes accessed | tf_op | source)
XLA Modules:
  0.0 161.7 jit_solution(7502528059311989755)
XLA Ops:
  6.5 3.8 %collective-permute-start = (bf16[1,576,256]{2,1,0:T(8,128)(2,1)}, bf16[1,576,256]{2,1,0:T(8,128)(2,1)S(1)}, u32[]{:S(2)}, u32[]{:S(2)}) collective-permute-start(bf16[1,576,256]{2,1,0:T(8,128)(2,1)} %param.8), channel_id=1, source_target_pairs={{0,64},{64,128},{128,192},{192,0},{1,65},{65,129},{129,193},{193,1... | collective-permute-start | bytes 884744 | tf_op jit(solution)/shard_map/ppermute | solution.py:326
  10.4 5.1 %collective-permute-start.1 = (bf16[1,576,256]{2,1,0:T(8,128)(2,1)}, bf16[1,576,256]{2,1,0:T(8,128)(2,1)S(1)}, u32[]{:S(2)}, u32[]{:S(2)}) collective-permute-start(bf16[1,576,256]{2,1,0:T(8,128)(2,1)} %param.8), channel_id=1, source_target_pairs={{0,128},{64,192},{128,0},{192,64},{1,129},{65,193},{129,1},{193,65... | collective-permute-start | bytes 884744 | tf_op jit(solution)/shard_map/ppermute | solution.py:326
  15.5 2.4 %collective-permute-start.2 = (bf16[1,576,256]{2,1,0:T(8,128)(2,1)}, bf16[1,576,256]{2,1,0:T(8,128)(2,1)S(1)}, u32[]{:S(2)}, u32[]{:S(2)}) collective-permute-start(bf16[1,576,256]{2,1,0:T(8,128)(2,1)} %param.8), channel_id=1, source_target_pairs={{0,192},{64,0},{128,64},{192,128},{1,193},{65,1},{129,65},{193,129... | collective-permute-start | bytes 884744 | tf_op jit(solution)/shard_map/ppermute | solution.py:326
  17.9 1.4 copy.17.prompt_ref
  19.2 1.3 fusion.22.base_ref
  20.5 3.8 %place.3 = bf16[512,2304]{1,0:T(8,128)(2,1)} custom-call(s32[64,1]{1,0:T(8,128)} %copy.17.prompt_ref, s32[1,64]{1,0:T(1,128)} %fusion.22.base_ref, bf16[64,18432]{1,0:T(8,128)(2,1)} %refs_3_.3, bf16[64,18432]{1,0:T(8,128)(2,1)} %refs_3_.3, bf16[64,18432]{1,0:T(8,128)(2,1)} %refs_3_.3, bf16[64,18432]{1,0:T(8,128)(2,1)} %refs_3_.3), custom_call_target="tpu_custom_call" | custom-call | tf_op jit(solution)/shard_map/place/pallas_call | solution.py:76
  24.3 0.0 copy-start.4
  24.3 0.0 collective-permute-done
  24.3 8.5 %collective-permute-done.1 = bf16[1,576,256]{2,1,0:T(8,128)(2,1)S(1)} collective-permute-done((bf16[1,576,256]{2,1,0:T(8,128)(2,1)}, bf16[1,576,256]{2,1,0:T(8,128)(2,1)S(1)}, u32[]{:S(2)}, u32[]{:S(2)}) %collective-permute-start.1) | collective-permute-done | bytes 294944 | tf_op jit(solution)/shard_map/ppermute | solution.py:326
  32.8 9.8 %collective-permute-done.2 = bf16[1,576,256]{2,1,0:T(8,128)(2,1)S(1)} collective-permute-done((bf16[1,576,256]{2,1,0:T(8,128)(2,1)}, bf16[1,576,256]{2,1,0:T(8,128)(2,1)S(1)}, u32[]{:S(2)}, u32[]{:S(2)}) %collective-permute-start.2) | collective-permute-done | bytes 294944 | tf_op jit(solution)/shard_map/ppermute | solution.py:326
  42.6 4.8 %all-to-all-start.1 = ((bf16[16,32,2304]{2,1,0:T(8,128)(2,1)}), bf16[16,32,2304]{2,1,0:T(8,128)(2,1)}, u32[]{:S(2)}, u32[]{:S(2)}) async-start(bf16[16,32,2304]{2,1,0:T(8,128)(2,1)} %bitcast.21), calls=%async_computation.1 | async-start | bytes 4718592 | tf_op jit(solution)/shard_map/all_to_all | solution.py:331
  47.4 0.0 all-gather.2.cloned.1.call-start
  47.5 0.0 copy-done.4
  47.5 1.2 pad_maximum_fusion
  48.7 0.0 all-gather.2.cloned.1.call-update
  48.7 0.0 copy-start.2
  48.7 4.0 %place.2 = bf16[512,2304]{1,0:T(8,128)(2,1)} custom-call(s32[64,1]{1,0:T(8,128)} %copy.17.prompt_ref, s32[1,64]{1,0:T(1,128)} %fusion.22.base_ref, bf16[64,18432]{1,0:T(8,128)(2,1)} %refs_3_.3, bf16[64,18432]{1,0:T(8,128)(2,1)} %refs_3_.3, bf16[64,18432]{1,0:T(8,128)(2,1)} %refs_3_.3, bf16[64,18432]{1,0:T(8,128)(2,1)} %refs_3_.3), custom_call_target="tpu_custom_call" | custom-call | tf_op jit(solution)/shard_map/place/pallas_call | solution.py:76
  52.7 0.0 copy-done.2
  52.7 0.0 copy-start.5
  52.7 4.0 %reshape.47 = bf16[64,32,576]{2,1,0:T(8,128)(2,1)} reshape(bf16[64,18432]{1,0:T(8,128)(2,1)S(1)} %copy-done.2) | data formatting | bytes 4718592 | tf_op jit(solution)/shard_map/reshape | solution.py:296
  56.8 0.0 copy-done.5
  56.8 0.1 iota_compare_fusion
  56.8 6.2 %fusion.24 = (f32[64,32]{1,0:T(8,128)S(1)}, f32[64,32,128]{2,1,0:T(8,128)S(1)}) fusion(bf16[64,32,576]{2,1,0:T(8,128)(2,1)} %reshape.47, bf16[64,576,128]{2,1,0:T(8,128)(2,1)} %param.9, pred[64,128]{1,0:T(8,128)(4,1)S(1)} %iota_compare_fusion), kind=kOutput, calls=%fused_computation.33 | convolution fusion | flops 302774272 | bytes 12861440 | tf_op jit(solution)/shard_map/fhe,fes->fhs/dot_general | solution.py:298
  63.0 0.6 fusion.12
  63.7 0.1 copy.14
  63.7 0.0 copy-start.6
  63.7 5.9 %fusion = f32[64,32,512]{2,1,0:T(8,128)S(1)} fusion(bf16[64,576,128]{2,1,0:T(8,128)(2,1)} %param.9, f32[64,32,128]{2,1,0:T(8,128)S(1)} %get-tuple-element.24, f32[64,32]{1,0:T(8,128)S(1)} %get-tuple-element.23, pred[64,128]{1,0:T(8,128)(4,1)S(1)} %iota_compare_fusion), kind=kOutput, calls=%fused_computation | convolution fusion | flops 269221888 | bytes 13647872 | tf_op jit(solution)/shard_map/fhs,frs->fhr/dot_general | solution.py:307
  69.6 0.0 copy-done.6
  69.6 2.6 %fusion.9 = bf16[32,8,8,128]{3,2,1,0:T(8,128)(2,1)S(1)} fusion(bf16[32,512,128]{2,1,0:T(8,128)(2,1)S(1)} %copy-done.6, f32[64,32,512]{2,1,0:T(8,128)S(1)} %fusion, f32[64,32]{0,1:T(8,128)S(1)} %copy.14), kind=kOutput, calls=%fused_computation.8 | convolution fusion | flops 270794752 | bytes 8921088 | tf_op jit(solution)/shard_map/nhr,hrv->nhv/dot_general | solution.py:314
  72.2 0.1 copy.29
  72.3 6.0 %all-to-all-done.1.q_ref = bf16[16,32,2304]{2,1,0:T(8,128)(2,1)} async-done(((bf16[16,32,2304]{2,1,0:T(8,128)(2,1)}), bf16[16,32,2304]{2,1,0:T(8,128)(2,1)}, u32[]{:S(2)}, u32[]{:S(2)}) %all-to-all-start.1) | async-done | bytes 2359328 | tf_op jit(solution)/shard_map/all_to_all | solution.py:331
  78.3 7.5 %all-to-all-start = ((bf16[16,32,2304]{2,1,0:T(8,128)(2,1)}), bf16[16,32,2304]{2,1,0:T(8,128)(2,1)S(1)}, u32[]{:S(2)}, u32[]{:S(2)}) async-start(bf16[16,32,2304]{2,1,0:T(8,128)(2,1)} %bitcast.2), calls=%async_computation | async-start | bytes 4718592 | tf_op jit(solution)/shard_map/all_to_all | solution.py:331
  85.8 19.5 %all-gather.2.cloned.1.call-done = bf16[16,576,256]{2,1,0:T(8,128)(2,1)} async-done(((bf16[4,576,256]{2,1,0:T(8,128)(2,1)}), bf16[16,576,256]{2,1,0:T(8,128)(2,1)}) %all-gather.2.cloned.1.call-update) | async-done | bytes 4718608 | tf_op jit(solution)/shard_map/all_gather | solution.py:338
  105.3 10.9 %prefix.2 = bf16[128,2304]{1,0:T(8,128)(2,1)} custom-call(bf16[16,32,2304]{2,1,0:T(8,128)(2,1)} %all-to-all-done.1.q_ref, bf16[4,4,576,256]{3,2,1,0:T(8,128)(2,1)} %bitcast.24, bf16[32,512,128]{2,1,0:T(8,128)(2,1)} %w_hbm.3), custom_call_target="tpu_custom_call" | custom-call | flops 4831838208 | bytes 9764864 | tf_op jit(solution)/shard_map/prefix/pallas_call | solution.py:218
  116.3 0.3 all-to-all-done.q_ref
  116.6 0.0 copy-start.3
  116.6 7.5 %all-to-all-start.2 = ((bf16[16,8,2304]{2,1,0:T(8,128)(2,1)}), bf16[16,8,2304]{2,1,0:T(8,128)(2,1)S(1)}, u32[]{:S(2)}, u32[]{:S(2)}) async-start(bf16[16,8,2304]{2,1,0:T(8,128)(2,1)} %bitcast.22), calls=%async_computation.2 | async-start | bytes 1179648 | tf_op jit(solution)/shard_map/all_to_all | solution.py:331
  124.1 0.0 copy-done.3
  124.1 0.0 copy-start
  124.1 0.0 copy-start.1
  124.1 11.0 %prefix.3 = bf16[128,2304]{1,0:T(8,128)(2,1)} custom-call(bf16[16,32,2304]{2,1,0:T(8,128)(2,1)} %copy-done.3, bf16[4,4,576,256]{3,2,1,0:T(8,128)(2,1)} %bitcast.25, bf16[32,512,128]{2,1,0:T(8,128)(2,1)} %w_hbm.3), custom_call_target="tpu_custom_call" | custom-call | flops 4831838208 | bytes 9764864 | tf_op jit(solution)/shard_map/prefix/pallas_call | solution.py:218
  135.1 0.0 all-to-all-done.2
  135.1 17.0 %all_to_all.20 = bf16[16,8,2304]{2,1,0:T(8,128)(2,1)S(1)} all-to-all(bf16[16,8,2304]{2,1,0:T(8,128)(2,1)} %bitcast.23), channel_id=1, replica_groups=mesh['zh'=4,'zl'=2,'xc'=8,'tp'=4] {'zl','xc'}, dimensions={0} | all-to-all | bytes 1179648 | tf_op jit(solution)/shard_map/all_to_all | solution.py:331
  152.1 0.0 copy-done
  152.1 0.0 copy-done.1
  152.1 2.8 %merge.1 = bf16[64,4096]{1,0:T(8,128)(2,1)} custom-call(s32[64,1]{1,0:T(8,128)S(1)} %copy-done, s32[1,64]{1,0:T(1,128)S(1)} %copy-done.1, bf16[128,2304]{1,0:T(8,128)(2,1)S(1)} %bitcast.18, bf16[128,2304]{1,0:T(8,128)(2,1)S(1)} %bitcast.19, bf16[64,4096]{1,0:T(8,128)(2,1)S(1)} %bitcast.20, f32[64,32]{1,0:T(8,128)S(1)} %log_add_fusion.refs_3_), custom_call_target="tpu_custom_call" | custom-call | tf_op jit(solution)/shard_map/merge/pallas_call | solution.py:285
  (1 shorter events, 0.0 us)
Async XLA Ops:
  6.5 17.8 %collective-permute-start = (bf16[1,576,256]{2,1,0:T(8,128)(2,1)}, bf16[1,576,256]{2,1,0:T(8,128)(2,1)S(1)}, u32[]{:S(2)}, u32[]{:S(2)}) collective-permute-start(bf16[1,576,256]{2,1,0:T(8,128)(2,1)} %param.8), channel_id=1, source_target_pairs={{0,64},{64,128},{128,192},{192,0},{1,65},{65,129},{129,193},{193,1... | collective-permute-start | bytes 884744 | tf_op jit(solution)/shard_map/ppermute | solution.py:326
  10.4 22.5 %collective-permute-start.1 = (bf16[1,576,256]{2,1,0:T(8,128)(2,1)}, bf16[1,576,256]{2,1,0:T(8,128)(2,1)S(1)}, u32[]{:S(2)}, u32[]{:S(2)}) collective-permute-start(bf16[1,576,256]{2,1,0:T(8,128)(2,1)} %param.8), channel_id=1, source_target_pairs={{0,128},{64,192},{128,0},{192,64},{1,129},{65,193},{129,1},{193,65... | collective-permute-start | bytes 884744 | tf_op jit(solution)/shard_map/ppermute | solution.py:326
  15.5 27.1 %collective-permute-start.2 = (bf16[1,576,256]{2,1,0:T(8,128)(2,1)}, bf16[1,576,256]{2,1,0:T(8,128)(2,1)S(1)}, u32[]{:S(2)}, u32[]{:S(2)}) collective-permute-start(bf16[1,576,256]{2,1,0:T(8,128)(2,1)} %param.8), channel_id=1, source_target_pairs={{0,192},{64,0},{128,64},{192,128},{1,193},{65,1},{129,65},{193,129... | collective-permute-start | bytes 884744 | tf_op jit(solution)/shard_map/ppermute | solution.py:326
  24.3 23.2 %copy-start.4 = (bf16[1,576,256]{2,1,0:T(8,128)(2,1)S(1)}, bf16[1,576,256]{2,1,0:T(8,128)(2,1)}, u32[]{:S(2)}) copy-start(bf16[1,576,256]{2,1,0:T(8,128)(2,1)} %param.8) | copy-start | bytes 884740
  42.6 35.7 %all-to-all-start.1 = ((bf16[16,32,2304]{2,1,0:T(8,128)(2,1)}), bf16[16,32,2304]{2,1,0:T(8,128)(2,1)}, u32[]{:S(2)}, u32[]{:S(2)}) async-start(bf16[16,32,2304]{2,1,0:T(8,128)(2,1)} %bitcast.21), calls=%async_computation.1 | async-start | bytes 4718592 | tf_op jit(solution)/shard_map/all_to_all | solution.py:331
  47.4 57.9 %all-gather.2.cloned.1.call-start = ((), (), s32[]{:S(2)}) async-start(), calls=%async_computation.4 | async-start | bytes 5898240 | tf_op jit(solution)/shard_map/all_gather | solution.py:338
  48.7 4.0 %copy-start.2 = (bf16[64,18432]{1,0:T(8,128)(2,1)S(1)}, bf16[64,18432]{1,0:T(8,128)(2,1)}, u32[]{:S(2)}) copy-start(bf16[64,18432]{1,0:T(8,128)(2,1)} %refs_3_.3) | copy-start | bytes 7077892
  52.7 4.1 %copy-start.5 = (s32[64]{0:T(128)S(1)}, s32[64]{0:T(128)}, u32[]{:S(2)}) copy-start(s32[64]{0:T(128)} %param.13) | copy-start | bytes 772
  63.7 5.9 %copy-start.6 = (bf16[32,512,128]{2,1,0:T(8,128)(2,1)S(1)}, bf16[32,512,128]{2,1,0:T(8,128)(2,1)}, u32[]{:S(2)}) copy-start(bf16[32,512,128]{2,1,0:T(8,128)(2,1)} %w_hbm.3) | copy-start | bytes 12582916
  78.3 38.3 %all-to-all-start = ((bf16[16,32,2304]{2,1,0:T(8,128)(2,1)}), bf16[16,32,2304]{2,1,0:T(8,128)(2,1)S(1)}, u32[]{:S(2)}, u32[]{:S(2)}) async-start(bf16[16,32,2304]{2,1,0:T(8,128)(2,1)} %bitcast.2), calls=%async_computation | async-start | bytes 4718592 | tf_op jit(solution)/shard_map/all_to_all | solution.py:331
  116.6 7.5 %copy-start.3 = (bf16[16,32,2304]{2,1,0:T(8,128)(2,1)}, bf16[16,32,2304]{2,1,0:T(8,128)(2,1)S(1)}, u32[]{:S(2)}) copy-start(bf16[16,32,2304]{2,1,0:T(8,128)(2,1)S(1)} %all-to-all-done.q_ref) | copy-start | bytes 7077892
  116.6 18.5 %all-to-all-start.2 = ((bf16[16,8,2304]{2,1,0:T(8,128)(2,1)}), bf16[16,8,2304]{2,1,0:T(8,128)(2,1)S(1)}, u32[]{:S(2)}, u32[]{:S(2)}) async-start(bf16[16,8,2304]{2,1,0:T(8,128)(2,1)} %bitcast.22), calls=%async_computation.2 | async-start | bytes 1179648 | tf_op jit(solution)/shard_map/all_to_all | solution.py:331
  124.1 28.0 %copy-start = (s32[64,1]{1,0:T(8,128)S(1)}, s32[64,1]{1,0:T(8,128)}, u32[]{:S(2)}) copy-start(s32[64,1]{1,0:T(8,128)} %copy.17.prompt_ref) | copy-start | bytes 772
  124.1 28.0 %copy-start.1 = (s32[1,64]{1,0:T(1,128)S(1)}, s32[1,64]{1,0:T(1,128)}, u32[]{:S(2)}) copy-start(s32[1,64]{1,0:T(1,128)} %fusion.22.base_ref) | copy-start | bytes 772
Sparse Core Ops, SparseCore 0:
  50.0 55.2 all-gather.1

commit v4 on v3

--- a/solution.py
+++ b/solution.py
@@ -15,7 +15,7 @@
 MOST = 2
 COPIES = 4
 SPLIT = 4
-HALVES = 2
+PARTS = ((0, 3), (3, 1))
 CHUNKS = 2
 LANES = 128
 SCALE = 192.0 ** (-0.5)
@@ -40,12 +40,12 @@
 
 def place_kernel(prompt_ref, base_ref, *refs):
     parts = refs[:SPLIT]
-    out_ref, placing_ref = refs[SPLIT:]
+    out_ref, target_ref, placing_ref = refs[SPLIT:]
     forks = parts[0].shape[0]
 
     @pl.when(pl.program_id(0) == 0)
     def _():
-        target_row, _ = row_targets(prompt_ref[...], base_ref[...])
+        target_row, target_ref[...] = row_targets(prompt_ref[...], base_ref[...])
         at = lax.broadcasted_iota(jnp.int32, (out_ref.shape[0], forks), 0)
         for n in range(SPLIT):
             placing_ref[:, n * forks : (n + 1) * forks] = (at == target_row * SPLIT + n).astype(
@@ -62,35 +62,40 @@
     ).astype(jnp.bfloat16)
 
 
-def place(prompt, base, queries, group, half):
+def place(prompt, base, queries, group, part):
     forks, width = queries.shape
     rows = group * COPIES * MOST * SPLIT
-    part = width // SPLIT
     tile = 2 * KEY
-    steps = part // tile
-    mine = steps // HALVES
+    steps = width // SPLIT // tile
+    first, mine = part
 
     def part_spec(n):
-        return pl.BlockSpec((forks, tile), lambda i: (0, n * steps + half * mine + i))
+        return pl.BlockSpec((forks, tile), lambda i: (0, n * steps + first + i))
 
     return pl.pallas_call(
         place_kernel,
-        out_shape=jax.ShapeDtypeStruct((rows, part // HALVES), jnp.bfloat16),
+        out_shape=(
+            jax.ShapeDtypeStruct((rows, mine * tile), jnp.bfloat16),
+            jax.ShapeDtypeStruct((forks, 1), jnp.int32),
+        ),
         grid=(mine,),
         in_specs=[
             pl.BlockSpec(prompt.shape, lambda i: (0, 0)),
             pl.BlockSpec(base.shape, lambda i: (0, 0)),
             *[part_spec(n) for n in range(SPLIT)],
         ],
-        out_specs=pl.BlockSpec((rows, tile), lambda i: (0, i)),
+        out_specs=(
+            pl.BlockSpec((rows, tile), lambda i: (0, i)),
+            pl.BlockSpec((forks, 1), lambda i: (0, 0)),
+        ),
         scratch_shapes=[pltpu.VMEM((rows, SPLIT * forks), jnp.bfloat16)],
         name="place",
     )(prompt, base, *[queries] * SPLIT)
 
 
-def prefix_kernel(
-    half, q_ref, kv_ref, w_hbm, out_ref, w_ref, key_ref, lat_ref, part_ref, cell_ref, mass_ref, sem
-):
+def prefix_kernel(part, q_ref, own_ref, kv_ref, w_hbm, *refs):
+    *earlier, out_ref, w_ref, key_ref, lat_ref, part_ref, cell_ref, mass_ref, sem = refs
+    ahead_of_it = earlier[0].shape[1] if earlier else 0
     step = pl.program_id(0)
     last = pl.num_programs(0) - 1
     heads = w_ref.shape[0]
@@ -98,9 +103,10 @@
     held = COPIES * MOST
     quarter = kv_ref.shape[2]
     run = heads // SPLIT
+    group_heads = w_hbm.shape[0] // SPLIT
     fetches = [
         pltpu.make_async_copy(
-            w_hbm.at[pl.ds((n * HALVES + half) * run, run)],
+            w_hbm.at[pl.ds(n * group_heads + 2 * part[0], run)],
             w_ref.at[pl.ds(n * run, run)],
             sem.at[n],
         )
@@ -111,11 +117,22 @@
     def _():
         for fetch in fetches:
             fetch.start()
-
-    for n in range(kv_ref.shape[0]):
-        cut = slice(n * quarter, (n + 1) * quarter)
-        key_ref[0:KEY, cut] = kv_ref[n]
-        key_ref[KEY : KEY + P_SIZE, cut] = kv_ref[n, R:KEY, :]
+        if earlier:
+            out_ref[:, :ahead_of_it] = earlier[0][...]
+
+    def keep(ref):
+        for n in range(ref.shape[0]):
+            cut = slice(n * quarter, (n + 1) * quarter)
+            key_ref[0:KEY, cut] = ref[n]
+            key_ref[KEY : KEY + P_SIZE, cut] = ref[n, R:KEY, :]
+
+    @pl.when(step == 0)
+    def _():
+        keep(own_ref)
+
+    @pl.when(step > 0)
+    def _():
+        keep(kv_ref)
 
     tall = group * MOST * SPLIT
     span = group * MOST
@@ -136,7 +153,7 @@
         )
 
     order = [(pair, odd) for odd in range(2) for pair in range(pairs)]
-    chunks = CHUNKS
+    chunks = CHUNKS if len(order) > CHUNKS else 1
     per = len(order) // chunks
 
     def score(chunk):
@@ -191,7 +208,8 @@
         turn = (come == (slot // MOST) * span + source * MOST + slot % MOST).astype(jnp.bfloat16)
 
         def put(at, block):
-            out_ref[:, at : at + block.shape[1]] = jnp.dot(
+            begin = ahead_of_it + at
+            out_ref[:, begin : begin + block.shape[1]] = jnp.dot(
                 turn, block, preferred_element_type=jnp.float32
             ).astype(jnp.bfloat16)
 
@@ -206,23 +224,29 @@
         put(heads * V, jnp.concatenate([high, low], axis=1))
 
 
-def prefix(received, caches, w_uv, half):
-    group, _, part = received.shape
-    heads = w_uv.shape[0] // HALVES
+def prefix(received, own, caches, w_uv, part, *earlier):
+    group, _, width = received.shape
+    heads = 2 * part[1] * SPLIT
     rows = group * COPIES * MOST
     tall = group * MOST * SPLIT
-    parts = caches.shape[0] // COPIES
-    length = parts * caches.shape[2]
-    caches = caches.reshape(parts, COPIES, *caches.shape[1:])
-    wide = heads * V + 2 * LANES
+    parts = own.shape[0]
+    length = parts * own.shape[2]
+    wide = heads * V + 2 * LANES + sum(one.shape[1] for one in earlier)
     return pl.pallas_call(
-        functools.partial(prefix_kernel, half),
+        functools.partial(prefix_kernel, part),
         out_shape=jax.ShapeDtypeStruct((rows, wide), jnp.bfloat16),
         grid=(COPIES,),
         in_specs=[
-            pl.BlockSpec((group, MOST * SPLIT, part), lambda i: (0, i, 0)),
-            pl.BlockSpec((parts, None, *caches.shape[2:]), lambda i: (0, i, 0, 0)),
+            pl.BlockSpec((group, MOST * SPLIT, width), lambda i: (0, i, 0)),
+            pl.BlockSpec(own.shape, lambda i: (0, 0, 0), pipeline_mode=pl.Buffered(1)),
+            pl.BlockSpec(
+                (parts, None, *caches.shape[2:]), lambda i: (0, jnp.maximum(i - 1, 0), 0, 0)
+            ),
             pl.BlockSpec(memory_space=pl.ANY),
+            *[
+                pl.BlockSpec(one.shape, lambda i: (0, 0), pipeline_mode=pl.Buffered(1))
+                for one in earlier
+            ],
         ],
         out_specs=pl.BlockSpec((rows, wide), lambda i: (0, 0)),
         scratch_shapes=[
@@ -237,32 +261,32 @@
         compiler_params=pltpu.CompilerParams(vmem_limit_bytes=56 << 20),
         cost_estimate=pl.CostEstimate(
             flops=2 * rows * heads * length * (KEY + R) + 2 * rows * heads * R * V,
-            bytes_accessed=2 * (received.size + caches.size + w_uv.size // HALVES + rows * wide),
+            bytes_accessed=2 * (received.size + own.size + caches.size + heads * R * V + rows * wide),
             transcendentals=rows * heads * length,
         ),
         name="prefix",
-    )(received, caches, w_uv)
-
-
-def merge_kernel(prompt_ref, base_ref, *refs):
-    answers = refs[:HALVES]
-    value_ref, mass_ref, out_ref = refs[HALVES:]
-    _, target = row_targets(prompt_ref[...], base_ref[...])
+    )(received, own, caches, w_uv, *earlier)
+
+
+def merge_kernel(target_ref, answer_ref, value_ref, mass_ref, out_ref):
     forks, heads = mass_ref.shape
-    run = heads // SPLIT // HALVES
-    at = lax.broadcasted_iota(jnp.int32, (forks, answers[0].shape[0]), 1)
-    picking = (at == target).astype(jnp.bfloat16)
-
-    def pick(ref, start, size):
+    group_heads = heads // SPLIT
+    at = lax.broadcasted_iota(jnp.int32, (forks, answer_ref.shape[0]), 1)
+    picking = (at == target_ref[...]).astype(jnp.bfloat16)
+
+    def pick(start, size):
         return jnp.dot(
-            picking, ref[:, start : start + size], preferred_element_type=jnp.float32
-        )
-
-    for half, answer in enumerate(answers):
-        come = pick(answer, heads // HALVES * V, 2 * LANES)
+            picking, answer_ref[:, start : start + size], preferred_element_type=jnp.float32
+        )
+
+    begin = 0
+
+    for lead, count in PARTS:
+        run = 2 * count
+        come = pick(begin + run * SPLIT * V, 2 * LANES)
         mass = come[:, :LANES] + come[:, LANES:]
         for n in range(SPLIT):
-            first = (n * HALVES + half) * run
+            first = n * group_heads + 2 * lead
             mass_prefix = mass[:, n * run : (n + 1) * run]
             mass_suffix = mass_ref[:, first : first + run]
             top = jnp.maximum(mass_prefix, mass_suffix)
@@ -271,23 +295,24 @@
             both = share_prefix + share_suffix
             part_prefix = share_prefix / both
             part_suffix = share_suffix / both
-            value = pick(answer, n * run * V, run * V)
+            value = pick(begin + n * run * V, run * V)
             for h in range(run):
                 cut = slice((first + h) * V, (first + h + 1) * V)
                 out_ref[:, cut] = (
                     part_prefix[:, h : h + 1] * value[:, h * V : (h + 1) * V]
                     + part_suffix[:, h : h + 1] * value_ref[:, cut].astype(jnp.float32)
                 ).astype(out_ref.dtype)
-
-
-def merge(prompt, base, answers, value_suffix, mass_suffix):
+        begin += run * SPLIT * V + 2 * LANES
+
+
+def merge(target, answer, value_suffix, mass_suffix):
     forks = value_suffix.shape[0]
     return pl.pallas_call(
         merge_kernel,
         out_shape=jax.ShapeDtypeStruct((forks, value_suffix.shape[1]), jnp.bfloat16),
         compiler_params=pltpu.CompilerParams(vmem_limit_bytes=24 << 20),
         name="merge",
-    )(prompt, base, *answers, value_suffix, mass_suffix)
+    )(target, answer, value_suffix, mass_suffix)
 
 
 def suffix(queries, suffix_cache, suffix_len, w_uv):
@@ -332,24 +357,22 @@
             value.reshape(group, -1, value.shape[1]), near, split_axis=0, concat_axis=0, tiled=True
         )
 
+    own = lax.all_gather(prefix_cache, "tp", axis=0, tiled=True)
     moved = [from_behind(n) for n in range(1, COPIES)]
-    outbound = [place(fork_prompt, base, queries, group, half) for half in range(HALVES)]
-    outbound[0], *moved = lax.optimization_barrier((outbound[0], *moved))
-    caches = lax.all_gather(
-        jnp.concatenate([prefix_cache, *moved], axis=0), "tp", axis=0, tiled=True
-    )
+    outbound, targets = zip(*[place(fork_prompt, base, queries, group, part) for part in PARTS])
+    outbound = list(outbound)
+    outbound[0], own, *moved = lax.optimization_barrier((outbound[0], own, *moved))
+    caches = lax.all_gather(jnp.stack(moved, axis=1), "tp", axis=0, tiled=True)
     value_suffix, mass_suffix = suffix(queries, suffix_cache, suffix_len, w_uv)
     received = [exchange(outbound[0])]
     outbound[1], value_suffix, mass_suffix = lax.optimization_barrier(
         (outbound[1], value_suffix, mass_suffix)
     )
     received.append(exchange(outbound[1]))
-    results = [prefix(received[0], caches, w_uv, 0)]
-    received[1], results[0] = lax.optimization_barrier((received[1], results[0]))
-    results.append(prefix(received[1], caches, w_uv, 1))
-    answers = [exchange(result) for result in results]
-    answers = [answer.reshape(-1, answer.shape[2]) for answer in answers]
-    return merge(fork_prompt, base, answers, value_suffix, mass_suffix)
+    result = prefix(received[0], own, caches, w_uv, PARTS[0])
+    result = prefix(received[1], own, caches, w_uv, PARTS[1], result)
+    answer = exchange(result).reshape(result.shape)
+    return merge(targets[0], answer, value_suffix, mass_suffix)
 
 
 def solution(mesh):

time: 162 us -> 167 us (1.031)
  waiting for transfers between devices: 44.2 us -> 35.2 us
  Pallas kernels: 32.5 us -> 38.2 us
  blocking collectives: 17 us -> 22.5 us
  starting transfers between devices: 31.1 us -> 33.1 us
    all_gather x1 -> x2, waiting for transfers between devices: 19.5 us -> 2.89 us  [the longest x1 2.87 us: shards(): own = lax.all_gather(prefix_cache, 'tp', axis=0, tiled=True)]
    all_to_all x3 -> x2, waiting for transfers between devices: 6.32 us -> 22.4 us  [exchange(): lax.all_to_all(value.reshape(group, -1, value.shape[1]), near, split_axis...]
    ppermute x3, waiting for transfers between devices: 18.3 us -> 9.24 us  [from_behind(): lax.ppermute(prefix_cache, 'zh', [(n, (n + steps) % COPIES) for n in rang...]
    all_to_all x1, blocking collectives: 17 us -> 22.5 us  [exchange(): lax.all_to_all(value.reshape(group, -1, value.shape[1]), near, split_axis...]
    pallas_call x4, Pallas kernels: 29.7 us -> 35 us  [the longest x2 26.1 us: prefix(): pl.pallas_call(functools.partial(prefix_kernel, part), out_shape=jax.Shap...]
    all_to_all x3 -> x2, starting transfers between devices: 19.8 us -> 21.7 us  [exchange(): lax.all_to_all(value.reshape(group, -1, value.shape[1]), near, split_axis...]
  transfers between devices with their start and end apart: 7 -> 7, of which waited for: 5 -> 4; matrix products, arithmetic and copies ran while one was open for 14% -> 14% of each run, Pallas kernels for 18% -> 15%
where the time goes in v4:
time: 167 us
  Pallas kernels  38.2 us (23%)
  waiting for transfers between devices  35.2 us (21%)
  starting transfers between devices  33.1 us (20%)
  blocking collectives  22.5 us (13%)
  matrix products  14.8 us (9%)
  between operations  13.5 us (8%)
  local copies, waits for them, and re-layouts  6.68 us (4%)
  other arithmetic  3.05 us (2%)
    pallas_call x2, Pallas kernels, prefix(): pl.pallas_call(functools.partial(prefix_kernel, part), out_shape=jax.Shap...  26.1 us
    all_to_all x1, blocking collectives, exchange(): lax.all_to_all(value.reshape(group, -1, value.shape[1]), near, split_axis...  22.5 us
    all_to_all x2, waiting for transfers between devices, exchange(): lax.all_to_all(value.reshape(group, -1, value.shape[1]), near, split_axis...  22.4 us
    all_to_all x2, starting transfers between devices, exchange(): lax.all_to_all(value.reshape(group, -1, value.shape[1]), near, split_axis...  21.7 us
    ppermute x3, starting transfers between devices, from_behind(): lax.ppermute(prefix_cache, 'zh', [(n, (n + steps) % COPIES) for n in rang...  11.4 us
    ppermute x3, waiting for transfers between devices, from_behind(): lax.ppermute(prefix_cache, 'zh', [(n, (n + steps) % COPIES) for n in rang...  9.24 us
    pallas_call x2, Pallas kernels, place(): pl.pallas_call(place_kernel, out_shape=(jax.ShapeDtypeStruct((rows, mine...  8.93 us
    dot_general x1, matrix products, suffix(): jnp.einsum('fhe,fes->fhs', query_heads, suffix_cache, preferred_element_t...  6.68 us
  transfers between devices with their start and end apart: 7, of which 4 were waited for; matrix products, arithmetic and copies ran while one was open for 14% of the time, Pallas kernels for 15%

profile of v4, /device:TPU:1, one launch (start us, length us, event | category | flops | bytes accessed | tf_op | source)
XLA Modules:
  0.0 167.0 jit_solution(5378530563486569610)
XLA Ops:
  6.5 0.0 all-gather.3.cloned.1.call-start
  6.5 0.7 all-gather.3.cloned.1.call-update
  7.3 3.9 %collective-permute-start = (bf16[1,576,256]{2,1,0:T(8,128)(2,1)}, bf16[1,576,256]{2,1,0:T(8,128)(2,1)S(1)}, u32[]{:S(2)}, u32[]{:S(2)}) collective-permute-start(bf16[1,576,256]{2,1,0:T(8,128)(2,1)} %param.8), channel_id=1, source_target_pairs={{0,64},{64,128},{128,192},{192,0},{1,65},{65,129},{129,193},{193,1... | collective-permute-start | bytes 884744 | tf_op jit(solution)/shard_map/ppermute | solution.py:351
  11.2 3.1 %collective-permute-start.2 = (bf16[1,576,256]{2,1,0:T(8,128)(2,1)}, bf16[1,576,256]{2,1,0:T(8,128)(2,1)S(1)}, u32[]{:S(2)}, u32[]{:S(2)}) collective-permute-start(bf16[1,576,256]{2,1,0:T(8,128)(2,1)} %param.8), channel_id=1, source_target_pairs={{0,192},{64,0},{128,64},{192,128},{1,193},{65,1},{129,65},{193,129... | collective-permute-start | bytes 884744 | tf_op jit(solution)/shard_map/ppermute | solution.py:351
  14.3 4.4 %collective-permute-start.1 = (bf16[1,576,256]{2,1,0:T(8,128)(2,1)}, bf16[1,576,256]{2,1,0:T(8,128)(2,1)S(1)}, u32[]{:S(2)}, u32[]{:S(2)}) collective-permute-start(bf16[1,576,256]{2,1,0:T(8,128)(2,1)} %param.8), channel_id=1, source_target_pairs={{0,128},{64,192},{128,0},{192,64},{1,129},{65,193},{129,1},{193,65... | collective-permute-start | bytes 884744 | tf_op jit(solution)/shard_map/ppermute | solution.py:351
  18.6 1.4 copy.12.prompt_ref
  20.0 1.3 fusion.22.base_ref
  21.3 5.6 %place.2 = (bf16[512,3456]{1,0:T(8,128)(2,1)}, s32[64,1]{1,0:T(8,128)}) custom-call(s32[64,1]{1,0:T(8,128)} %copy.12.prompt_ref, s32[1,64]{1,0:T(1,128)} %fusion.22.base_ref, bf16[64,18432]{1,0:T(8,128)(2,1)} %refs_3_.3, bf16[64,18432]{1,0:T(8,128)(2,1)} %refs_3_.3, bf16[64,18432]{1,0:T(8,128)(2,1)} %refs_3_.3, bf16[64,18432]{1,0:T(8,128)(2,1)} %refs_3_.3), custom_call_target="tpu_custom_call" | custom-call | tf_op jit(solution)/shard_map/place/pallas_call | solution.py:75
  26.9 0.0 collective-permute-done
  26.9 9.2 %collective-permute-done.2 = bf16[1,576,256]{2,1,0:T(8,128)(2,1)S(1)} collective-permute-done((bf16[1,576,256]{2,1,0:T(8,128)(2,1)}, bf16[1,576,256]{2,1,0:T(8,128)(2,1)S(1)}, u32[]{:S(2)}, u32[]{:S(2)}) %collective-permute-start.2) | collective-permute-done | bytes 294944 | tf_op jit(solution)/shard_map/ppermute | solution.py:351
  36.1 0.0 collective-permute-done.1
  36.1 2.9 %all-gather.3.cloned.1.call-done.own_ref = bf16[4,576,256]{2,1,0:T(8,128)(2,1)} async-done(((bf16[1,576,256]{2,1,0:T(8,128)(2,1)}), bf16[4,576,256]{2,1,0:T(8,128)(2,1)}) %all-gather.3.cloned.1.call-update) | async-done | bytes 1179664 | tf_op jit(solution)/shard_map/all_gather | solution.py:360
  39.0 11.0 %all-to-all-start.1 = ((bf16[16,32,3456]{2,1,0:T(8,128)(2,1)}), bf16[16,32,3456]{2,1,0:T(8,128)(2,1)}, u32[]{:S(2)}, u32[]{:S(2)}) async-start(bf16[16,32,3456]{2,1,0:T(8,128)(2,1)} %bitcast.21), calls=%async_computation.1 | async-start | bytes 7077888 | tf_op jit(solution)/shard_map/all_to_all | solution.py:356
  50.0 0.0 all-gather.5.cloned.1.call-start
  50.0 1.1 pad_maximum_fusion
  51.1 0.0 all-gather.5.cloned.1.call-update
  51.1 0.0 copy-start.1
  51.1 3.3 %place.3 = (bf16[512,1152]{1,0:T(8,128)(2,1)}, s32[64,1]{1,0:T(8,128)}) custom-call(s32[64,1]{1,0:T(8,128)} %copy.12.prompt_ref, s32[1,64]{1,0:T(1,128)} %fusion.22.base_ref, bf16[64,18432]{1,0:T(8,128)(2,1)} %refs_3_.3, bf16[64,18432]{1,0:T(8,128)(2,1)} %refs_3_.3, bf16[64,18432]{1,0:T(8,128)(2,1)} %refs_3_.3, bf16[64,18432]{1,0:T(8,128)(2,1)} %refs_3_.3), custom_call_target="tpu_custom_call" | custom-call | tf_op jit(solution)/shard_map/place/pallas_call | solution.py:75
  54.4 0.0 copy-done.1
  54.4 0.0 copy-start.4
  54.4 4.1 %reshape.37 = bf16[64,32,576]{2,1,0:T(8,128)(2,1)} reshape(bf16[64,18432]{1,0:T(8,128)(2,1)S(1)} %copy-done.1) | data formatting | bytes 4718592 | tf_op jit(solution)/shard_map/reshape | solution.py:321
  58.6 0.0 copy-done.4
  58.6 0.1 iota_compare_fusion
  58.6 6.7 %fusion.24 = (f32[64,32]{1,0:T(8,128)S(1)}, f32[64,32,128]{2,1,0:T(8,128)S(1)}) fusion(bf16[64,32,576]{2,1,0:T(8,128)(2,1)} %reshape.37, bf16[64,576,128]{2,1,0:T(8,128)(2,1)} %param.9, pred[64,128]{1,0:T(8,128)(4,1)S(1)} %iota_compare_fusion), kind=kOutput, calls=%fused_computation.33 | convolution fusion | flops 302774272 | bytes 12861440 | tf_op jit(solution)/shard_map/fhe,fes->fhs/dot_general | solution.py:323
  65.3 0.6 fusion.12
  66.0 0.1 copy.14
  66.0 0.0 copy-start.3
  66.0 5.5 %fusion = f32[64,32,512]{2,1,0:T(8,128)S(1)} fusion(bf16[64,576,128]{2,1,0:T(8,128)(2,1)} %param.9, f32[64,32,128]{2,1,0:T(8,128)S(1)} %get-tuple-element.28, f32[64,32]{1,0:T(8,128)S(1)} %get-tuple-element.27, pred[64,128]{1,0:T(8,128)(4,1)S(1)} %iota_compare_fusion), kind=kOutput, calls=%fused_computation | convolution fusion | flops 269221888 | bytes 13647872 | tf_op jit(solution)/shard_map/fhs,frs->fhr/dot_general | solution.py:332
  71.6 0.0 copy-done.3
  71.6 2.6 %fusion.9 = bf16[32,8,8,128]{3,2,1,0:T(8,128)(2,1)S(1)} fusion(bf16[32,512,128]{2,1,0:T(8,128)(2,1)S(1)} %copy-done.3, f32[64,32,512]{2,1,0:T(8,128)S(1)} %fusion, f32[64,32]{0,1:T(8,128)S(1)} %copy.14), kind=kOutput, calls=%fused_computation.8 | convolution fusion | flops 270794752 | bytes 8921088 | tf_op jit(solution)/shard_map/nhr,hrv->nhv/dot_general | solution.py:339
  74.2 0.1 copy.27
  74.3 21.7 %all-to-all-done.1.q_ref = bf16[16,32,3456]{2,1,0:T(8,128)(2,1)} async-done(((bf16[16,32,3456]{2,1,0:T(8,128)(2,1)}), bf16[16,32,3456]{2,1,0:T(8,128)(2,1)}, u32[]{:S(2)}, u32[]{:S(2)}) %all-to-all-start.1) | async-done | bytes 3538976 | tf_op jit(solution)/shard_map/all_to_all | solution.py:356
  96.0 10.7 %all-to-all-start = ((bf16[16,32,1152]{2,1,0:T(8,128)(2,1)}), bf16[16,32,1152]{2,1,0:T(8,128)(2,1)S(1)}, u32[]{:S(2)}, u32[]{:S(2)}) async-start(bf16[16,32,1152]{2,1,0:T(8,128)(2,1)} %bitcast.2), calls=%async_computation | async-start | bytes 2359296 | tf_op jit(solution)/shard_map/all_to_all | solution.py:356
  106.7 0.0 all-gather.5.cloned.1.call-done.kv_ref
  106.8 16.6 %prefix.2.refs_0_ = bf16[128,3328]{1,0:T(8,128)(2,1)} custom-call(bf16[16,32,3456]{2,1,0:T(8,128)(2,1)} %all-to-all-done.1.q_ref, bf16[4,576,256]{2,1,0:T(8,128)(2,1)} %all-gather.3.cloned.1.call-done.own_ref, bf16[4,3,576,256]{3,2,1,0:T(8,128)(2,1)} %all-gather.5.cloned.1.call-done.kv_ref, bf16[32,512,128]{2,1,0:T(8,128)(2,1)} %w_hbm.3), custom_call_target="tpu_custom_call" | custom-call | flops 7247757312 | bytes 12255232 | tf_op jit(solution)/shard_map/prefix/pallas_call | solution.py:235
  123.3 0.0 copy-start
  123.4 0.7 all-to-all-done.q_ref
  124.0 0.0 copy-start.2
  124.0 1.0 copy-done.2
  125.1 9.5 %prefix.3 = bf16[128,4608]{1,0:T(8,128)(2,1)} custom-call(bf16[16,32,1152]{2,1,0:T(8,128)(2,1)} %copy-done.2, bf16[4,576,256]{2,1,0:T(8,128)(2,1)} %all-gather.3.cloned.1.call-done.own_ref, bf16[4,3,576,256]{3,2,1,0:T(8,128)(2,1)} %all-gather.5.cloned.1.call-done.kv_ref, bf16[32,512,128]{2,1,0:T(8,128)(2,1)} %w_hbm.3, bf16[128,3328]{1,0:T(8,128)(2,1)} %prefix.2.refs_0_), custom_call_target="tpu_custom_call" | custom-call | flops 2415919104 | bytes 8126464 | tf_op jit(solution)/shard_map/prefix/pallas_call | solution.py:235
  134.5 22.5 %all_to_all.15 = bf16[16,8,4608]{2,1,0:T(8,128)(2,1)S(1)} all-to-all(bf16[16,8,4608]{2,1,0:T(8,128)(2,1)} %bitcast.20), channel_id=1, replica_groups=mesh['zh'=4,'zl'=2,'xc'=8,'tp'=4] {'zl','xc'}, dimensions={0} | all-to-all | bytes 2359296 | tf_op jit(solution)/shard_map/all_to_all | solution.py:356
  157.0 0.0 copy-done
  157.0 3.2 %merge.1 = bf16[64,4096]{1,0:T(8,128)(2,1)} custom-call(s32[64,1]{1,0:T(8,128)S(1)} %copy-done, bf16[128,4608]{1,0:T(8,128)(2,1)S(1)} %bitcast.18, bf16[64,4096]{1,0:T(8,128)(2,1)S(1)} %bitcast.19, f32[64,32]{1,0:T(8,128)S(1)} %log_add_fusion.mass_ref), custom_call_target="tpu_custom_call" | custom-call | tf_op jit(solution)/shard_map/merge/pallas_call | solution.py:310
  (1 shorter events, 0.0 us)
Async XLA Ops:
  6.5 32.5 %all-gather.3.cloned.1.call-start = ((), (), s32[]{:S(2)}) async-start(), calls=%async_computation.3 | async-start | bytes 1474560 | tf_op jit(solution)/shard_map/all_gather | solution.py:360
  7.3 19.7 %collective-permute-start = (bf16[1,576,256]{2,1,0:T(8,128)(2,1)}, bf16[1,576,256]{2,1,0:T(8,128)(2,1)S(1)}, u32[]{:S(2)}, u32[]{:S(2)}) collective-permute-start(bf16[1,576,256]{2,1,0:T(8,128)(2,1)} %param.8), channel_id=1, source_target_pairs={{0,64},{64,128},{128,192},{192,0},{1,65},{65,129},{129,193},{193,1... | collective-permute-start | bytes 884744 | tf_op jit(solution)/shard_map/ppermute | solution.py:351
  11.2 25.0 %collective-permute-start.2 = (bf16[1,576,256]{2,1,0:T(8,128)(2,1)}, bf16[1,576,256]{2,1,0:T(8,128)(2,1)S(1)}, u32[]{:S(2)}, u32[]{:S(2)}) collective-permute-start(bf16[1,576,256]{2,1,0:T(8,128)(2,1)} %param.8), channel_id=1, source_target_pairs={{0,192},{64,0},{128,64},{192,128},{1,193},{65,1},{129,65},{193,129... | collective-permute-start | bytes 884744 | tf_op jit(solution)/shard_map/ppermute | solution.py:351
  14.3 21.9 %collective-permute-start.1 = (bf16[1,576,256]{2,1,0:T(8,128)(2,1)}, bf16[1,576,256]{2,1,0:T(8,128)(2,1)S(1)}, u32[]{:S(2)}, u32[]{:S(2)}) collective-permute-start(bf16[1,576,256]{2,1,0:T(8,128)(2,1)} %param.8), channel_id=1, source_target_pairs={{0,128},{64,192},{128,0},{192,64},{1,129},{65,193},{129,1},{193,65... | collective-permute-start | bytes 884744 | tf_op jit(solution)/shard_map/ppermute | solution.py:351
  39.0 57.0 %all-to-all-start.1 = ((bf16[16,32,3456]{2,1,0:T(8,128)(2,1)}), bf16[16,32,3456]{2,1,0:T(8,128)(2,1)}, u32[]{:S(2)}, u32[]{:S(2)}) async-start(bf16[16,32,3456]{2,1,0:T(8,128)(2,1)} %bitcast.21), calls=%async_computation.1 | async-start | bytes 7077888 | tf_op jit(solution)/shard_map/all_to_all | solution.py:356
  50.0 56.8 %all-gather.5.cloned.1.call-start = ((), (), s32[]{:S(2)}) async-start(), calls=%async_computation.4 | async-start | bytes 4423680 | tf_op jit(solution)/shard_map/all_gather | solution.py:365
  51.1 3.3 %copy-start.1 = (bf16[64,18432]{1,0:T(8,128)(2,1)S(1)}, bf16[64,18432]{1,0:T(8,128)(2,1)}, u32[]{:S(2)}) copy-start(bf16[64,18432]{1,0:T(8,128)(2,1)} %refs_3_.3) | copy-start | bytes 7077892
  54.4 4.1 %copy-start.4 = (s32[64]{0:T(128)S(1)}, s32[64]{0:T(128)}, u32[]{:S(2)}) copy-start(s32[64]{0:T(128)} %param.13) | copy-start | bytes 772
  66.0 5.5 %copy-start.3 = (bf16[32,512,128]{2,1,0:T(8,128)(2,1)S(1)}, bf16[32,512,128]{2,1,0:T(8,128)(2,1)}, u32[]{:S(2)}) copy-start(bf16[32,512,128]{2,1,0:T(8,128)(2,1)} %w_hbm.3) | copy-start | bytes 12582916
  96.0 28.0 %all-to-all-start = ((bf16[16,32,1152]{2,1,0:T(8,128)(2,1)}), bf16[16,32,1152]{2,1,0:T(8,128)(2,1)S(1)}, u32[]{:S(2)}, u32[]{:S(2)}) async-start(bf16[16,32,1152]{2,1,0:T(8,128)(2,1)} %bitcast.2), calls=%async_computation | async-start | bytes 2359296 | tf_op jit(solution)/shard_map/all_to_all | solution.py:356
  123.3 33.7 %copy-start = (s32[64,1]{1,0:T(8,128)S(1)}, s32[64,1]{1,0:T(8,128)}, u32[]{:S(2)}) copy-start(s32[64,1]{1,0:T(8,128)} %get-tuple-element.16.target_ref) | copy-start | bytes 772
  124.0 1.0 copy-start.2
Sparse Core Ops, SparseCore 0:
  9.2 29.8 all-gather.2
  52.6 42.8 all-gather.4

commit v5 on v4

--- a/solution.py
+++ b/solution.py
@@ -15,7 +15,7 @@
 MOST = 2
 COPIES = 4
 SPLIT = 4
-PARTS = ((0, 3), (3, 1))
+PARTS = ((0, 2), (2, 2))
 CHUNKS = 2
 LANES = 128
 SCALE = 192.0 ** (-0.5)
@@ -93,7 +93,7 @@
     )(prompt, base, *[queries] * SPLIT)
 
 
-def prefix_kernel(part, q_ref, own_ref, kv_ref, w_hbm, *refs):
+def prefix_kernel(part, q_ref, kv_ref, w_hbm, *refs):
     *earlier, out_ref, w_ref, key_ref, lat_ref, part_ref, cell_ref, mass_ref, sem = refs
     ahead_of_it = earlier[0].shape[1] if earlier else 0
     step = pl.program_id(0)
@@ -120,19 +120,10 @@
         if earlier:
             out_ref[:, :ahead_of_it] = earlier[0][...]
 
-    def keep(ref):
-        for n in range(ref.shape[0]):
-            cut = slice(n * quarter, (n + 1) * quarter)
-            key_ref[0:KEY, cut] = ref[n]
-            key_ref[KEY : KEY + P_SIZE, cut] = ref[n, R:KEY, :]
-
-    @pl.when(step == 0)
-    def _():
-        keep(own_ref)
-
-    @pl.when(step > 0)
-    def _():
-        keep(kv_ref)
+    for n in range(kv_ref.shape[0]):
+        cut = slice(n * quarter, (n + 1) * quarter)
+        key_ref[0:KEY, cut] = kv_ref[n]
+        key_ref[KEY : KEY + P_SIZE, cut] = kv_ref[n, R:KEY, :]
 
     tall = group * MOST * SPLIT
     span = group * MOST
@@ -224,13 +215,13 @@
         put(heads * V, jnp.concatenate([high, low], axis=1))
 
 
-def prefix(received, own, caches, w_uv, part, *earlier):
+def prefix(received, caches, w_uv, part, *earlier):
     group, _, width = received.shape
     heads = 2 * part[1] * SPLIT
     rows = group * COPIES * MOST
     tall = group * MOST * SPLIT
-    parts = own.shape[0]
-    length = parts * own.shape[2]
+    parts = caches.shape[0]
+    length = parts * caches.shape[3]
     wide = heads * V + 2 * LANES + sum(one.shape[1] for one in earlier)
     return pl.pallas_call(
         functools.partial(prefix_kernel, part),
@@ -238,10 +229,7 @@
         grid=(COPIES,),
         in_specs=[
             pl.BlockSpec((group, MOST * SPLIT, width), lambda i: (0, i, 0)),
-            pl.BlockSpec(own.shape, lambda i: (0, 0, 0), pipeline_mode=pl.Buffered(1)),
-            pl.BlockSpec(
-                (parts, None, *caches.shape[2:]), lambda i: (0, jnp.maximum(i - 1, 0), 0, 0)
-            ),
+            pl.BlockSpec((parts, None, *caches.shape[2:]), lambda i: (0, i, 0, 0)),
             pl.BlockSpec(memory_space=pl.ANY),
             *[
                 pl.BlockSpec(one.shape, lambda i: (0, 0), pipeline_mode=pl.Buffered(1))
@@ -261,11 +249,11 @@
         compiler_params=pltpu.CompilerParams(vmem_limit_bytes=56 << 20),
         cost_estimate=pl.CostEstimate(
             flops=2 * rows * heads * length * (KEY + R) + 2 * rows * heads * R * V,
-            bytes_accessed=2 * (received.size + own.size + caches.size + heads * R * V + rows * wide),
+            bytes_accessed=2 * (received.size + caches.size + heads * R * V + rows * wide),
             transcendentals=rows * heads * length,
         ),
         name="prefix",
-    )(received, own, caches, w_uv, *earlier)
+    )(received, caches, w_uv, *earlier)
 
 
 def merge_kernel(target_ref, answer_ref, value_ref, mass_ref, out_ref):
@@ -347,30 +335,32 @@
     back = (lax.axis_index("zh") - prompt_slot // group) % COPIES
     base = ((prompt_slot % group) * held + back * MOST)[None, :].astype(jnp.int32)
 
-    def from_behind(steps):
-        return lax.ppermute(
-            prefix_cache, "zh", [(n, (n + steps) % COPIES) for n in range(COPIES)]
-        )
+    def along(value, steps):
+        return lax.ppermute(value, "zh", [(n, (n + steps) % COPIES) for n in range(COPIES)])
 
     def exchange(value):
         return lax.all_to_all(
             value.reshape(group, -1, value.shape[1]), near, split_axis=0, concat_axis=0, tiled=True
         )
 
-    own = lax.all_gather(prefix_cache, "tp", axis=0, tiled=True)
-    moved = [from_behind(n) for n in range(1, COPIES)]
+    middle = prefix_cache.shape[1] // 2
+    behind, before = along(prefix_cache, 1), along(prefix_cache, COPIES - 1)
+    across = [along(behind[:, :middle], 1), along(before[:, middle:], COPIES - 1)]
     outbound, targets = zip(*[place(fork_prompt, base, queries, group, part) for part in PARTS])
     outbound = list(outbound)
-    outbound[0], own, *moved = lax.optimization_barrier((outbound[0], own, *moved))
-    caches = lax.all_gather(jnp.stack(moved, axis=1), "tp", axis=0, tiled=True)
+    outbound[0], behind, before, *across = lax.optimization_barrier(
+        (outbound[0], behind, before, *across)
+    )
+    held_here = [prefix_cache, behind, jnp.concatenate(across, axis=1), before]
+    caches = lax.all_gather(jnp.stack(held_here, axis=1), "tp", axis=0, tiled=True)
     value_suffix, mass_suffix = suffix(queries, suffix_cache, suffix_len, w_uv)
     received = [exchange(outbound[0])]
     outbound[1], value_suffix, mass_suffix = lax.optimization_barrier(
         (outbound[1], value_suffix, mass_suffix)
     )
     received.append(exchange(outbound[1]))
-    result = prefix(received[0], own, caches, w_uv, PARTS[0])
-    result = prefix(received[1], own, caches, w_uv, PARTS[1], result)
+    result = prefix(received[0], caches, w_uv, PARTS[0])
+    result = prefix(received[1], caches, w_uv, PARTS[1], result)
     answer = exchange(result).reshape(result.shape)
     return merge(targets[0], answer, value_suffix, mass_suffix)
 

time: 167 us -> 160 us (0.958)
  starting transfers between devices: 33.1 us -> 27.9 us
  Pallas kernels: 38.2 us -> 33.1 us
  blocking collectives: 22.5 us -> 24.9 us
  local copies, waits for them, and re-layouts: 6.68 us -> 8.65 us
    all_to_all x2, waiting for transfers between devices: 22.4 us -> 4.33 us  [exchange(): lax.all_to_all(value.reshape(group, -1, value.shape[1]), near, split_axis...]
    all_gather x2 -> x1, waiting for transfers between devices: 2.89 us -> 19.7 us  [shards(): lax.all_gather(jnp.stack(held_here, axis=1), 'tp', axis=0, tiled=True)]
    all_to_all x2, starting transfers between devices: 21.7 us -> 13.2 us  [exchange(): lax.all_to_all(value.reshape(group, -1, value.shape[1]), near, split_axis...]
    pallas_call x2, Pallas kernels: 26.1 us -> 22.3 us  [prefix(): pl.pallas_call(functools.partial(prefix_kernel, part), out_shape=jax.Shap...]
    ppermute x3 -> x4, starting transfers between devices: 11.4 us -> 14.4 us  [along(): lax.ppermute(value, 'zh', [(n, (n + steps) % COPIES) for n in range(COPIE...]
    all_to_all x1, blocking collectives: 22.5 us -> 24.9 us  [exchange(): lax.all_to_all(value.reshape(group, -1, value.shape[1]), near, split_axis...]
    unnamed x11 -> x17, local copies, waits for them, and re-layouts: 2.41 us -> 4.42 us
    dot_general x1, matrix products: 6.68 us -> 4.74 us  [suffix(): jnp.einsum('fhe,fes->fhs', query_heads, suffix_cache, preferred_element_t...]
  transfers between devices with their start and end apart: 7 -> 7, of which waited for: 4 -> 6; matrix products, arithmetic and copies ran while one was open for 14% -> 15% of each run, Pallas kernels for 15% -> 12%
where the time goes in v5:
time: 160 us
  waiting for transfers between devices  34.1 us (21%)
  Pallas kernels  33.1 us (21%)
  starting transfers between devices  27.9 us (17%)
  blocking collectives  24.9 us (16%)
  matrix products  14.6 us (9%)
  between operations  13.5 us (8%)
  local copies, waits for them, and re-layouts  8.65 us (5%)
  other arithmetic  3.12 us (2%)
    all_to_all x1, blocking collectives, exchange(): lax.all_to_all(value.reshape(group, -1, value.shape[1]), near, split_axis...  24.9 us
    pallas_call x2, Pallas kernels, prefix(): pl.pallas_call(functools.partial(prefix_kernel, part), out_shape=jax.Shap...  22.3 us
    all_gather x1, waiting for transfers between devices, shards(): lax.all_gather(jnp.stack(held_here, axis=1), 'tp', axis=0, tiled=True)  19.7 us
    ppermute x4, starting transfers between devices, along(): lax.ppermute(value, 'zh', [(n, (n + steps) % COPIES) for n in range(COPIE...  14.4 us
    all_to_all x2, starting transfers between devices, exchange(): lax.all_to_all(value.reshape(group, -1, value.shape[1]), near, split_axis...  13.2 us
    ppermute x4, waiting for transfers between devices, along(): lax.ppermute(value, 'zh', [(n, (n + steps) % COPIES) for n in range(COPIE...  9.98 us
    pallas_call x2, Pallas kernels, place(): pl.pallas_call(place_kernel, out_shape=(jax.ShapeDtypeStruct((rows, mine...  7.86 us
    dot_general x1, matrix products, suffix(): jnp.einsum('fhs,frs->fhr', weights.astype(jnp.bfloat16), suffix_cache[:,...  7.27 us
  transfers between devices with their start and end apart: 7, of which 6 were waited for; matrix products, arithmetic and copies ran while one was open for 15% of the time, Pallas kernels for 12%

profile of v5, /device:TPU:1, one launch (start us, length us, event | category | flops | bytes accessed | tf_op | source)
XLA Modules:
  0.0 159.8 jit_solution(17172654693942660606)
XLA Ops:
  6.5 3.8 %collective-permute-start = (bf16[1,576,256]{2,1,0:T(8,128)(2,1)}, bf16[1,576,256]{2,1,0:T(8,128)(2,1)S(1)}, u32[]{:S(2)}, u32[]{:S(2)}) collective-permute-start(bf16[1,576,256]{2,1,0:T(8,128)(2,1)} %param.8), channel_id=1, source_target_pairs={{0,64},{64,128},{128,192},{192,0},{1,65},{65,129},{129,193},{193,1... | collective-permute-start | bytes 884744 | tf_op jit(solution)/shard_map/ppermute | solution.py:339
  10.4 3.0 %collective-permute-start.1 = (bf16[1,576,256]{2,1,0:T(8,128)(2,1)}, bf16[1,576,256]{2,1,0:T(8,128)(2,1)S(1)}, u32[]{:S(2)}, u32[]{:S(2)}) collective-permute-start(bf16[1,576,256]{2,1,0:T(8,128)(2,1)} %param.8), channel_id=1, source_target_pairs={{0,192},{64,0},{128,64},{192,128},{1,193},{65,1},{129,65},{193,129... | collective-permute-start | bytes 884744 | tf_op jit(solution)/shard_map/ppermute | solution.py:339
  13.4 1.4 copy.12.prompt_ref
  14.7 7.6 %collective-permute-done = bf16[1,576,256]{2,1,0:T(8,128)(2,1)S(1)} collective-permute-done((bf16[1,576,256]{2,1,0:T(8,128)(2,1)}, bf16[1,576,256]{2,1,0:T(8,128)(2,1)S(1)}, u32[]{:S(2)}, u32[]{:S(2)}) %collective-permute-start) | collective-permute-done | bytes 294944 | tf_op jit(solution)/shard_map/ppermute | solution.py:339
  22.3 5.1 %collective-permute-start.2 = (bf16[1,288,256]{2,1,0:T(8,128)(2,1)S(1)}, bf16[1,288,256]{2,1,0:T(8,128)(2,1)S(1)}, u32[]{:S(2)}, u32[]{:S(2)}) collective-permute-start(bf16[1,288,256]{2,1,0:T(8,128)(2,1)S(1)} %slice.12), channel_id=1, source_target_pairs={{0,64},{64,128},{128,192},{192,0},{1,65},{65,129},{129,193},{193,1... | collective-permute-start | bytes 442376 | tf_op jit(solution)/shard_map/ppermute | solution.py:339
  27.4 0.7 collective-permute-done.1
  28.1 2.4 %collective-permute-start.3 = (bf16[1,288,256]{2,1,0:T(8,128)(2,1)S(1)}, bf16[1,288,256]{2,1,0:T(8,128)(2,1)S(1)}, u32[]{:S(2)}, u32[]{:S(2)}) collective-permute-start(bf16[1,288,256]{2,1,0:T(8,128)(2,1)S(1)} %slice.13), channel_id=1, source_target_pairs={{0,192},{64,0},{128,64},{192,128},{1,193},{65,1},{129,65},{193,129... | collective-permute-start | bytes 442376 | tf_op jit(solution)/shard_map/ppermute | solution.py:339
  30.6 1.2 fusion.22.base_ref
  31.8 3.8 %place.2 = (bf16[512,2304]{1,0:T(8,128)(2,1)}, s32[64,1]{1,0:T(8,128)}) custom-call(s32[64,1]{1,0:T(8,128)} %copy.12.prompt_ref, s32[1,64]{1,0:T(1,128)} %fusion.22.base_ref, bf16[64,18432]{1,0:T(8,128)(2,1)} %refs_3_.3, bf16[64,18432]{1,0:T(8,128)(2,1)} %refs_3_.3, bf16[64,18432]{1,0:T(8,128)(2,1)} %refs_3_.3, bf16[64,18432]{1,0:T(8,128)(2,1)} %refs_3_.3), custom_call_target="tpu_custom_call" | custom-call | tf_op jit(solution)/shard_map/place/pallas_call | solution.py:75
  35.6 0.0 collective-permute-done.2
  35.6 1.7 %collective-permute-done.3 = bf16[1,288,256]{2,1,0:T(8,128)(2,1)S(1)} collective-permute-done((bf16[1,288,256]{2,1,0:T(8,128)(2,1)S(1)}, bf16[1,288,256]{2,1,0:T(8,128)(2,1)S(1)}, u32[]{:S(2)}, u32[]{:S(2)}) %collective-permute-start.3) | collective-permute-done | bytes 147488 | tf_op jit(solution)/shard_map/ppermute | solution.py:339
  37.3 0.0 copy-start.5
  37.3 5.8 %all-to-all-start.1 = ((bf16[16,32,2304]{2,1,0:T(8,128)(2,1)}), bf16[16,32,2304]{2,1,0:T(8,128)(2,1)}, u32[]{:S(2)}, u32[]{:S(2)}) async-start(bf16[16,32,2304]{2,1,0:T(8,128)(2,1)} %bitcast.22), calls=%async_computation.1 | async-start | bytes 4718592 | tf_op jit(solution)/shard_map/all_to_all | solution.py:342
  43.1 0.0 copy-start.1
  43.1 0.2 all-gather.2.cloned.1.call-start
  43.4 0.0 copy-done.5
  43.4 1.2 pad_maximum_fusion
  44.6 0.0 all-gather.2.cloned.1.call-update
  44.6 0.6 copy-done.1
  45.2 4.0 %reshape.37 = bf16[64,32,576]{2,1,0:T(8,128)(2,1)} reshape(bf16[64,18432]{1,0:T(8,128)(2,1)S(1)} %copy-done.1) | data formatting | bytes 4718592 | tf_op jit(solution)/shard_map/reshape | solution.py:309
  49.2 0.0 copy-start.6
  49.2 0.0 copy-start.2
  49.2 4.0 %place.3 = (bf16[512,2304]{1,0:T(8,128)(2,1)}, s32[64,1]{1,0:T(8,128)}) custom-call(s32[64,1]{1,0:T(8,128)} %copy.12.prompt_ref, s32[1,64]{1,0:T(1,128)} %fusion.22.base_ref, bf16[64,18432]{1,0:T(8,128)(2,1)} %refs_3_.3, bf16[64,18432]{1,0:T(8,128)(2,1)} %refs_3_.3, bf16[64,18432]{1,0:T(8,128)(2,1)} %refs_3_.3, bf16[64,18432]{1,0:T(8,128)(2,1)} %refs_3_.3), custom_call_target="tpu_custom_call" | custom-call | tf_op jit(solution)/shard_map/place/pallas_call | solution.py:75
  53.3 0.0 copy-done.6
  53.3 0.1 iota_compare_fusion
  53.3 0.0 copy-done.2
  53.4 4.7 %fusion.24 = (f32[64,32]{1,0:T(8,128)S(1)}, f32[64,32,128]{2,1,0:T(8,128)S(1)}) fusion(bf16[64,32,576]{2,1,0:T(8,128)(2,1)S(1)} %copy-done.2, bf16[64,576,128]{2,1,0:T(8,128)(2,1)} %param.9, pred[64,128]{1,0:T(8,128)(4,1)S(1)} %iota_compare_fusion), kind=kOutput, calls=%fused_computation.34 | convolution fusion | flops 302774272 | bytes 12861440 | tf_op jit(solution)/shard_map/fhe,fes->fhs/dot_general | solution.py:311
  58.1 0.0 copy-start.3
  58.1 1.0 copy-done.3
  59.1 0.6 fusion.12
  59.7 0.1 copy.14
  59.8 0.0 copy-start.7
  59.8 7.3 %fusion = f32[64,32,512]{2,1,0:T(8,128)S(1)} fusion(bf16[64,576,128]{2,1,0:T(8,128)(2,1)} %param.9, f32[64,32,128]{2,1,0:T(8,128)} %copy-done.3, f32[64,32]{1,0:T(8,128)S(1)} %get-tuple-element.27, pred[64,128]{1,0:T(8,128)(4,1)S(1)} %iota_compare_fusion), kind=kOutput, calls=%fused_computation | convolution fusion | flops 269221888 | bytes 13647872 | tf_op jit(solution)/shard_map/fhs,frs->fhr/dot_general | solution.py:320
  67.1 0.0 copy-done.7
  67.1 2.6 %fusion.9 = bf16[32,8,8,128]{3,2,1,0:T(8,128)(2,1)S(1)} fusion(bf16[32,512,128]{2,1,0:T(8,128)(2,1)S(1)} %copy-done.7, f32[64,32,512]{2,1,0:T(8,128)S(1)} %fusion, f32[64,32]{0,1:T(8,128)S(1)} %copy.14), kind=kOutput, calls=%fused_computation.8 | convolution fusion | flops 270794752 | bytes 8921088 | tf_op jit(solution)/shard_map/nhr,hrv->nhv/dot_general | solution.py:327
  69.7 0.1 copy.27
  69.8 4.2 %all-to-all-done.1.q_ref = bf16[16,32,2304]{2,1,0:T(8,128)(2,1)} async-done(((bf16[16,32,2304]{2,1,0:T(8,128)(2,1)}), bf16[16,32,2304]{2,1,0:T(8,128)(2,1)}, u32[]{:S(2)}, u32[]{:S(2)}) %all-to-all-start.1) | async-done | bytes 2359328 | tf_op jit(solution)/shard_map/all_to_all | solution.py:342
  74.0 7.5 %all-to-all-start = ((bf16[16,32,2304]{2,1,0:T(8,128)(2,1)}), bf16[16,32,2304]{2,1,0:T(8,128)(2,1)S(1)}, u32[]{:S(2)}, u32[]{:S(2)}) async-start(bf16[16,32,2304]{2,1,0:T(8,128)(2,1)} %bitcast.2), calls=%async_computation | async-start | bytes 4718592 | tf_op jit(solution)/shard_map/all_to_all | solution.py:342
  81.5 19.7 %all-gather.2.cloned.1.call-done.kv_ref = bf16[4,4,576,256]{3,2,1,0:T(8,128)(2,1)} async-done(((bf16[1,4,576,256]{3,2,1,0:T(8,128)(2,1)}), bf16[4,4,576,256]{3,2,1,0:T(8,128)(2,1)}) %all-gather.2.cloned.1.call-update) | async-done | bytes 4718608 | tf_op jit(solution)/shard_map/all_gather | solution.py:355
  101.2 10.9 %prefix.2.refs_0_ = bf16[128,2304]{1,0:T(8,128)(2,1)} custom-call(bf16[16,32,2304]{2,1,0:T(8,128)(2,1)} %all-to-all-done.1.q_ref, bf16[4,4,576,256]{3,2,1,0:T(8,128)(2,1)} %all-gather.2.cloned.1.call-done.kv_ref, bf16[32,512,128]{2,1,0:T(8,128)(2,1)} %w_hbm.3), custom_call_target="tpu_custom_call" | custom-call | flops 4831838208 | bytes 9764864 | tf_op jit(solution)/shard_map/prefix/pallas_call | solution.py:226
  112.2 0.0 copy-start
  112.2 0.1 all-to-all-done.q_ref
  112.3 0.0 copy-start.4
  112.3 1.4 copy-done.4
  113.7 11.4 %prefix.3 = bf16[128,4608]{1,0:T(8,128)(2,1)} custom-call(bf16[16,32,2304]{2,1,0:T(8,128)(2,1)} %copy-done.4, bf16[4,4,576,256]{3,2,1,0:T(8,128)(2,1)} %all-gather.2.cloned.1.call-done.kv_ref, bf16[32,512,128]{2,1,0:T(8,128)(2,1)} %w_hbm.3, bf16[128,2304]{1,0:T(8,128)(2,1)} %prefix.2.refs_0_), custom_call_target="tpu_custom_call" | custom-call | flops 4831838208 | bytes 10354688 | tf_op jit(solution)/shard_map/prefix/pallas_call | solution.py:226
  125.1 24.9 %all_to_all.15 = bf16[16,8,4608]{2,1,0:T(8,128)(2,1)S(1)} all-to-all(bf16[16,8,4608]{2,1,0:T(8,128)(2,1)} %bitcast.23), channel_id=1, replica_groups=mesh['zh'=4,'zl'=2,'xc'=8,'tp'=4] {'zl','xc'}, dimensions={0} | all-to-all | bytes 2359296 | tf_op jit(solution)/shard_map/all_to_all | solution.py:342
  150.0 0.0 copy-done
  150.0 3.0 %merge.1 = bf16[64,4096]{1,0:T(8,128)(2,1)} custom-call(s32[64,1]{1,0:T(8,128)S(1)} %copy-done, bf16[128,4608]{1,0:T(8,128)(2,1)S(1)} %bitcast.20, bf16[64,4096]{1,0:T(8,128)(2,1)S(1)} %bitcast.21, f32[64,32]{1,0:T(8,128)S(1)} %log_add_fusion.mass_ref), custom_call_target="tpu_custom_call" | custom-call | tf_op jit(solution)/shard_map/merge/pallas_call | solution.py:298
  (4 shorter events, 0.1 us)
Async XLA Ops:
  6.5 15.8 %collective-permute-start = (bf16[1,576,256]{2,1,0:T(8,128)(2,1)}, bf16[1,576,256]{2,1,0:T(8,128)(2,1)S(1)}, u32[]{:S(2)}, u32[]{:S(2)}) collective-permute-start(bf16[1,576,256]{2,1,0:T(8,128)(2,1)} %param.8), channel_id=1, source_target_pairs={{0,64},{64,128},{128,192},{192,0},{1,65},{65,129},{129,193},{193,1... | collective-permute-start | bytes 884744 | tf_op jit(solution)/shard_map/ppermute | solution.py:339
  10.4 17.8 %collective-permute-start.1 = (bf16[1,576,256]{2,1,0:T(8,128)(2,1)}, bf16[1,576,256]{2,1,0:T(8,128)(2,1)S(1)}, u32[]{:S(2)}, u32[]{:S(2)}) collective-permute-start(bf16[1,576,256]{2,1,0:T(8,128)(2,1)} %param.8), channel_id=1, source_target_pairs={{0,192},{64,0},{128,64},{192,128},{1,193},{65,1},{129,65},{193,129... | collective-permute-start | bytes 884744 | tf_op jit(solution)/shard_map/ppermute | solution.py:339
  22.3 13.3 %collective-permute-start.2 = (bf16[1,288,256]{2,1,0:T(8,128)(2,1)S(1)}, bf16[1,288,256]{2,1,0:T(8,128)(2,1)S(1)}, u32[]{:S(2)}, u32[]{:S(2)}) collective-permute-start(bf16[1,288,256]{2,1,0:T(8,128)(2,1)S(1)} %slice.12), channel_id=1, source_target_pairs={{0,64},{64,128},{128,192},{192,0},{1,65},{65,129},{129,193},{193,1... | collective-permute-start | bytes 442376 | tf_op jit(solution)/shard_map/ppermute | solution.py:339
  28.1 9.2 %collective-permute-start.3 = (bf16[1,288,256]{2,1,0:T(8,128)(2,1)S(1)}, bf16[1,288,256]{2,1,0:T(8,128)(2,1)S(1)}, u32[]{:S(2)}, u32[]{:S(2)}) collective-permute-start(bf16[1,288,256]{2,1,0:T(8,128)(2,1)S(1)} %slice.13), channel_id=1, source_target_pairs={{0,192},{64,0},{128,64},{192,128},{1,193},{65,1},{129,65},{193,129... | collective-permute-start | bytes 442376 | tf_op jit(solution)/shard_map/ppermute | solution.py:339
  37.3 6.0 %copy-start.5 = (bf16[1,576,256]{2,1,0:T(8,128)(2,1)S(1)}, bf16[1,576,256]{2,1,0:T(8,128)(2,1)}, u32[]{:S(2)}) copy-start(bf16[1,576,256]{2,1,0:T(8,128)(2,1)} %param.8) | copy-start | bytes 884740
  37.3 36.7 %all-to-all-start.1 = ((bf16[16,32,2304]{2,1,0:T(8,128)(2,1)}), bf16[16,32,2304]{2,1,0:T(8,128)(2,1)}, u32[]{:S(2)}, u32[]{:S(2)}) async-start(bf16[16,32,2304]{2,1,0:T(8,128)(2,1)} %bitcast.22), calls=%async_computation.1 | async-start | bytes 4718592 | tf_op jit(solution)/shard_map/all_to_all | solution.py:342
  43.1 2.1 %copy-start.1 = (bf16[64,18432]{1,0:T(8,128)(2,1)S(1)}, bf16[64,18432]{1,0:T(8,128)(2,1)}, u32[]{:S(2)}) copy-start(bf16[64,18432]{1,0:T(8,128)(2,1)} %refs_3_.3) | copy-start | bytes 7077892
  43.1 58.1 %all-gather.2.cloned.1.call-start = ((), (), s32[]{:S(2)}) async-start(), calls=%async_computation.3 | async-start | bytes 5898240 | tf_op jit(solution)/shard_map/all_gather | solution.py:355
  49.2 4.0 %copy-start.6 = (s32[64]{0:T(128)S(1)}, s32[64]{0:T(128)}, u32[]{:S(2)}) copy-start(s32[64]{0:T(128)} %param.13) | copy-start | bytes 772
  49.2 4.1 %copy-start.2 = (bf16[64,32,576]{2,1,0:T(8,128)(2,1)S(1)}, bf16[64,32,576]{2,1,0:T(8,128)(2,1)}, u32[]{:S(2)}) copy-start(bf16[64,32,576]{2,1,0:T(8,128)(2,1)} %reshape.37) | copy-start | bytes 7077892
  58.1 1.0 copy-start.3
  59.8 7.3 %copy-start.7 = (bf16[32,512,128]{2,1,0:T(8,128)(2,1)S(1)}, bf16[32,512,128]{2,1,0:T(8,128)(2,1)}, u32[]{:S(2)}) copy-start(bf16[32,512,128]{2,1,0:T(8,128)(2,1)} %w_hbm.3) | copy-start | bytes 12582916
  74.0 38.3 %all-to-all-start = ((bf16[16,32,2304]{2,1,0:T(8,128)(2,1)}), bf16[16,32,2304]{2,1,0:T(8,128)(2,1)S(1)}, u32[]{:S(2)}, u32[]{:S(2)}) async-start(bf16[16,32,2304]{2,1,0:T(8,128)(2,1)} %bitcast.2), calls=%async_computation | async-start | bytes 4718592 | tf_op jit(solution)/shard_map/all_to_all | solution.py:342
  112.2 37.9 %copy-start = (s32[64,1]{1,0:T(8,128)S(1)}, s32[64,1]{1,0:T(8,128)}, u32[]{:S(2)}) copy-start(s32[64,1]{1,0:T(8,128)} %get-tuple-element.16.target_ref) | copy-start | bytes 772
  112.3 1.4 copy-start.4
Sparse Core Ops, SparseCore 0:
  45.8 55.4 all-gather.1

commit v6 on v5

--- a/solution.py
+++ b/solution.py
@@ -93,9 +93,8 @@
     )(prompt, base, *[queries] * SPLIT)
 
 
-def prefix_kernel(part, q_ref, kv_ref, w_hbm, *refs):
-    *earlier, out_ref, w_ref, key_ref, lat_ref, part_ref, cell_ref, mass_ref, sem = refs
-    ahead_of_it = earlier[0].shape[1] if earlier else 0
+def prefix_kernel(part, q_ref, kv_ref, w_hbm, out_ref, *scratch):
+    w_ref, key_ref, lat_ref, part_ref, cell_ref, mass_ref, sem = scratch
     step = pl.program_id(0)
     last = pl.num_programs(0) - 1
     heads = w_ref.shape[0]
@@ -117,8 +116,6 @@
     def _():
         for fetch in fetches:
             fetch.start()
-        if earlier:
-            out_ref[:, :ahead_of_it] = earlier[0][...]
 
     for n in range(kv_ref.shape[0]):
         cut = slice(n * quarter, (n + 1) * quarter)
@@ -199,8 +196,7 @@
         turn = (come == (slot // MOST) * span + source * MOST + slot % MOST).astype(jnp.bfloat16)
 
         def put(at, block):
-            begin = ahead_of_it + at
-            out_ref[:, begin : begin + block.shape[1]] = jnp.dot(
+            out_ref[:, at : at + block.shape[1]] = jnp.dot(
                 turn, block, preferred_element_type=jnp.float32
             ).astype(jnp.bfloat16)
 
@@ -215,14 +211,14 @@
         put(heads * V, jnp.concatenate([high, low], axis=1))
 
 
-def prefix(received, caches, w_uv, part, *earlier):
+def prefix(received, caches, w_uv, part):
     group, _, width = received.shape
     heads = 2 * part[1] * SPLIT
     rows = group * COPIES * MOST
     tall = group * MOST * SPLIT
     parts = caches.shape[0]
     length = parts * caches.shape[3]
-    wide = heads * V + 2 * LANES + sum(one.shape[1] for one in earlier)
+    wide = heads * V + 2 * LANES
     return pl.pallas_call(
         functools.partial(prefix_kernel, part),
         out_shape=jax.ShapeDtypeStruct((rows, wide), jnp.bfloat16),
@@ -231,10 +227,6 @@
             pl.BlockSpec((group, MOST * SPLIT, width), lambda i: (0, i, 0)),
             pl.BlockSpec((parts, None, *caches.shape[2:]), lambda i: (0, i, 0, 0)),
             pl.BlockSpec(memory_space=pl.ANY),
-            *[
-                pl.BlockSpec(one.shape, lambda i: (0, 0), pipeline_mode=pl.Buffered(1))
-                for one in earlier
-            ],
         ],
         out_specs=pl.BlockSpec((rows, wide), lambda i: (0, 0)),
         scratch_shapes=[
@@ -246,33 +238,28 @@
             pltpu.VMEM((rows, LANES), jnp.float32),
             pltpu.SemaphoreType.DMA((SPLIT,)),
         ],
-        compiler_params=pltpu.CompilerParams(vmem_limit_bytes=56 << 20),
+        compiler_params=pltpu.CompilerParams(vmem_limit_bytes=62 << 20),
         cost_estimate=pl.CostEstimate(
             flops=2 * rows * heads * length * (KEY + R) + 2 * rows * heads * R * V,
             bytes_accessed=2 * (received.size + caches.size + heads * R * V + rows * wide),
             transcendentals=rows * heads * length,
         ),
         name="prefix",
-    )(received, caches, w_uv, *earlier)
-
-
-def merge_kernel(target_ref, answer_ref, value_ref, mass_ref, out_ref):
+    )(received, caches, w_uv)
+
+
+def merge_kernel(target_ref, *refs):
+    answers = refs[: len(PARTS)]
+    value_ref, mass_ref, out_ref = refs[len(PARTS) :]
     forks, heads = mass_ref.shape
     group_heads = heads // SPLIT
-    at = lax.broadcasted_iota(jnp.int32, (forks, answer_ref.shape[0]), 1)
+    at = lax.broadcasted_iota(jnp.int32, (forks, answers[0].shape[0]), 1)
     picking = (at == target_ref[...]).astype(jnp.bfloat16)
-
-    def pick(start, size):
-        return jnp.dot(
-            picking, answer_ref[:, start : start + size], preferred_element_type=jnp.float32
-        )
-
-    begin = 0
-
-    for lead, count in PARTS:
+    for (lead, count), answer in zip(PARTS, answers, strict=True):
         run = 2 * count
-        come = pick(begin + run * SPLIT * V, 2 * LANES)
-        mass = come[:, :LANES] + come[:, LANES:]
+        come = jnp.dot(picking, answer[...], preferred_element_type=jnp.float32)
+        masses = come[:, run * SPLIT * V :]
+        mass = masses[:, :LANES] + masses[:, LANES:]
         for n in range(SPLIT):
             first = n * group_heads + 2 * lead
             mass_prefix = mass[:, n * run : (n + 1) * run]
@@ -283,24 +270,22 @@
             both = share_prefix + share_suffix
             part_prefix = share_prefix / both
             part_suffix = share_suffix / both
-            value = pick(begin + n * run * V, run * V)
             for h in range(run):
                 cut = slice((first + h) * V, (first + h + 1) * V)
+                come_at = (n * run + h) * V
                 out_ref[:, cut] = (
-                    part_prefix[:, h : h + 1] * value[:, h * V : (h + 1) * V]
+                    part_prefix[:, h : h + 1] * come[:, come_at : come_at + V]
                     + part_suffix[:, h : h + 1] * value_ref[:, cut].astype(jnp.float32)
                 ).astype(out_ref.dtype)
-        begin += run * SPLIT * V + 2 * LANES
-
-
-def merge(target, answer, value_suffix, mass_suffix):
-    forks = value_suffix.shape[0]
+
+
+def merge(target, answers, value_suffix, mass_suffix):
     return pl.pallas_call(
         merge_kernel,
-        out_shape=jax.ShapeDtypeStruct((forks, value_suffix.shape[1]), jnp.bfloat16),
+        out_shape=jax.ShapeDtypeStruct(value_suffix.shape, jnp.bfloat16),
         compiler_params=pltpu.CompilerParams(vmem_limit_bytes=24 << 20),
         name="merge",
-    )(target, answer, value_suffix, mass_suffix)
+    )(target, *answers, value_suffix, mass_suffix)
 
 
 def suffix(queries, suffix_cache, suffix_len, w_uv):
@@ -359,10 +344,13 @@
         (outbound[1], value_suffix, mass_suffix)
     )
     received.append(exchange(outbound[1]))
-    result = prefix(received[0], caches, w_uv, PARTS[0])
-    result = prefix(received[1], caches, w_uv, PARTS[1], result)
-    answer = exchange(result).reshape(result.shape)
-    return merge(targets[0], answer, value_suffix, mass_suffix)
+    results = [prefix(received[0], caches, w_uv, PARTS[0])]
+    received[1], results[0] = lax.optimization_barrier((received[1], results[0]))
+    answers = [exchange(results[0]).reshape(results[0].shape)]
+    results.append(prefix(received[1], caches, w_uv, PARTS[1]))
+    results[1], answers[0] = lax.optimization_barrier((results[1], answers[0]))
+    answers.append(exchange(results[1]).reshape(results[1].shape))
+    return merge(targets[0], answers, value_suffix, mass_suffix)
 
 
 def solution(mesh):

time: 160 us -> 158 us (0.988)
  blocking collectives: 24.9 us -> 17 us
  starting transfers between devices: 27.9 us -> 35.4 us
  local copies, waits for them, and re-layouts: 8.65 us -> 6.62 us
    all_to_all x1, blocking collectives: 24.9 us -> 17 us  [exchange(): lax.all_to_all(value.reshape(group, -1, value.shape[1]), near, split_axis...]
    all_to_all x2 -> x3, starting transfers between devices: 13.2 us -> 20.7 us  [exchange(): lax.all_to_all(value.reshape(group, -1, value.shape[1]), near, split_axis...]
    unnamed x17 -> x15, local copies, waits for them, and re-layouts: 4.42 us -> 2.37 us
    all_to_all x2 -> x3, waiting for transfers between devices: 4.33 us -> 4.97 us  [exchange(): lax.all_to_all(value.reshape(group, -1, value.shape[1]), near, split_axis...]
  transfers between devices with their start and end apart: 7 -> 8, of which waited for: 6 -> 6; matrix products, arithmetic and copies ran while one was open for 15% -> 15% of each run, Pallas kernels for 12% -> 19%
where the time goes in v6:
time: 158 us
  starting transfers between devices  35.4 us (22%)
  waiting for transfers between devices  34.7 us (22%)
  Pallas kernels  32.6 us (21%)
  blocking collectives  17 us (11%)
  matrix products  14.7 us (9%)
  between operations  13.5 us (9%)
  local copies, waits for them, and re-layouts  6.62 us (4%)
  other arithmetic  3.1 us (2%)
    pallas_call x2, Pallas kernels, prefix(): pl.pallas_call(functools.partial(prefix_kernel, part), out_shape=jax.Shap...  21.9 us
    all_to_all x3, starting transfers between devices, exchange(): lax.all_to_all(value.reshape(group, -1, value.shape[1]), near, split_axis...  20.7 us
    all_gather x1, waiting for transfers between devices, shards(): lax.all_gather(jnp.stack(held_here, axis=1), 'tp', axis=0, tiled=True)  19.7 us
    all_to_all x1, blocking collectives, exchange(): lax.all_to_all(value.reshape(group, -1, value.shape[1]), near, split_axis...  17 us
    ppermute x4, starting transfers between devices, along(): lax.ppermute(value, 'zh', [(n, (n + steps) % COPIES) for n in range(COPIE...  14.4 us
    ppermute x4, waiting for transfers between devices, along(): lax.ppermute(value, 'zh', [(n, (n + steps) % COPIES) for n in range(COPIE...  10 us
    pallas_call x2, Pallas kernels, place(): pl.pallas_call(place_kernel, out_shape=(jax.ShapeDtypeStruct((rows, mine...  7.83 us
    dot_general x1, matrix products, suffix(): jnp.einsum('fhs,frs->fhr', weights.astype(jnp.bfloat16), suffix_cache[:,...  7.34 us
  transfers between devices with their start and end apart: 8, of which 6 were waited for; matrix products, arithmetic and copies ran while one was open for 15% of the time, Pallas kernels for 19%

profile of v6, /device:TPU:1, one launch (start us, length us, event | category | flops | bytes accessed | tf_op | source)
XLA Modules:
  0.0 157.6 jit_solution(2036101668142648693)
XLA Ops:
  6.5 3.8 %collective-permute-start = (bf16[1,576,256]{2,1,0:T(8,128)(2,1)}, bf16[1,576,256]{2,1,0:T(8,128)(2,1)S(1)}, u32[]{:S(2)}, u32[]{:S(2)}) collective-permute-start(bf16[1,576,256]{2,1,0:T(8,128)(2,1)} %param.8), channel_id=1, source_target_pairs={{0,64},{64,128},{128,192},{192,0},{1,65},{65,129},{129,193},{193,1... | collective-permute-start | bytes 884744 | tf_op jit(solution)/shard_map/ppermute | solution.py:324
  10.4 3.0 %collective-permute-start.1 = (bf16[1,576,256]{2,1,0:T(8,128)(2,1)}, bf16[1,576,256]{2,1,0:T(8,128)(2,1)S(1)}, u32[]{:S(2)}, u32[]{:S(2)}) collective-permute-start(bf16[1,576,256]{2,1,0:T(8,128)(2,1)} %param.8), channel_id=1, source_target_pairs={{0,192},{64,0},{128,64},{192,128},{1,193},{65,1},{129,65},{193,129... | collective-permute-start | bytes 884744 | tf_op jit(solution)/shard_map/ppermute | solution.py:324
  13.4 1.4 copy.12.prompt_ref
  14.7 7.6 %collective-permute-done = bf16[1,576,256]{2,1,0:T(8,128)(2,1)S(1)} collective-permute-done((bf16[1,576,256]{2,1,0:T(8,128)(2,1)}, bf16[1,576,256]{2,1,0:T(8,128)(2,1)S(1)}, u32[]{:S(2)}, u32[]{:S(2)}) %collective-permute-start) | collective-permute-done | bytes 294944 | tf_op jit(solution)/shard_map/ppermute | solution.py:324
  22.3 5.1 %collective-permute-start.2 = (bf16[1,288,256]{2,1,0:T(8,128)(2,1)S(1)}, bf16[1,288,256]{2,1,0:T(8,128)(2,1)S(1)}, u32[]{:S(2)}, u32[]{:S(2)}) collective-permute-start(bf16[1,288,256]{2,1,0:T(8,128)(2,1)S(1)} %slice.12), channel_id=1, source_target_pairs={{0,64},{64,128},{128,192},{192,0},{1,65},{65,129},{129,193},{193,1... | collective-permute-start | bytes 442376 | tf_op jit(solution)/shard_map/ppermute | solution.py:324
  27.4 0.7 collective-permute-done.1
  28.1 2.4 %collective-permute-start.3 = (bf16[1,288,256]{2,1,0:T(8,128)(2,1)S(1)}, bf16[1,288,256]{2,1,0:T(8,128)(2,1)S(1)}, u32[]{:S(2)}, u32[]{:S(2)}) collective-permute-start(bf16[1,288,256]{2,1,0:T(8,128)(2,1)S(1)} %slice.13), channel_id=1, source_target_pairs={{0,192},{64,0},{128,64},{192,128},{1,193},{65,1},{129,65},{193,129... | collective-permute-start | bytes 442376 | tf_op jit(solution)/shard_map/ppermute | solution.py:324
  30.6 1.2 fusion.22.base_ref
  31.7 3.8 %place.2 = (bf16[512,2304]{1,0:T(8,128)(2,1)}, s32[64,1]{1,0:T(8,128)}) custom-call(s32[64,1]{1,0:T(8,128)} %copy.12.prompt_ref, s32[1,64]{1,0:T(1,128)} %fusion.22.base_ref, bf16[64,18432]{1,0:T(8,128)(2,1)} %refs_3_.3, bf16[64,18432]{1,0:T(8,128)(2,1)} %refs_3_.3, bf16[64,18432]{1,0:T(8,128)(2,1)} %refs_3_.3, bf16[64,18432]{1,0:T(8,128)(2,1)} %refs_3_.3), custom_call_target="tpu_custom_call" | custom-call | tf_op jit(solution)/shard_map/place/pallas_call | solution.py:75
  35.6 0.0 copy-start.4
  35.6 0.0 collective-permute-done.2
  35.6 1.8 %collective-permute-done.3 = bf16[1,288,256]{2,1,0:T(8,128)(2,1)S(1)} collective-permute-done((bf16[1,288,256]{2,1,0:T(8,128)(2,1)S(1)}, bf16[1,288,256]{2,1,0:T(8,128)(2,1)S(1)}, u32[]{:S(2)}, u32[]{:S(2)}) %collective-permute-start.3) | collective-permute-done | bytes 147488 | tf_op jit(solution)/shard_map/ppermute | solution.py:324
  37.3 0.0 copy-start.1
  37.3 5.8 %all-to-all-start.1 = ((bf16[16,32,2304]{2,1,0:T(8,128)(2,1)}), bf16[16,32,2304]{2,1,0:T(8,128)(2,1)}, u32[]{:S(2)}, u32[]{:S(2)}) async-start(bf16[16,32,2304]{2,1,0:T(8,128)(2,1)} %bitcast.25), calls=%async_computation.1 | async-start | bytes 4718592 | tf_op jit(solution)/shard_map/all_to_all | solution.py:327
  43.1 0.2 all-gather.2.cloned.1.call-start
  43.4 0.0 copy-done.4
  43.4 1.2 pad_maximum_fusion
  44.5 0.0 all-gather.2.cloned.1.call-update
  44.6 0.0 copy-done.1
  44.6 4.1 %reshape.43 = bf16[64,32,576]{2,1,0:T(8,128)(2,1)} reshape(bf16[64,18432]{1,0:T(8,128)(2,1)S(1)} %copy-done.1) | data formatting | bytes 4718592 | tf_op jit(solution)/shard_map/reshape | solution.py:294
  48.6 0.0 copy-start.5
  48.6 0.0 copy-start.2
  48.6 4.0 %place.3 = (bf16[512,2304]{1,0:T(8,128)(2,1)}, s32[64,1]{1,0:T(8,128)}) custom-call(s32[64,1]{1,0:T(8,128)} %copy.12.prompt_ref, s32[1,64]{1,0:T(1,128)} %fusion.22.base_ref, bf16[64,18432]{1,0:T(8,128)(2,1)} %refs_3_.3, bf16[64,18432]{1,0:T(8,128)(2,1)} %refs_3_.3, bf16[64,18432]{1,0:T(8,128)(2,1)} %refs_3_.3, bf16[64,18432]{1,0:T(8,128)(2,1)} %refs_3_.3), custom_call_target="tpu_custom_call" | custom-call | tf_op jit(solution)/shard_map/place/pallas_call | solution.py:75
  52.7 0.0 copy-done.5
  52.7 0.1 iota_compare_fusion
  52.7 0.0 copy-done.2
  52.7 4.7 %fusion.24 = (f32[64,32]{1,0:T(8,128)S(1)}, f32[64,32,128]{2,1,0:T(8,128)S(1)}) fusion(bf16[64,32,576]{2,1,0:T(8,128)(2,1)S(1)} %copy-done.2, bf16[64,576,128]{2,1,0:T(8,128)(2,1)} %param.9, pred[64,128]{1,0:T(8,128)(4,1)S(1)} %iota_compare_fusion), kind=kOutput, calls=%fused_computation.34 | convolution fusion | flops 302774272 | bytes 12861440 | tf_op jit(solution)/shard_map/fhe,fes->fhs/dot_general | solution.py:296
  57.5 0.0 copy-start.3
  57.5 1.0 copy-done.3
  58.5 0.6 fusion.12
  59.1 0.1 copy.14
  59.2 0.0 copy-start.6
  59.2 7.3 %fusion = f32[64,32,512]{2,1,0:T(8,128)S(1)} fusion(bf16[64,576,128]{2,1,0:T(8,128)(2,1)} %param.9, f32[64,32,128]{2,1,0:T(8,128)} %copy-done.3, f32[64,32]{1,0:T(8,128)S(1)} %get-tuple-element.35, pred[64,128]{1,0:T(8,128)(4,1)S(1)} %iota_compare_fusion), kind=kOutput, calls=%fused_computation | convolution fusion | flops 269221888 | bytes 13647872 | tf_op jit(solution)/shard_map/fhs,frs->fhr/dot_general | solution.py:305
  66.5 0.0 copy-done.6
  66.6 2.6 %fusion.9 = bf16[32,8,8,128]{3,2,1,0:T(8,128)(2,1)S(1)} fusion(bf16[32,512,128]{2,1,0:T(8,128)(2,1)S(1)} %copy-done.6, f32[64,32,512]{2,1,0:T(8,128)S(1)} %fusion, f32[64,32]{0,1:T(8,128)S(1)} %copy.14), kind=kOutput, calls=%fused_computation.8 | convolution fusion | flops 270794752 | bytes 8921088 | tf_op jit(solution)/shard_map/nhr,hrv->nhv/dot_general | solution.py:312
  69.1 0.1 copy.27
  69.3 4.7 %all-to-all-done.1.q_ref = bf16[16,32,2304]{2,1,0:T(8,128)(2,1)} async-done(((bf16[16,32,2304]{2,1,0:T(8,128)(2,1)}), bf16[16,32,2304]{2,1,0:T(8,128)(2,1)}, u32[]{:S(2)}, u32[]{:S(2)}) %all-to-all-start.1) | async-done | bytes 2359328 | tf_op jit(solution)/shard_map/all_to_all | solution.py:327
  74.0 7.5 %all-to-all-start = ((bf16[16,32,2304]{2,1,0:T(8,128)(2,1)}), bf16[16,32,2304]{2,1,0:T(8,128)(2,1)}, u32[]{:S(2)}, u32[]{:S(2)}) async-start(bf16[16,32,2304]{2,1,0:T(8,128)(2,1)} %bitcast.26), calls=%async_computation | async-start | bytes 4718592 | tf_op jit(solution)/shard_map/all_to_all | solution.py:327
  81.5 19.7 %all-gather.2.cloned.1.call-done.kv_ref = bf16[4,4,576,256]{3,2,1,0:T(8,128)(2,1)} async-done(((bf16[1,4,576,256]{3,2,1,0:T(8,128)(2,1)}), bf16[4,4,576,256]{3,2,1,0:T(8,128)(2,1)}) %all-gather.2.cloned.1.call-update) | async-done | bytes 4718608 | tf_op jit(solution)/shard_map/all_gather | solution.py:340
  101.2 11.0 %prefix.2 = bf16[128,2304]{1,0:T(8,128)(2,1)} custom-call(bf16[16,32,2304]{2,1,0:T(8,128)(2,1)} %all-to-all-done.1.q_ref, bf16[4,4,576,256]{3,2,1,0:T(8,128)(2,1)} %all-gather.2.cloned.1.call-done.kv_ref, bf16[32,512,128]{2,1,0:T(8,128)(2,1)} %w_hbm.3), custom_call_target="tpu_custom_call" | custom-call | flops 4831838208 | bytes 9764864 | tf_op jit(solution)/shard_map/prefix/pallas_call | solution.py:222
  112.2 0.2 all-to-all-done.q_ref
  112.4 7.5 %all-to-all-start.2 = ((bf16[16,8,2304]{2,1,0:T(8,128)(2,1)}), bf16[16,8,2304]{2,1,0:T(8,128)(2,1)S(1)}, u32[]{:S(2)}, u32[]{:S(2)}) async-start(bf16[16,8,2304]{2,1,0:T(8,128)(2,1)} %bitcast.29), calls=%async_computation.2 | async-start | bytes 1179648 | tf_op jit(solution)/shard_map/all_to_all | solution.py:327
  119.9 0.0 copy-start
  119.9 11.0 %prefix.3 = bf16[128,2304]{1,0:T(8,128)(2,1)} custom-call(bf16[16,32,2304]{2,1,0:T(8,128)(2,1)} %all-to-all-done.q_ref, bf16[4,4,576,256]{3,2,1,0:T(8,128)(2,1)} %all-gather.2.cloned.1.call-done.kv_ref, bf16[32,512,128]{2,1,0:T(8,128)(2,1)} %w_hbm.3), custom_call_target="tpu_custom_call" | custom-call | flops 4831838208 | bytes 9764864 | tf_op jit(solution)/shard_map/prefix/pallas_call | solution.py:222
  130.9 0.0 all-to-all-done.2
  130.9 17.0 %all_to_all.20 = bf16[16,8,2304]{2,1,0:T(8,128)(2,1)S(1)} all-to-all(bf16[16,8,2304]{2,1,0:T(8,128)(2,1)} %bitcast.30), channel_id=1, replica_groups=mesh['zh'=4,'zl'=2,'xc'=8,'tp'=4] {'zl','xc'}, dimensions={0} | all-to-all | bytes 1179648 | tf_op jit(solution)/shard_map/all_to_all | solution.py:327
  147.9 0.0 copy-done
  147.9 2.9 %merge.1 = bf16[64,4096]{1,0:T(8,128)(2,1)} custom-call(s32[64,1]{1,0:T(8,128)S(1)} %copy-done, bf16[128,2304]{1,0:T(8,128)(2,1)S(1)} %bitcast.22, bf16[128,2304]{1,0:T(8,128)(2,1)S(1)} %bitcast.23, bf16[64,4096]{1,0:T(8,128)(2,1)S(1)} %bitcast.24, f32[64,32]{1,0:T(8,128)S(1)} %log_add_fusion.refs_3_), custom_call_target="tpu_custom_call" | custom-call | tf_op jit(solution)/shard_map/merge/pallas_call | solution.py:283
  (4 shorter events, 0.1 us)
Async XLA Ops:
  6.5 15.8 %collective-permute-start = (bf16[1,576,256]{2,1,0:T(8,128)(2,1)}, bf16[1,576,256]{2,1,0:T(8,128)(2,1)S(1)}, u32[]{:S(2)}, u32[]{:S(2)}) collective-permute-start(bf16[1,576,256]{2,1,0:T(8,128)(2,1)} %param.8), channel_id=1, source_target_pairs={{0,64},{64,128},{128,192},{192,0},{1,65},{65,129},{129,193},{193,1... | collective-permute-start | bytes 884744 | tf_op jit(solution)/shard_map/ppermute | solution.py:324
  10.4 17.8 %collective-permute-start.1 = (bf16[1,576,256]{2,1,0:T(8,128)(2,1)}, bf16[1,576,256]{2,1,0:T(8,128)(2,1)S(1)}, u32[]{:S(2)}, u32[]{:S(2)}) collective-permute-start(bf16[1,576,256]{2,1,0:T(8,128)(2,1)} %param.8), channel_id=1, source_target_pairs={{0,192},{64,0},{128,64},{192,128},{1,193},{65,1},{129,65},{193,129... | collective-permute-start | bytes 884744 | tf_op jit(solution)/shard_map/ppermute | solution.py:324
  22.3 13.2 %collective-permute-start.2 = (bf16[1,288,256]{2,1,0:T(8,128)(2,1)S(1)}, bf16[1,288,256]{2,1,0:T(8,128)(2,1)S(1)}, u32[]{:S(2)}, u32[]{:S(2)}) collective-permute-start(bf16[1,288,256]{2,1,0:T(8,128)(2,1)S(1)} %slice.12), channel_id=1, source_target_pairs={{0,64},{64,128},{128,192},{192,0},{1,65},{65,129},{129,193},{193,1... | collective-permute-start | bytes 442376 | tf_op jit(solution)/shard_map/ppermute | solution.py:324
  28.1 9.2 %collective-permute-start.3 = (bf16[1,288,256]{2,1,0:T(8,128)(2,1)S(1)}, bf16[1,288,256]{2,1,0:T(8,128)(2,1)S(1)}, u32[]{:S(2)}, u32[]{:S(2)}) collective-permute-start(bf16[1,288,256]{2,1,0:T(8,128)(2,1)S(1)} %slice.13), channel_id=1, source_target_pairs={{0,192},{64,0},{128,64},{192,128},{1,193},{65,1},{129,65},{193,129... | collective-permute-start | bytes 442376 | tf_op jit(solution)/shard_map/ppermute | solution.py:324
  35.6 7.8 %copy-start.4 = (bf16[1,576,256]{2,1,0:T(8,128)(2,1)S(1)}, bf16[1,576,256]{2,1,0:T(8,128)(2,1)}, u32[]{:S(2)}) copy-start(bf16[1,576,256]{2,1,0:T(8,128)(2,1)} %param.8) | copy-start | bytes 884740
  37.3 7.2 %copy-start.1 = (bf16[64,18432]{1,0:T(8,128)(2,1)S(1)}, bf16[64,18432]{1,0:T(8,128)(2,1)}, u32[]{:S(2)}) copy-start(bf16[64,18432]{1,0:T(8,128)(2,1)} %refs_3_.3) | copy-start | bytes 7077892
  37.3 36.7 %all-to-all-start.1 = ((bf16[16,32,2304]{2,1,0:T(8,128)(2,1)}), bf16[16,32,2304]{2,1,0:T(8,128)(2,1)}, u32[]{:S(2)}, u32[]{:S(2)}) async-start(bf16[16,32,2304]{2,1,0:T(8,128)(2,1)} %bitcast.25), calls=%async_computation.1 | async-start | bytes 4718592 | tf_op jit(solution)/shard_map/all_to_all | solution.py:327
  43.1 58.1 %all-gather.2.cloned.1.call-start = ((), (), s32[]{:S(2)}) async-start(), calls=%async_computation.4 | async-start | bytes 5898240 | tf_op jit(solution)/shard_map/all_gather | solution.py:340
  48.6 4.0 %copy-start.5 = (s32[64]{0:T(128)S(1)}, s32[64]{0:T(128)}, u32[]{:S(2)}) copy-start(s32[64]{0:T(128)} %param.13) | copy-start | bytes 772
  48.6 4.1 %copy-start.2 = (bf16[64,32,576]{2,1,0:T(8,128)(2,1)S(1)}, bf16[64,32,576]{2,1,0:T(8,128)(2,1)}, u32[]{:S(2)}) copy-start(bf16[64,32,576]{2,1,0:T(8,128)(2,1)} %reshape.43) | copy-start | bytes 7077892
  57.5 1.0 copy-start.3
  59.2 7.3 %copy-start.6 = (bf16[32,512,128]{2,1,0:T(8,128)(2,1)S(1)}, bf16[32,512,128]{2,1,0:T(8,128)(2,1)}, u32[]{:S(2)}) copy-start(bf16[32,512,128]{2,1,0:T(8,128)(2,1)} %w_hbm.3) | copy-start | bytes 12582916
  74.0 38.4 %all-to-all-start = ((bf16[16,32,2304]{2,1,0:T(8,128)(2,1)}), bf16[16,32,2304]{2,1,0:T(8,128)(2,1)}, u32[]{:S(2)}, u32[]{:S(2)}) async-start(bf16[16,32,2304]{2,1,0:T(8,128)(2,1)} %bitcast.26), calls=%async_computation | async-start | bytes 4718592 | tf_op jit(solution)/shard_map/all_to_all | solution.py:327
  112.4 18.5 %all-to-all-start.2 = ((bf16[16,8,2304]{2,1,0:T(8,128)(2,1)}), bf16[16,8,2304]{2,1,0:T(8,128)(2,1)S(1)}, u32[]{:S(2)}, u32[]{:S(2)}) async-start(bf16[16,8,2304]{2,1,0:T(8,128)(2,1)} %bitcast.29), calls=%async_computation.2 | async-start | bytes 1179648 | tf_op jit(solution)/shard_map/all_to_all | solution.py:327
  119.9 28.0 %copy-start = (s32[64,1]{1,0:T(8,128)S(1)}, s32[64,1]{1,0:T(8,128)}, u32[]{:S(2)}) copy-start(s32[64,1]{1,0:T(8,128)} %get-tuple-element.20.target_ref) | copy-start | bytes 772
Sparse Core Ops, SparseCore 0:
  45.7 55.4 all-gather.1

commit v7 on v6

--- a/solution.py
+++ b/solution.py
@@ -208,7 +208,9 @@
             put(head * V, jnp.concatenate(both, axis=1).astype(jnp.bfloat16))
         high = mass_ref[...].astype(jnp.bfloat16)
         low = (mass_ref[...] - high.astype(jnp.float32)).astype(jnp.bfloat16)
-        put(heads * V, jnp.concatenate([high, low], axis=1))
+        spot = lax.broadcasted_iota(jnp.int32, mass_ref.shape, 1)
+        moved = pltpu.roll(low.astype(jnp.float32), LANES // 2, 1)
+        put(heads * V, jnp.where(spot < LANES // 2, high.astype(jnp.float32), moved).astype(jnp.bfloat16))
 
 
 def prefix(received, caches, w_uv, part):
@@ -218,7 +220,7 @@
     tall = group * MOST * SPLIT
     parts = caches.shape[0]
     length = parts * caches.shape[3]
-    wide = heads * V + 2 * LANES
+    wide = heads * V + LANES
     return pl.pallas_call(
         functools.partial(prefix_kernel, part),
         out_shape=jax.ShapeDtypeStruct((rows, wide), jnp.bfloat16),
@@ -255,28 +257,28 @@
     group_heads = heads // SPLIT
     at = lax.broadcasted_iota(jnp.int32, (forks, answers[0].shape[0]), 1)
     picking = (at == target_ref[...]).astype(jnp.bfloat16)
+    done = 0
     for (lead, count), answer in zip(PARTS, answers, strict=True):
         run = 2 * count
+        mine = run * SPLIT
         come = jnp.dot(picking, answer[...], preferred_element_type=jnp.float32)
-        masses = come[:, run * SPLIT * V :]
-        mass = masses[:, :LANES] + masses[:, LANES:]
-        for n in range(SPLIT):
-            first = n * group_heads + 2 * lead
-            mass_prefix = mass[:, n * run : (n + 1) * run]
-            mass_suffix = mass_ref[:, first : first + run]
-            top = jnp.maximum(mass_prefix, mass_suffix)
-            share_prefix = jnp.exp(mass_prefix - top)
-            share_suffix = jnp.exp(mass_suffix - top)
-            both = share_prefix + share_suffix
-            part_prefix = share_prefix / both
-            part_suffix = share_suffix / both
-            for h in range(run):
-                cut = slice((first + h) * V, (first + h + 1) * V)
-                come_at = (n * run + h) * V
-                out_ref[:, cut] = (
-                    part_prefix[:, h : h + 1] * come[:, come_at : come_at + V]
-                    + part_suffix[:, h : h + 1] * value_ref[:, cut].astype(jnp.float32)
-                ).astype(out_ref.dtype)
+        masses = come[:, mine * V :]
+        mass_prefix = masses[:, :mine] + masses[:, LANES // 2 : LANES // 2 + mine]
+        mass_suffix = mass_ref[:, done : done + mine]
+        done += mine
+        top = jnp.maximum(mass_prefix, mass_suffix)
+        share_prefix = jnp.exp(mass_prefix - top)
+        share_suffix = jnp.exp(mass_suffix - top)
+        both = share_prefix + share_suffix
+        part_prefix = share_prefix / both
+        part_suffix = share_suffix / both
+        for h in range(mine):
+            head = h // run * group_heads + 2 * lead + h % run
+            cut = slice(head * V, (head + 1) * V)
+            out_ref[:, cut] = (
+                part_prefix[:, h : h + 1] * come[:, h * V : (h + 1) * V]
+                + part_suffix[:, h : h + 1] * value_ref[:, cut].astype(jnp.float32)
+            ).astype(out_ref.dtype)
 
 
 def merge(target, answers, value_suffix, mass_suffix):
@@ -339,6 +341,14 @@
     held_here = [prefix_cache, behind, jnp.concatenate(across, axis=1), before]
     caches = lax.all_gather(jnp.stack(held_here, axis=1), "tp", axis=0, tiled=True)
     value_suffix, mass_suffix = suffix(queries, suffix_cache, suffix_len, w_uv)
+    grouped = mass_suffix.reshape(mass_suffix.shape[0], SPLIT, -1)
+    mass_suffix = jnp.concatenate(
+        [
+            grouped[:, :, 2 * lead : 2 * (lead + count)].reshape(mass_suffix.shape[0], -1)
+            for lead, count in PARTS
+        ],
+        axis=1,
+    )
     received = [exchange(outbound[0])]
     outbound[1], value_suffix, mass_suffix = lax.optimization_barrier(
         (outbound[1], value_suffix, mass_suffix)

time: 158 us -> 157 us (level)
  matrix products: 14.7 us -> 12.4 us
  waiting for transfers between devices: 34.7 us -> 36.9 us
    dot_general x1, matrix products: 7.34 us -> 3.52 us  [suffix(): jnp.einsum('fhs,frs->fhr', weights.astype(jnp.bfloat16), suffix_cache[:,...]
    all_to_all x3, waiting for transfers between devices: 4.97 us -> 7.26 us  [exchange(): lax.all_to_all(value.reshape(group, -1, value.shape[1]), near, split_axis...]
    dot_general x1, matrix products: 4.74 us -> 6.34 us  [suffix(): jnp.einsum('fhe,fes->fhs', query_heads, suffix_cache, preferred_element_t...]
  transfers between devices with their start and end apart: 8 -> 8, of which waited for: 6 -> 6; matrix products, arithmetic and copies ran while one was open for 15% -> 14% of each run, Pallas kernels for 19% -> 19%
where the time goes in v7:
time: 157 us
  waiting for transfers between devices  36.9 us (24%)
  starting transfers between devices  35.4 us (23%)
  Pallas kernels  31.8 us (20%)
  blocking collectives  16.8 us (11%)
  between operations  13.6 us (9%)
  matrix products  12.4 us (8%)
  local copies, waits for them, and re-layouts  6.48 us (4%)
  other arithmetic  3.27 us (2%)
    pallas_call x2, Pallas kernels, prefix(): pl.pallas_call(functools.partial(prefix_kernel, part), out_shape=jax.Shap...  21.9 us
    all_to_all x3, starting transfers between devices, exchange(): lax.all_to_all(value.reshape(group, -1, value.shape[1]), near, split_axis...  20.8 us
    all_gather x1, waiting for transfers between devices, shards(): lax.all_gather(jnp.stack(held_here, axis=1), 'tp', axis=0, tiled=True)  19.7 us
    all_to_all x1, blocking collectives, exchange(): lax.all_to_all(value.reshape(group, -1, value.shape[1]), near, split_axis...  16.8 us
    ppermute x4, starting transfers between devices, along(): lax.ppermute(value, 'zh', [(n, (n + steps) % COPIES) for n in range(COPIE...  14.4 us
    ppermute x4, waiting for transfers between devices, along(): lax.ppermute(value, 'zh', [(n, (n + steps) % COPIES) for n in range(COPIE...  9.95 us
    pallas_call x2, Pallas kernels, place(): pl.pallas_call(place_kernel, out_shape=(jax.ShapeDtypeStruct((rows, mine...  7.84 us
    all_to_all x3, waiting for transfers between devices, exchange(): lax.all_to_all(value.reshape(group, -1, value.shape[1]), near, split_axis...  7.26 us
  transfers between devices with their start and end apart: 8, of which 6 were waited for; matrix products, arithmetic and copies ran while one was open for 14% of the time, Pallas kernels for 19%

profile of v7, /device:TPU:1, one launch (start us, length us, event | category | flops | bytes accessed | tf_op | source)
XLA Modules:
  0.0 156.6 jit_solution(17320203828365218924)
XLA Ops:
  6.5 3.8 %collective-permute-start = (bf16[1,576,256]{2,1,0:T(8,128)(2,1)}, bf16[1,576,256]{2,1,0:T(8,128)(2,1)S(1)}, u32[]{:S(2)}, u32[]{:S(2)}) collective-permute-start(bf16[1,576,256]{2,1,0:T(8,128)(2,1)} %param.8), channel_id=1, source_target_pairs={{0,64},{64,128},{128,192},{192,0},{1,65},{65,129},{129,193},{193,1... | collective-permute-start | bytes 884744 | tf_op jit(solution)/shard_map/ppermute | solution.py:326
  10.4 3.0 %collective-permute-start.1 = (bf16[1,576,256]{2,1,0:T(8,128)(2,1)}, bf16[1,576,256]{2,1,0:T(8,128)(2,1)S(1)}, u32[]{:S(2)}, u32[]{:S(2)}) collective-permute-start(bf16[1,576,256]{2,1,0:T(8,128)(2,1)} %param.8), channel_id=1, source_target_pairs={{0,192},{64,0},{128,64},{192,128},{1,193},{65,1},{129,65},{193,129... | collective-permute-start | bytes 884744 | tf_op jit(solution)/shard_map/ppermute | solution.py:326
  13.4 1.4 copy.18.prompt_ref
  14.7 7.6 %collective-permute-done = bf16[1,576,256]{2,1,0:T(8,128)(2,1)S(1)} collective-permute-done((bf16[1,576,256]{2,1,0:T(8,128)(2,1)}, bf16[1,576,256]{2,1,0:T(8,128)(2,1)S(1)}, u32[]{:S(2)}, u32[]{:S(2)}) %collective-permute-start) | collective-permute-done | bytes 294944 | tf_op jit(solution)/shard_map/ppermute | solution.py:326
  22.3 5.1 %collective-permute-start.2 = (bf16[1,288,256]{2,1,0:T(8,128)(2,1)S(1)}, bf16[1,288,256]{2,1,0:T(8,128)(2,1)S(1)}, u32[]{:S(2)}, u32[]{:S(2)}) collective-permute-start(bf16[1,288,256]{2,1,0:T(8,128)(2,1)S(1)} %slice.22), channel_id=1, source_target_pairs={{0,64},{64,128},{128,192},{192,0},{1,65},{65,129},{129,193},{193,1... | collective-permute-start | bytes 442376 | tf_op jit(solution)/shard_map/ppermute | solution.py:326
  27.4 0.7 collective-permute-done.1
  28.1 2.4 %collective-permute-start.3 = (bf16[1,288,256]{2,1,0:T(8,128)(2,1)S(1)}, bf16[1,288,256]{2,1,0:T(8,128)(2,1)S(1)}, u32[]{:S(2)}, u32[]{:S(2)}) collective-permute-start(bf16[1,288,256]{2,1,0:T(8,128)(2,1)S(1)} %slice.23), channel_id=1, source_target_pairs={{0,192},{64,0},{128,64},{192,128},{1,193},{65,1},{129,65},{193,129... | collective-permute-start | bytes 442376 | tf_op jit(solution)/shard_map/ppermute | solution.py:326
  30.6 1.2 fusion.23.base_ref
  31.8 3.8 %place.2 = (bf16[512,2304]{1,0:T(8,128)(2,1)}, s32[64,1]{1,0:T(8,128)}) custom-call(s32[64,1]{1,0:T(8,128)} %copy.18.prompt_ref, s32[1,64]{1,0:T(1,128)} %fusion.23.base_ref, bf16[64,18432]{1,0:T(8,128)(2,1)} %refs_3_.3, bf16[64,18432]{1,0:T(8,128)(2,1)} %refs_3_.3, bf16[64,18432]{1,0:T(8,128)(2,1)} %refs_3_.3, bf16[64,18432]{1,0:T(8,128)(2,1)} %refs_3_.3), custom_call_target="tpu_custom_call" | custom-call | tf_op jit(solution)/shard_map/place/pallas_call | solution.py:75
  35.6 0.0 collective-permute-done.2
  35.6 1.7 %collective-permute-done.3 = bf16[1,288,256]{2,1,0:T(8,128)(2,1)S(1)} collective-permute-done((bf16[1,288,256]{2,1,0:T(8,128)(2,1)S(1)}, bf16[1,288,256]{2,1,0:T(8,128)(2,1)S(1)}, u32[]{:S(2)}, u32[]{:S(2)}) %collective-permute-start.3) | collective-permute-done | bytes 147488 | tf_op jit(solution)/shard_map/ppermute | solution.py:326
  37.3 0.0 copy-start.3
  37.3 5.8 %all-to-all-start.1 = ((bf16[16,32,2304]{2,1,0:T(8,128)(2,1)}), bf16[16,32,2304]{2,1,0:T(8,128)(2,1)}, u32[]{:S(2)}, u32[]{:S(2)}) async-start(bf16[16,32,2304]{2,1,0:T(8,128)(2,1)} %bitcast.30), calls=%async_computation.1 | async-start | bytes 4718592 | tf_op jit(solution)/shard_map/all_to_all | solution.py:329
  43.1 0.2 all-gather.2.cloned.1.call-start
  43.4 0.0 copy-done.3
  43.4 1.2 pad_maximum_fusion
  44.5 0.0 all-gather.2.cloned.1.call-update
  44.6 0.0 copy-start.1
  44.6 4.0 %place.3 = (bf16[512,2304]{1,0:T(8,128)(2,1)}, s32[64,1]{1,0:T(8,128)}) custom-call(s32[64,1]{1,0:T(8,128)} %copy.18.prompt_ref, s32[1,64]{1,0:T(1,128)} %fusion.23.base_ref, bf16[64,18432]{1,0:T(8,128)(2,1)} %refs_3_.3, bf16[64,18432]{1,0:T(8,128)(2,1)} %refs_3_.3, bf16[64,18432]{1,0:T(8,128)(2,1)} %refs_3_.3, bf16[64,18432]{1,0:T(8,128)(2,1)} %refs_3_.3), custom_call_target="tpu_custom_call" | custom-call | tf_op jit(solution)/shard_map/place/pallas_call | solution.py:75
  48.6 0.0 copy-done.1
  48.6 0.0 copy-start.4
  48.6 0.0 slice-start
  48.6 4.1 %reshape.54 = bf16[64,32,576]{2,1,0:T(8,128)(2,1)} reshape(bf16[64,18432]{1,0:T(8,128)(2,1)S(1)} %copy-done.1) | data formatting | bytes 4718592 | tf_op jit(solution)/shard_map/reshape | solution.py:296
  52.7 0.0 copy-done.4
  52.7 0.1 iota_compare_fusion
  52.8 0.0 slice-start.1
  52.8 0.0 slice-start.2
  52.8 6.3 %fusion.26 = (f32[64,32]{1,0:T(8,128)S(1)}, f32[64,32,128]{2,1,0:T(8,128)S(1)}) fusion(bf16[64,32,576]{2,1,0:T(8,128)(2,1)} %reshape.54, bf16[64,576,128]{2,1,0:T(8,128)(2,1)} %param.9, pred[64,128]{1,0:T(8,128)(4,1)S(1)} %iota_compare_fusion), kind=kOutput, calls=%fused_computation.36 | convolution fusion | flops 302774272 | bytes 12861440 | tf_op jit(solution)/shard_map/fhe,fes->fhs/dot_general | solution.py:298
  59.1 0.7 fusion.13
  59.8 0.0 slice-done
  59.8 0.0 slice-done.1
  59.8 0.7 slice-done.2
  60.5 0.0 copy-start.2
  60.5 3.5 %divide_convert_fusion = bf16[64,32,512]{2,1,0:T(8,128)(2,1)S(1)} fusion(f32[64,32]{1,0:T(8,128)S(1)} %fusion.13, bf16[64,576,128]{2,1,0:T(8,128)(2,1)S(1)} %bitcast.29, f32[64,32,128]{2,1,0:T(8,128)S(1)} %get-tuple-element.38, f32[64,32]{1,0:T(8,128)S(1)} %get-tuple-element.37, pred[64,128]{1,0:T(8,128)(4,1)S(1)} %iota_compare_fusion), kind=kOutput, calls=%fused_computation.2 | convolution fusion | flops 271319040 | bytes 11608064 | tf_op jit(solution)/shard_map/fhs,frs->fhr/dot_general | solution.py:307
  64.0 0.0 copy-done.2
  64.0 2.5 %fusion.8 = bf16[32,8,8,128]{3,2,1,0:T(8,128)(2,1)S(1)} fusion(bf16[32,512,128]{2,1,0:T(8,128)(2,1)S(1)} %copy-done.2, bf16[64,32,512]{2,1,0:T(8,128)(2,1)S(1)} %divide_convert_fusion), kind=kOutput, calls=%fused_computation.8 | convolution fusion | flops 268697600 | bytes 6815744 | tf_op jit(solution)/shard_map/nhr,hrv->nhv/dot_general | solution.py:314
  66.5 0.1 copy.33
  66.7 0.1 copy.22
  66.7 0.1 copy.24
  66.8 0.1 copy.23
  66.9 0.1 pad_maximum_fusion.1.refs_3_
  67.0 7.0 %all-to-all-done.1.q_ref = bf16[16,32,2304]{2,1,0:T(8,128)(2,1)} async-done(((bf16[16,32,2304]{2,1,0:T(8,128)(2,1)}), bf16[16,32,2304]{2,1,0:T(8,128)(2,1)}, u32[]{:S(2)}, u32[]{:S(2)}) %all-to-all-start.1) | async-done | bytes 2359328 | tf_op jit(solution)/shard_map/all_to_all | solution.py:329
  74.0 7.5 %all-to-all-start = ((bf16[16,32,2304]{2,1,0:T(8,128)(2,1)}), bf16[16,32,2304]{2,1,0:T(8,128)(2,1)}, u32[]{:S(2)}, u32[]{:S(2)}) async-start(bf16[16,32,2304]{2,1,0:T(8,128)(2,1)} %bitcast.31), calls=%async_computation | async-start | bytes 4718592 | tf_op jit(solution)/shard_map/all_to_all | solution.py:329
  81.5 19.7 %all-gather.2.cloned.1.call-done.kv_ref = bf16[4,4,576,256]{3,2,1,0:T(8,128)(2,1)} async-done(((bf16[1,4,576,256]{3,2,1,0:T(8,128)(2,1)}), bf16[4,4,576,256]{3,2,1,0:T(8,128)(2,1)}) %all-gather.2.cloned.1.call-update) | async-done | bytes 4718608 | tf_op jit(solution)/shard_map/all_gather | solution.py:342
  101.2 10.9 %prefix.2 = bf16[128,2176]{1,0:T(8,128)(2,1)} custom-call(bf16[16,32,2304]{2,1,0:T(8,128)(2,1)} %all-to-all-done.1.q_ref, bf16[4,4,576,256]{3,2,1,0:T(8,128)(2,1)} %all-gather.2.cloned.1.call-done.kv_ref, bf16[32,512,128]{2,1,0:T(8,128)(2,1)} %w_hbm.3), custom_call_target="tpu_custom_call" | custom-call | flops 4831838208 | bytes 9732096 | tf_op jit(solution)/shard_map/prefix/pallas_call | solution.py:224
  112.2 0.2 all-to-all-done.q_ref
  112.4 7.5 %all-to-all-start.2 = ((bf16[16,8,2176]{2,1,0:T(8,128)(2,1)}), bf16[16,8,2176]{2,1,0:T(8,128)(2,1)S(1)}, u32[]{:S(2)}, u32[]{:S(2)}) async-start(bf16[16,8,2176]{2,1,0:T(8,128)(2,1)} %bitcast.34), calls=%async_computation.2 | async-start | bytes 1114112 | tf_op jit(solution)/shard_map/all_to_all | solution.py:329
  119.9 0.0 copy-start
  119.9 10.9 %prefix.3 = bf16[128,2176]{1,0:T(8,128)(2,1)} custom-call(bf16[16,32,2304]{2,1,0:T(8,128)(2,1)} %all-to-all-done.q_ref, bf16[4,4,576,256]{3,2,1,0:T(8,128)(2,1)} %all-gather.2.cloned.1.call-done.kv_ref, bf16[32,512,128]{2,1,0:T(8,128)(2,1)} %w_hbm.3), custom_call_target="tpu_custom_call" | custom-call | flops 4831838208 | bytes 9732096 | tf_op jit(solution)/shard_map/prefix/pallas_call | solution.py:224
  130.9 0.0 all-to-all-done.2
  130.9 16.8 %all_to_all.20 = bf16[16,8,2176]{2,1,0:T(8,128)(2,1)S(1)} all-to-all(bf16[16,8,2176]{2,1,0:T(8,128)(2,1)} %bitcast.35), channel_id=1, replica_groups=mesh['zh'=4,'zl'=2,'xc'=8,'tp'=4] {'zl','xc'}, dimensions={0} | all-to-all | bytes 1114112 | tf_op jit(solution)/shard_map/all_to_all | solution.py:329
  147.7 0.0 copy-done
  147.7 2.1 %merge.1 = bf16[64,4096]{1,0:T(8,128)(2,1)} custom-call(s32[64,1]{1,0:T(8,128)S(1)} %copy-done, bf16[128,2176]{1,0:T(8,128)(2,1)S(1)} %bitcast.25, bf16[128,2176]{1,0:T(8,128)(2,1)S(1)} %bitcast.26, bf16[64,4096]{1,0:T(8,128)(2,1)S(1)} %bitcast.27, f32[64,32]{1,0:T(8,128)S(1)} %pad_maximum_fusion.1.refs_3_), custom_call_target="tpu_custom_call" | custom-call | tf_op jit(solution)/shard_map/merge/pallas_call | solution.py:285
  (6 shorter events, 0.1 us)
Async XLA Ops:
  6.5 15.8 %collective-permute-start = (bf16[1,576,256]{2,1,0:T(8,128)(2,1)}, bf16[1,576,256]{2,1,0:T(8,128)(2,1)S(1)}, u32[]{:S(2)}, u32[]{:S(2)}) collective-permute-start(bf16[1,576,256]{2,1,0:T(8,128)(2,1)} %param.8), channel_id=1, source_target_pairs={{0,64},{64,128},{128,192},{192,0},{1,65},{65,129},{129,193},{193,1... | collective-permute-start | bytes 884744 | tf_op jit(solution)/shard_map/ppermute | solution.py:326
  10.4 17.8 %collective-permute-start.1 = (bf16[1,576,256]{2,1,0:T(8,128)(2,1)}, bf16[1,576,256]{2,1,0:T(8,128)(2,1)S(1)}, u32[]{:S(2)}, u32[]{:S(2)}) collective-permute-start(bf16[1,576,256]{2,1,0:T(8,128)(2,1)} %param.8), channel_id=1, source_target_pairs={{0,192},{64,0},{128,64},{192,128},{1,193},{65,1},{129,65},{193,129... | collective-permute-start | bytes 884744 | tf_op jit(solution)/shard_map/ppermute | solution.py:326
  22.3 13.3 %collective-permute-start.2 = (bf16[1,288,256]{2,1,0:T(8,128)(2,1)S(1)}, bf16[1,288,256]{2,1,0:T(8,128)(2,1)S(1)}, u32[]{:S(2)}, u32[]{:S(2)}) collective-permute-start(bf16[1,288,256]{2,1,0:T(8,128)(2,1)S(1)} %slice.22), channel_id=1, source_target_pairs={{0,64},{64,128},{128,192},{192,0},{1,65},{65,129},{129,193},{193,1... | collective-permute-start | bytes 442376 | tf_op jit(solution)/shard_map/ppermute | solution.py:326
  28.1 9.2 %collective-permute-start.3 = (bf16[1,288,256]{2,1,0:T(8,128)(2,1)S(1)}, bf16[1,288,256]{2,1,0:T(8,128)(2,1)S(1)}, u32[]{:S(2)}, u32[]{:S(2)}) collective-permute-start(bf16[1,288,256]{2,1,0:T(8,128)(2,1)S(1)} %slice.23), channel_id=1, source_target_pairs={{0,192},{64,0},{128,64},{192,128},{1,193},{65,1},{129,65},{193,129... | collective-permute-start | bytes 442376 | tf_op jit(solution)/shard_map/ppermute | solution.py:326
  37.3 6.0 %copy-start.3 = (bf16[1,576,256]{2,1,0:T(8,128)(2,1)S(1)}, bf16[1,576,256]{2,1,0:T(8,128)(2,1)}, u32[]{:S(2)}) copy-start(bf16[1,576,256]{2,1,0:T(8,128)(2,1)} %param.8) | copy-start | bytes 884740
  37.3 36.7 %all-to-all-start.1 = ((bf16[16,32,2304]{2,1,0:T(8,128)(2,1)}), bf16[16,32,2304]{2,1,0:T(8,128)(2,1)}, u32[]{:S(2)}, u32[]{:S(2)}) async-start(bf16[16,32,2304]{2,1,0:T(8,128)(2,1)} %bitcast.30), calls=%async_computation.1 | async-start | bytes 4718592 | tf_op jit(solution)/shard_map/all_to_all | solution.py:329
  43.1 58.1 %all-gather.2.cloned.1.call-start = ((), (), s32[]{:S(2)}) async-start(), calls=%async_computation.4 | async-start | bytes 5898240 | tf_op jit(solution)/shard_map/all_gather | solution.py:342
  44.6 4.0 %copy-start.1 = (bf16[64,18432]{1,0:T(8,128)(2,1)S(1)}, bf16[64,18432]{1,0:T(8,128)(2,1)}, u32[]{:S(2)}) copy-start(bf16[64,18432]{1,0:T(8,128)(2,1)} %refs_3_.3) | copy-start | bytes 7077892
  48.6 4.1 %copy-start.4 = (s32[64]{0:T(128)S(1)}, s32[64]{0:T(128)}, u32[]{:S(2)}) copy-start(s32[64]{0:T(128)} %param.13) | copy-start | bytes 772
  48.6 11.2 %slice-start = ((s8[9437184]{0:T(1024)(128)(4,1)}), s8[1048576]{0:T(1024)(128)(4,1)S(1)}, s32[]{:S(2)}) async-start(s8[9437184]{0:T(1024)(128)(4,1)} %bitcast.28), calls=%async_computation.5 | async-start | bytes 2097152
  52.8 7.0 %slice-start.1 = ((s8[9437184]{0:T(1024)(128)(4,1)}), s8[4194304]{0:T(1024)(128)(4,1)S(1)}, s32[]{:S(2)}) async-start(s8[9437184]{0:T(1024)(128)(4,1)} %bitcast.28), calls=%async_computation.6 | async-start | bytes 8388608
  52.8 7.7 %slice-start.2 = ((s8[9437184]{0:T(1024)(128)(4,1)}), s8[4194304]{0:T(1024)(128)(4,1)S(1)}, s32[]{:S(2)}) async-start(s8[9437184]{0:T(1024)(128)(4,1)} %bitcast.28), calls=%async_computation.7 | async-start | bytes 8388608
  60.5 3.5 %copy-start.2 = (bf16[32,512,128]{2,1,0:T(8,128)(2,1)S(1)}, bf16[32,512,128]{2,1,0:T(8,128)(2,1)}, u32[]{:S(2)}) copy-start(bf16[32,512,128]{2,1,0:T(8,128)(2,1)} %w_hbm.3) | copy-start | bytes 12582916
  74.0 38.4 %all-to-all-start = ((bf16[16,32,2304]{2,1,0:T(8,128)(2,1)}), bf16[16,32,2304]{2,1,0:T(8,128)(2,1)}, u32[]{:S(2)}, u32[]{:S(2)}) async-start(bf16[16,32,2304]{2,1,0:T(8,128)(2,1)} %bitcast.31), calls=%async_computation | async-start | bytes 4718592 | tf_op jit(solution)/shard_map/all_to_all | solution.py:329
  112.4 18.5 %all-to-all-start.2 = ((bf16[16,8,2176]{2,1,0:T(8,128)(2,1)}), bf16[16,8,2176]{2,1,0:T(8,128)(2,1)S(1)}, u32[]{:S(2)}, u32[]{:S(2)}) async-start(bf16[16,8,2176]{2,1,0:T(8,128)(2,1)} %bitcast.34), calls=%async_computation.2 | async-start | bytes 1114112 | tf_op jit(solution)/shard_map/all_to_all | solution.py:329
  119.9 27.8 %copy-start = (s32[64,1]{1,0:T(8,128)S(1)}, s32[64,1]{1,0:T(8,128)}, u32[]{:S(2)}) copy-start(s32[64,1]{1,0:T(8,128)} %get-tuple-element.20.target_ref) | copy-start | bytes 772
Sparse Core Ops, SparseCore 0:
  45.7 55.4 all-gather.1

commit v8 on v7

--- a/solution.py
+++ b/solution.py
@@ -200,12 +200,12 @@
                 turn, block, preferred_element_type=jnp.float32
             ).astype(jnp.bfloat16)
 
-        for head in range(0, heads, 2):
-            both = [
+        for head in range(0, heads, 4):
+            several = [
                 jnp.dot(lat_ref[h], w_ref[h], preferred_element_type=jnp.float32)
-                for h in (head, head + 1)
+                for h in range(head, head + 4)
             ]
-            put(head * V, jnp.concatenate(both, axis=1).astype(jnp.bfloat16))
+            put(head * V, jnp.concatenate(several, axis=1).astype(jnp.bfloat16))
         high = mass_ref[...].astype(jnp.bfloat16)
         low = (mass_ref[...] - high.astype(jnp.float32)).astype(jnp.bfloat16)
         spot = lax.broadcasted_iota(jnp.int32, mass_ref.shape, 1)

time: 157 us -> 156 us (level)
  transfers between devices with their start and end apart: 8 -> 8, of which waited for: 6 -> 6; matrix products, arithmetic and copies ran while one was open for 14% -> 14% of each run, Pallas kernels for 19% -> 18%
where the time goes in v8:
time: 156 us
  waiting for transfers between devices  37.5 us (24%)
  starting transfers between devices  35.4 us (23%)
  Pallas kernels  30.6 us (20%)
  blocking collectives  16.8 us (11%)
  between operations  13.6 us (9%)
  matrix products  12.4 us (8%)
  local copies, waits for them, and re-layouts  6.48 us (4%)
  other arithmetic  3.27 us (2%)
    all_to_all x3, starting transfers between devices, exchange(): lax.all_to_all(value.reshape(group, -1, value.shape[1]), near, split_axis...  20.8 us
    pallas_call x2, Pallas kernels, prefix(): pl.pallas_call(functools.partial(prefix_kernel, part), out_shape=jax.Shap...  20.7 us
    all_gather x1, waiting for transfers between devices, shards(): lax.all_gather(jnp.stack(held_here, axis=1), 'tp', axis=0, tiled=True)  19.7 us
    all_to_all x1, blocking collectives, exchange(): lax.all_to_all(value.reshape(group, -1, value.shape[1]), near, split_axis...  16.8 us
    ppermute x4, starting transfers between devices, along(): lax.ppermute(value, 'zh', [(n, (n + steps) % COPIES) for n in range(COPIE...  14.4 us
    ppermute x4, waiting for transfers between devices, along(): lax.ppermute(value, 'zh', [(n, (n + steps) % COPIES) for n in range(COPIE...  9.95 us
    all_to_all x3, waiting for transfers between devices, exchange(): lax.all_to_all(value.reshape(group, -1, value.shape[1]), near, split_axis...  7.88 us
    pallas_call x2, Pallas kernels, place(): pl.pallas_call(place_kernel, out_shape=(jax.ShapeDtypeStruct((rows, mine...  7.84 us
  transfers between devices with their start and end apart: 8, of which 6 were waited for; matrix products, arithmetic and copies ran while one was open for 14% of the time, Pallas kernels for 18%

profile of v8, /device:TPU:1, one launch (start us, length us, event | category | flops | bytes accessed | tf_op | source)
XLA Modules:
  0.0 156.0 jit_solution(1640545731967239666)
XLA Ops:
  6.5 3.8 %collective-permute-start = (bf16[1,576,256]{2,1,0:T(8,128)(2,1)}, bf16[1,576,256]{2,1,0:T(8,128)(2,1)S(1)}, u32[]{:S(2)}, u32[]{:S(2)}) collective-permute-start(bf16[1,576,256]{2,1,0:T(8,128)(2,1)} %param.8), channel_id=1, source_target_pairs={{0,64},{64,128},{128,192},{192,0},{1,65},{65,129},{129,193},{193,1... | collective-permute-start | bytes 884744 | tf_op jit(solution)/shard_map/ppermute | solution.py:326
  10.4 3.0 %collective-permute-start.1 = (bf16[1,576,256]{2,1,0:T(8,128)(2,1)}, bf16[1,576,256]{2,1,0:T(8,128)(2,1)S(1)}, u32[]{:S(2)}, u32[]{:S(2)}) collective-permute-start(bf16[1,576,256]{2,1,0:T(8,128)(2,1)} %param.8), channel_id=1, source_target_pairs={{0,192},{64,0},{128,64},{192,128},{1,193},{65,1},{129,65},{193,129... | collective-permute-start | bytes 884744 | tf_op jit(solution)/shard_map/ppermute | solution.py:326
  13.4 1.4 copy.18.prompt_ref
  14.7 7.6 %collective-permute-done = bf16[1,576,256]{2,1,0:T(8,128)(2,1)S(1)} collective-permute-done((bf16[1,576,256]{2,1,0:T(8,128)(2,1)}, bf16[1,576,256]{2,1,0:T(8,128)(2,1)S(1)}, u32[]{:S(2)}, u32[]{:S(2)}) %collective-permute-start) | collective-permute-done | bytes 294944 | tf_op jit(solution)/shard_map/ppermute | solution.py:326
  22.3 5.1 %collective-permute-start.2 = (bf16[1,288,256]{2,1,0:T(8,128)(2,1)S(1)}, bf16[1,288,256]{2,1,0:T(8,128)(2,1)S(1)}, u32[]{:S(2)}, u32[]{:S(2)}) collective-permute-start(bf16[1,288,256]{2,1,0:T(8,128)(2,1)S(1)} %slice.22), channel_id=1, source_target_pairs={{0,64},{64,128},{128,192},{192,0},{1,65},{65,129},{129,193},{193,1... | collective-permute-start | bytes 442376 | tf_op jit(solution)/shard_map/ppermute | solution.py:326
  27.4 0.7 collective-permute-done.1
  28.1 2.4 %collective-permute-start.3 = (bf16[1,288,256]{2,1,0:T(8,128)(2,1)S(1)}, bf16[1,288,256]{2,1,0:T(8,128)(2,1)S(1)}, u32[]{:S(2)}, u32[]{:S(2)}) collective-permute-start(bf16[1,288,256]{2,1,0:T(8,128)(2,1)S(1)} %slice.23), channel_id=1, source_target_pairs={{0,192},{64,0},{128,64},{192,128},{1,193},{65,1},{129,65},{193,129... | collective-permute-start | bytes 442376 | tf_op jit(solution)/shard_map/ppermute | solution.py:326
  30.6 1.2 fusion.23.base_ref
  31.8 3.8 %place.2 = (bf16[512,2304]{1,0:T(8,128)(2,1)}, s32[64,1]{1,0:T(8,128)}) custom-call(s32[64,1]{1,0:T(8,128)} %copy.18.prompt_ref, s32[1,64]{1,0:T(1,128)} %fusion.23.base_ref, bf16[64,18432]{1,0:T(8,128)(2,1)} %refs_3_.3, bf16[64,18432]{1,0:T(8,128)(2,1)} %refs_3_.3, bf16[64,18432]{1,0:T(8,128)(2,1)} %refs_3_.3, bf16[64,18432]{1,0:T(8,128)(2,1)} %refs_3_.3), custom_call_target="tpu_custom_call" | custom-call | tf_op jit(solution)/shard_map/place/pallas_call | solution.py:75
  35.6 0.0 collective-permute-done.2
  35.6 1.7 %collective-permute-done.3 = bf16[1,288,256]{2,1,0:T(8,128)(2,1)S(1)} collective-permute-done((bf16[1,288,256]{2,1,0:T(8,128)(2,1)S(1)}, bf16[1,288,256]{2,1,0:T(8,128)(2,1)S(1)}, u32[]{:S(2)}, u32[]{:S(2)}) %collective-permute-start.3) | collective-permute-done | bytes 147488 | tf_op jit(solution)/shard_map/ppermute | solution.py:326
  37.3 0.0 copy-start.3
  37.3 5.8 %all-to-all-start.1 = ((bf16[16,32,2304]{2,1,0:T(8,128)(2,1)}), bf16[16,32,2304]{2,1,0:T(8,128)(2,1)}, u32[]{:S(2)}, u32[]{:S(2)}) async-start(bf16[16,32,2304]{2,1,0:T(8,128)(2,1)} %bitcast.30), calls=%async_computation.1 | async-start | bytes 4718592 | tf_op jit(solution)/shard_map/all_to_all | solution.py:329
  43.1 0.2 all-gather.2.cloned.1.call-start
  43.4 0.0 copy-done.3
  43.4 1.2 pad_maximum_fusion
  44.5 0.0 all-gather.2.cloned.1.call-update
  44.6 0.0 copy-start.1
  44.6 4.0 %place.3 = (bf16[512,2304]{1,0:T(8,128)(2,1)}, s32[64,1]{1,0:T(8,128)}) custom-call(s32[64,1]{1,0:T(8,128)} %copy.18.prompt_ref, s32[1,64]{1,0:T(1,128)} %fusion.23.base_ref, bf16[64,18432]{1,0:T(8,128)(2,1)} %refs_3_.3, bf16[64,18432]{1,0:T(8,128)(2,1)} %refs_3_.3, bf16[64,18432]{1,0:T(8,128)(2,1)} %refs_3_.3, bf16[64,18432]{1,0:T(8,128)(2,1)} %refs_3_.3), custom_call_target="tpu_custom_call" | custom-call | tf_op jit(solution)/shard_map/place/pallas_call | solution.py:75
  48.6 0.0 copy-done.1
  48.6 0.0 copy-start.4
  48.6 0.0 slice-start
  48.6 4.1 %reshape.54 = bf16[64,32,576]{2,1,0:T(8,128)(2,1)} reshape(bf16[64,18432]{1,0:T(8,128)(2,1)S(1)} %copy-done.1) | data formatting | bytes 4718592 | tf_op jit(solution)/shard_map/reshape | solution.py:296
  52.7 0.0 copy-done.4
  52.7 0.1 iota_compare_fusion
  52.8 0.0 slice-start.1
  52.8 0.0 slice-start.2
  52.8 6.3 %fusion.26 = (f32[64,32]{1,0:T(8,128)S(1)}, f32[64,32,128]{2,1,0:T(8,128)S(1)}) fusion(bf16[64,32,576]{2,1,0:T(8,128)(2,1)} %reshape.54, bf16[64,576,128]{2,1,0:T(8,128)(2,1)} %param.9, pred[64,128]{1,0:T(8,128)(4,1)S(1)} %iota_compare_fusion), kind=kOutput, calls=%fused_computation.36 | convolution fusion | flops 302774272 | bytes 12861440 | tf_op jit(solution)/shard_map/fhe,fes->fhs/dot_general | solution.py:298
  59.1 0.7 fusion.13
  59.8 0.0 slice-done
  59.8 0.0 slice-done.1
  59.8 0.7 slice-done.2
  60.5 0.0 copy-start.2
  60.5 3.5 %divide_convert_fusion = bf16[64,32,512]{2,1,0:T(8,128)(2,1)S(1)} fusion(f32[64,32]{1,0:T(8,128)S(1)} %fusion.13, bf16[64,576,128]{2,1,0:T(8,128)(2,1)S(1)} %bitcast.29, f32[64,32,128]{2,1,0:T(8,128)S(1)} %get-tuple-element.38, f32[64,32]{1,0:T(8,128)S(1)} %get-tuple-element.37, pred[64,128]{1,0:T(8,128)(4,1)S(1)} %iota_compare_fusion), kind=kOutput, calls=%fused_computation.2 | convolution fusion | flops 271319040 | bytes 11608064 | tf_op jit(solution)/shard_map/fhs,frs->fhr/dot_general | solution.py:307
  64.0 0.0 copy-done.2
  64.0 2.5 %fusion.8 = bf16[32,8,8,128]{3,2,1,0:T(8,128)(2,1)S(1)} fusion(bf16[32,512,128]{2,1,0:T(8,128)(2,1)S(1)} %copy-done.2, bf16[64,32,512]{2,1,0:T(8,128)(2,1)S(1)} %divide_convert_fusion), kind=kOutput, calls=%fused_computation.8 | convolution fusion | flops 268697600 | bytes 6815744 | tf_op jit(solution)/shard_map/nhr,hrv->nhv/dot_general | solution.py:314
  66.5 0.1 copy.33
  66.7 0.1 copy.22
  66.7 0.1 copy.24
  66.8 0.1 copy.23
  66.9 0.1 pad_maximum_fusion.1.refs_3_
  67.0 7.0 %all-to-all-done.1.q_ref = bf16[16,32,2304]{2,1,0:T(8,128)(2,1)} async-done(((bf16[16,32,2304]{2,1,0:T(8,128)(2,1)}), bf16[16,32,2304]{2,1,0:T(8,128)(2,1)}, u32[]{:S(2)}, u32[]{:S(2)}) %all-to-all-start.1) | async-done | bytes 2359328 | tf_op jit(solution)/shard_map/all_to_all | solution.py:329
  74.0 7.5 %all-to-all-start = ((bf16[16,32,2304]{2,1,0:T(8,128)(2,1)}), bf16[16,32,2304]{2,1,0:T(8,128)(2,1)}, u32[]{:S(2)}, u32[]{:S(2)}) async-start(bf16[16,32,2304]{2,1,0:T(8,128)(2,1)} %bitcast.31), calls=%async_computation | async-start | bytes 4718592 | tf_op jit(solution)/shard_map/all_to_all | solution.py:329
  81.5 19.7 %all-gather.2.cloned.1.call-done.kv_ref = bf16[4,4,576,256]{3,2,1,0:T(8,128)(2,1)} async-done(((bf16[1,4,576,256]{3,2,1,0:T(8,128)(2,1)}), bf16[4,4,576,256]{3,2,1,0:T(8,128)(2,1)}) %all-gather.2.cloned.1.call-update) | async-done | bytes 4718608 | tf_op jit(solution)/shard_map/all_gather | solution.py:342
  101.2 10.3 %prefix.2 = bf16[128,2176]{1,0:T(8,128)(2,1)} custom-call(bf16[16,32,2304]{2,1,0:T(8,128)(2,1)} %all-to-all-done.1.q_ref, bf16[4,4,576,256]{3,2,1,0:T(8,128)(2,1)} %all-gather.2.cloned.1.call-done.kv_ref, bf16[32,512,128]{2,1,0:T(8,128)(2,1)} %w_hbm.3), custom_call_target="tpu_custom_call" | custom-call | flops 4831838208 | bytes 9732096 | tf_op jit(solution)/shard_map/prefix/pallas_call | solution.py:224
  111.6 0.9 all-to-all-done.q_ref
  112.4 7.5 %all-to-all-start.2 = ((bf16[16,8,2176]{2,1,0:T(8,128)(2,1)}), bf16[16,8,2176]{2,1,0:T(8,128)(2,1)S(1)}, u32[]{:S(2)}, u32[]{:S(2)}) async-start(bf16[16,8,2176]{2,1,0:T(8,128)(2,1)} %bitcast.34), calls=%async_computation.2 | async-start | bytes 1114112 | tf_op jit(solution)/shard_map/all_to_all | solution.py:329
  119.9 0.0 copy-start
  119.9 10.3 %prefix.3 = bf16[128,2176]{1,0:T(8,128)(2,1)} custom-call(bf16[16,32,2304]{2,1,0:T(8,128)(2,1)} %all-to-all-done.q_ref, bf16[4,4,576,256]{3,2,1,0:T(8,128)(2,1)} %all-gather.2.cloned.1.call-done.kv_ref, bf16[32,512,128]{2,1,0:T(8,128)(2,1)} %w_hbm.3), custom_call_target="tpu_custom_call" | custom-call | flops 4831838208 | bytes 9732096 | tf_op jit(solution)/shard_map/prefix/pallas_call | solution.py:224
  130.3 0.0 all-to-all-done.2
  130.3 16.8 %all_to_all.20 = bf16[16,8,2176]{2,1,0:T(8,128)(2,1)S(1)} all-to-all(bf16[16,8,2176]{2,1,0:T(8,128)(2,1)} %bitcast.35), channel_id=1, replica_groups=mesh['zh'=4,'zl'=2,'xc'=8,'tp'=4] {'zl','xc'}, dimensions={0} | all-to-all | bytes 1114112 | tf_op jit(solution)/shard_map/all_to_all | solution.py:329
  147.1 0.0 copy-done
  147.1 2.1 %merge.1 = bf16[64,4096]{1,0:T(8,128)(2,1)} custom-call(s32[64,1]{1,0:T(8,128)S(1)} %copy-done, bf16[128,2176]{1,0:T(8,128)(2,1)S(1)} %bitcast.25, bf16[128,2176]{1,0:T(8,128)(2,1)S(1)} %bitcast.26, bf16[64,4096]{1,0:T(8,128)(2,1)S(1)} %bitcast.27, f32[64,32]{1,0:T(8,128)S(1)} %pad_maximum_fusion.1.refs_3_), custom_call_target="tpu_custom_call" | custom-call | tf_op jit(solution)/shard_map/merge/pallas_call | solution.py:285
  (6 shorter events, 0.1 us)
Async XLA Ops:
  6.5 15.8 %collective-permute-start = (bf16[1,576,256]{2,1,0:T(8,128)(2,1)}, bf16[1,576,256]{2,1,0:T(8,128)(2,1)S(1)}, u32[]{:S(2)}, u32[]{:S(2)}) collective-permute-start(bf16[1,576,256]{2,1,0:T(8,128)(2,1)} %param.8), channel_id=1, source_target_pairs={{0,64},{64,128},{128,192},{192,0},{1,65},{65,129},{129,193},{193,1... | collective-permute-start | bytes 884744 | tf_op jit(solution)/shard_map/ppermute | solution.py:326
  10.4 17.8 %collective-permute-start.1 = (bf16[1,576,256]{2,1,0:T(8,128)(2,1)}, bf16[1,576,256]{2,1,0:T(8,128)(2,1)S(1)}, u32[]{:S(2)}, u32[]{:S(2)}) collective-permute-start(bf16[1,576,256]{2,1,0:T(8,128)(2,1)} %param.8), channel_id=1, source_target_pairs={{0,192},{64,0},{128,64},{192,128},{1,193},{65,1},{129,65},{193,129... | collective-permute-start | bytes 884744 | tf_op jit(solution)/shard_map/ppermute | solution.py:326
  22.3 13.3 %collective-permute-start.2 = (bf16[1,288,256]{2,1,0:T(8,128)(2,1)S(1)}, bf16[1,288,256]{2,1,0:T(8,128)(2,1)S(1)}, u32[]{:S(2)}, u32[]{:S(2)}) collective-permute-start(bf16[1,288,256]{2,1,0:T(8,128)(2,1)S(1)} %slice.22), channel_id=1, source_target_pairs={{0,64},{64,128},{128,192},{192,0},{1,65},{65,129},{129,193},{193,1... | collective-permute-start | bytes 442376 | tf_op jit(solution)/shard_map/ppermute | solution.py:326
  28.1 9.2 %collective-permute-start.3 = (bf16[1,288,256]{2,1,0:T(8,128)(2,1)S(1)}, bf16[1,288,256]{2,1,0:T(8,128)(2,1)S(1)}, u32[]{:S(2)}, u32[]{:S(2)}) collective-permute-start(bf16[1,288,256]{2,1,0:T(8,128)(2,1)S(1)} %slice.23), channel_id=1, source_target_pairs={{0,192},{64,0},{128,64},{192,128},{1,193},{65,1},{129,65},{193,129... | collective-permute-start | bytes 442376 | tf_op jit(solution)/shard_map/ppermute | solution.py:326
  37.3 6.0 %copy-start.3 = (bf16[1,576,256]{2,1,0:T(8,128)(2,1)S(1)}, bf16[1,576,256]{2,1,0:T(8,128)(2,1)}, u32[]{:S(2)}) copy-start(bf16[1,576,256]{2,1,0:T(8,128)(2,1)} %param.8) | copy-start | bytes 884740
  37.3 36.7 %all-to-all-start.1 = ((bf16[16,32,2304]{2,1,0:T(8,128)(2,1)}), bf16[16,32,2304]{2,1,0:T(8,128)(2,1)}, u32[]{:S(2)}, u32[]{:S(2)}) async-start(bf16[16,32,2304]{2,1,0:T(8,128)(2,1)} %bitcast.30), calls=%async_computation.1 | async-start | bytes 4718592 | tf_op jit(solution)/shard_map/all_to_all | solution.py:329
  43.1 58.1 %all-gather.2.cloned.1.call-start = ((), (), s32[]{:S(2)}) async-start(), calls=%async_computation.4 | async-start | bytes 5898240 | tf_op jit(solution)/shard_map/all_gather | solution.py:342
  44.6 4.0 %copy-start.1 = (bf16[64,18432]{1,0:T(8,128)(2,1)S(1)}, bf16[64,18432]{1,0:T(8,128)(2,1)}, u32[]{:S(2)}) copy-start(bf16[64,18432]{1,0:T(8,128)(2,1)} %refs_3_.3) | copy-start | bytes 7077892
  48.6 4.1 %copy-start.4 = (s32[64]{0:T(128)S(1)}, s32[64]{0:T(128)}, u32[]{:S(2)}) copy-start(s32[64]{0:T(128)} %param.13) | copy-start | bytes 772
  48.6 11.2 %slice-start = ((s8[9437184]{0:T(1024)(128)(4,1)}), s8[1048576]{0:T(1024)(128)(4,1)S(1)}, s32[]{:S(2)}) async-start(s8[9437184]{0:T(1024)(128)(4,1)} %bitcast.28), calls=%async_computation.5 | async-start | bytes 2097152
  52.8 7.0 %slice-start.1 = ((s8[9437184]{0:T(1024)(128)(4,1)}), s8[4194304]{0:T(1024)(128)(4,1)S(1)}, s32[]{:S(2)}) async-start(s8[9437184]{0:T(1024)(128)(4,1)} %bitcast.28), calls=%async_computation.6 | async-start | bytes 8388608
  52.8 7.7 %slice-start.2 = ((s8[9437184]{0:T(1024)(128)(4,1)}), s8[4194304]{0:T(1024)(128)(4,1)S(1)}, s32[]{:S(2)}) async-start(s8[9437184]{0:T(1024)(128)(4,1)} %bitcast.28), calls=%async_computation.7 | async-start | bytes 8388608
  60.5 3.5 %copy-start.2 = (bf16[32,512,128]{2,1,0:T(8,128)(2,1)S(1)}, bf16[32,512,128]{2,1,0:T(8,128)(2,1)}, u32[]{:S(2)}) copy-start(bf16[32,512,128]{2,1,0:T(8,128)(2,1)} %w_hbm.3) | copy-start | bytes 12582916
  74.0 38.4 %all-to-all-start = ((bf16[16,32,2304]{2,1,0:T(8,128)(2,1)}), bf16[16,32,2304]{2,1,0:T(8,128)(2,1)}, u32[]{:S(2)}, u32[]{:S(2)}) async-start(bf16[16,32,2304]{2,1,0:T(8,128)(2,1)} %bitcast.31), calls=%async_computation | async-start | bytes 4718592 | tf_op jit(solution)/shard_map/all_to_all | solution.py:329
  112.4 17.8 %all-to-all-start.2 = ((bf16[16,8,2176]{2,1,0:T(8,128)(2,1)}), bf16[16,8,2176]{2,1,0:T(8,128)(2,1)S(1)}, u32[]{:S(2)}, u32[]{:S(2)}) async-start(bf16[16,8,2176]{2,1,0:T(8,128)(2,1)} %bitcast.34), calls=%async_computation.2 | async-start | bytes 1114112 | tf_op jit(solution)/shard_map/all_to_all | solution.py:329
  119.9 27.1 %copy-start = (s32[64,1]{1,0:T(8,128)S(1)}, s32[64,1]{1,0:T(8,128)}, u32[]{:S(2)}) copy-start(s32[64,1]{1,0:T(8,128)} %get-tuple-element.20.target_ref) | copy-start | bytes 772
Sparse Core Ops, SparseCore 0:
  45.7 55.4 all-gather.1
